TPU v7x, 128 devices: a whole 4x4x4 slice. The times are simulated.
128 devices in a mesh: tp: 2 (over core), ep: 64 (over z, y, x).
Axes of the slice: x: 4, y: 4, z: 4, core: 2. Of those that a mesh axis runs over, the one named last changes fastest.
Arguments:
- context: bfloat16 [64, 256, 2048], P('ep', None, 'tp'), may hold values from -6 to 6
- out_weight: bfloat16 [2048, 2048], P('tp'), may hold values from -0.125 to 0.125
- residual_in: bfloat16 [64, 256, 2048], P('ep', 'tp'), may hold values from -6 to 6
- norm_gain: float32 [2048], replicated, may hold values from 0.5 to 1.5
- expert_ids: int32 [64, 256, 2], P('ep', 'tp'), may hold values from 0 to 63, all different within a row; in each aligned block of 128 rows (0 to 127, 128 to 255, ..., all dimensions but the last counted through in order) at most 6 rows name the same one
- gate_weights: float32 [64, 256, 2], P('ep', 'tp'), may hold values from 0.2 to 1
- keep_mask: int32 [64, 256, 2], P('ep', 'tp'), may hold values 0 or 1
- expert_in: bfloat16 [64, 2048, 4096], P('ep', None, 'tp'), may hold values from -0.125 to 0.125
- expert_out: bfloat16 [64, 4096, 2048], P('ep', 'tp'), may hold values from -0.09375 to 0.09375
Outputs:
- layer_out: bfloat16 [64, 256, 2048], P('ep', 'tp')
Inputs may be any that keep to these rules, and one draw needn't show every extreme that they name: `expert_ids`: among the 128 tokens of one device (aligned blocks of token rows), at most 6 name any one expert; a token's two experts differ; every expert is named somewhere.
All inputs are finite; a program needn't handle non-finite values. No bound on the sum of `keep_mask` on one device may be relied on, other than what follows from the above.
Results may differ from a plain program's by a relative error of at most 0.0054.
Values may be sent and summed in bfloat16 or wider, within the bound.
No kernel may reach another device: no remote copies, remote signals or barrier semaphores. Data moves between devices by JAX's collectives and lax.ppermute only.
A program may use at most 128 MiB of HBM per device.

v0:
```python
import jax
import jax.numpy as jnp
from jax import lax
from jax.sharding import PartitionSpec as P


def expert_ffn(picked_rows, weight_in, weight_out):
    hidden = jnp.maximum(
        jnp.einsum("smd,df->smf", picked_rows, weight_in, preferred_element_type=jnp.float32), 0.0
    ).astype(jnp.bfloat16)
    return jnp.einsum("smf,fd->smd", hidden, weight_out, preferred_element_type=jnp.float32)


def body(
    context,
    out_weight,
    residual_in,
    norm_gain,
    expert_ids,
    gate_weights,
    keep_mask,
    expert_in,
    expert_out,
):
    tok_rows = residual_in.shape[1]
    feature_count = residual_in.shape[2]
    local_context = context[0]
    attended = lax.psum_scatter(
        jnp.dot(local_context, out_weight, preferred_element_type=jnp.float32),
        "tp",
        scatter_dimension=0,
        tiled=True,
    )
    stream = (residual_in[0].astype(jnp.float32) + attended).astype(jnp.bfloat16)
    stream_f32 = stream.astype(jnp.float32)
    average = jnp.mean(stream_f32, axis=1, keepdims=True)
    centred = stream_f32 - average
    variance = jnp.mean(centred * centred, axis=1, keepdims=True)
    normed = (centred / jnp.sqrt(variance + 1e-05) * norm_gain[None, :]).astype(jnp.bfloat16)
    expert_count = lax.axis_size("ep")
    capacity = 3 * tok_rows // expert_count
    total_slots = expert_count * capacity
    routed = expert_ids[0].reshape(-1)
    kept_flags = keep_mask[0].reshape(-1)
    assign_count = routed.shape[0]
    onehot = (routed[:, None] == jnp.arange(expert_count, dtype=jnp.int32)[None, :]).astype(
        jnp.int32
    ) * kept_flags[:, None]
    rank_table = jnp.cumsum(onehot, axis=0) - onehot
    rank_own = jnp.sum(rank_table * onehot, axis=1)
    slot_index = jnp.where(kept_flags > 0, routed * capacity + rank_own, -1)
    slot_match = (slot_index[None, :] == jnp.arange(total_slots, dtype=jnp.int32)[:, None]).astype(
        jnp.int32
    )
    source = jnp.sum(slot_match * jnp.arange(assign_count, dtype=jnp.int32)[None, :], axis=1)
    filled = jnp.sum(slot_match, axis=1)
    outgoing = jnp.where(filled[:, None] > 0, normed[source // 2], jnp.zeros((), jnp.bfloat16))
    outgoing = outgoing.reshape(expert_count, capacity, feature_count)
    weight_in = expert_in[0]
    weight_out = expert_out[0]
    doubled = jnp.concatenate([outgoing, outgoing], axis=0)
    partial_value = expert_ffn(
        lax.all_to_all(doubled, ("tp", "ep"), split_axis=0, concat_axis=0, tiled=True),
        weight_in,
        weight_out,
    )
    halves_back = lax.all_to_all(
        partial_value, ("tp", "ep"), split_axis=0, concat_axis=0, tiled=True
    )
    returned = jnp.sum(
        halves_back.reshape(2, expert_count, capacity, feature_count), axis=0
    ).astype(jnp.bfloat16)
    returned = returned.reshape(total_slots, feature_count)
    pulled = returned[jnp.maximum(slot_index, 0)].astype(jnp.float32)
    gate_flat = jnp.where(kept_flags > 0, gate_weights[0].reshape(-1), 0.0)
    mixed = jnp.sum((gate_flat[:, None] * pulled).reshape(tok_rows, 2, feature_count), axis=1)
    layer_out = (stream_f32 + mixed).astype(jnp.bfloat16)
    return layer_out[None]


def solution(mesh):
    return jax.shard_map(
        body,
        mesh=mesh,
        in_specs=(
            P("ep", None, "tp"),
            P("tp", None),
            P("ep", "tp", None),
            P(),
            P("ep", "tp", None),
            P("ep", "tp", None),
            P("ep", "tp", None),
            P("ep", None, "tp"),
            P("ep", "tp", None),
        ),
        out_specs=P("ep", "tp", None),
        check_vma=False,
    )
```

profile of v0, /device:TPU:19, one launch (start us, length us, event | category | flops | bytes accessed | tf_op | source)
XLA Modules:
  0.0 290.2 jit_solution(18252746649218533198)
XLA Ops:
  6.5 0.0 copy-start
  6.5 0.0 copy-start.4
  6.5 0.0 copy-start.5
  6.5 0.0 copy-start.2
  6.5 0.0 reduce-scatter.2.cloned.1.call-start
  6.6 1.0 copy-done
  7.6 4.8 %fusion.19 = f32[256,2048]{1,0:T(8,128)} fusion(bf16[1024,2048]{1,0:T(8,128)(2,1)} %param.10, bf16[1,256,1024]{2,1,0:T(8,128)(2,1)S(1)} %copy-done), kind=kOutput, calls=%fused_computation.25 | convolution fusion | flops 1073741824 | bytes 6815744 | tf_op jit(solution)/shard_map/dot_general | solution.py:29
  12.4 0.0 copy-start.3
  12.4 0.0 reduce-scatter.2.cloned.1.call-update
  12.4 0.0 copy-done.4
  12.4 0.1 copy.45
  12.5 0.1 mul.72
  12.7 0.1 reshape_squeeze.7
  12.8 0.0 copy-done.5
  12.8 0.1 copy.46
  12.9 0.1 eq.36
  13.1 0.1 reshape_squeeze.8
  13.2 0.6 reduce-window.6
  13.8 0.2 slice_reduce_fusion
  14.1 0.1 fusion.21
  14.2 0.2 convert_reduce_fusion.1
  14.4 0.2 gt.44
  14.6 13.1 %reduce-scatter.2.cloned.1.call-done = f32[128,2048]{1,0:T(8,128)} async-done(((f32[256,2048]{1,0:T(8,128)}), f32[128,2048]{1,0:T(8,128)}) %reduce-scatter.2.cloned.1.call-update) | async-done | bytes 1048592 | tf_op jit(solution)/shard_map/reduce_scatter | solution.py:28
  27.7 0.0 copy-done.2
  27.7 1.4 convert_reduce_fusion
  29.1 0.3 fusion.13
  29.4 0.0 copy-done.3
  29.4 0.2 fusion.15
  29.7 3.1 %gather_fusion = bf16[384,2048]{1,0:T(8,128)(2,1)} fusion(bf16[128,2048]{1,0:T(8,128)(2,1)S(1)} %fusion.15, s32[1024]{0:T(1024)S(1)} %pad_clamp_fusion.1), kind=kCustom, calls=%fused_computation | custom fusion | bytes 3147264 | tf_op jit(solution)/shard_map/gather | solution.py:57
  32.8 2.5 gather.9
  35.3 0.3 broadcast_select_fusion
  35.6 0.8 pad_maximum_fusion
  36.4 64.6 %all_to_all.10 = bf16[128,6,2048]{2,1,0:T(8,128)(2,1)} all-to-all(bf16[128,6,2048]{2,1,0:T(8,128)(2,1)S(1)} %pad_maximum_fusion), channel_id=1, replica_groups=mesh['tp'=2,'ep'=64] {'tp','ep'}, dimensions={0} | all-to-all | bytes 6291456 | tf_op jit(solution)/shard_map/all_to_all | solution.py:63
  101.0 24.9 %fusion = f32[128,6,2048]{2,0,1:T(8,128)} fusion(bf16[1,2048,2048]{2,1,0:T(8,128)(2,1)} %param.17, bf16[1,2048,2048]{2,1,0:T(8,128)(2,1)} %param.16, bf16[128,6,2048]{2,1,0:T(8,128)(2,1)} %all_to_all.10), kind=kOutput, calls=%fused_computation.2 | convolution fusion | flops 12888047616 | bytes 26214400 | tf_op jit(solution)/shard_map/smf,fd->smd/dot_general | solution.py:11
  125.9 10.0 %copy.51 = f32[128,6,2048]{2,1,0:T(8,128)} copy(f32[128,6,2048]{2,0,1:T(8,128)} %fusion) | data formatting | bytes 12582912 | tf_op jit(solution)/shard_map/smf,fd->smd/dot_general | solution.py:11
  135.9 0.0 copy-start.6
  135.9 7.3 %all-to-all-start.1 = ((f32[128,6,2048]{2,1,0:T(8,128)}), f32[128,6,2048]{2,1,0:T(8,128)}, u32[]{:S(2)}, u32[]{:S(2)}) async-start(f32[128,6,2048]{2,1,0:T(8,128)} %copy.51), calls=%async_computation.2 | async-start | bytes 16777216 | tf_op jit(solution)/shard_map/all_to_all | solution.py:67
  143.2 0.0 copy-done.6
  143.2 0.1 copy.54
  143.3 0.1 gt.46
  143.5 0.1 copy.55
  143.6 0.1 mul.85
  143.7 0.1 copy.44
  143.9 119.0 %all-to-all-done.1 = f32[128,6,2048]{2,1,0:T(8,128)} async-done(((f32[128,6,2048]{2,1,0:T(8,128)}), f32[128,6,2048]{2,1,0:T(8,128)}, u32[]{:S(2)}, u32[]{:S(2)}) %all-to-all-start.1) | async-done | bytes 6291488 | tf_op jit(solution)/shard_map/all_to_all | solution.py:67
  262.9 5.9 %reduce_sum.73 = bf16[64,6,2048]{2,1,0:T(8,128)(2,1)S(1)} reduce(f32[2,64,6,2048]{3,2,1,0:T(8,128)} %bitcast.8, f32[]{:T(128)} %constant.17.clone.1), dimensions={0}, to_apply=%region_8.9 | reduce | flops 786432 | bytes 7864324 | tf_op jit(solution)/shard_map/reduce_sum | solution.py:70
  268.8 0.9 copy.63
  269.7 2.2 copy.53
  271.9 2.6 convert_element_type.47
  274.5 0.0 copy-start.1
  274.5 2.3 gather_fusion.1
  276.9 2.4 reshape.192
  279.3 3.2 %multiply_reduce_fusion = f32[128,2048]{1,0:T(8,128)S(1)} fusion(f32[128,2,2048]{2,1,0:T(2,128)S(1)} %reshape.192, f32[128,2]{1,0:T(8,128)S(1)} %copy.44), kind=kLoop, calls=%fused_computation.11 | loop fusion | flops 786432 | bytes 3146752 | tf_op jit(solution)/shard_map/reduce_sum | solution.py:76
  282.4 0.9 fusion.18
  283.4 0.0 copy-done.1
  (13 shorter events, 0.1 us)
Async XLA Ops:
  6.5 1.0 copy-start
  6.5 5.9 %copy-start.4 = (s32[1,128,2]{1,2,0:T(2,128)S(1)}, s32[1,128,2]{1,2,0:T(2,128)}, u32[]{:S(2)}) copy-start(s32[1,128,2]{1,2,0:T(2,128)} %param.15) | copy-start | bytes 3076
  6.5 6.3 %copy-start.5 = (s32[1,128,2]{1,2,0:T(2,128)S(1)}, s32[1,128,2]{1,2,0:T(2,128)}, u32[]{:S(2)}) copy-start(s32[1,128,2]{1,2,0:T(2,128)} %param.13) | copy-start | bytes 3076
  6.5 21.1 %copy-start.2 = (bf16[1,128,2048]{2,1,0:T(8,128)(2,1)S(1)}, bf16[1,128,2048]{2,1,0:T(8,128)(2,1)}, u32[]{:S(2)}) copy-start(bf16[1,128,2048]{2,1,0:T(8,128)(2,1)} %param.11) | copy-start | bytes 1572868
  6.5 21.1 %reduce-scatter.2.cloned.1.call-start = ((), (), s32[]{:S(2)}) async-start(), calls=%async_computation.3 | async-start | bytes 3145728 | tf_op jit(solution)/shard_map/reduce_scatter | solution.py:28
  12.4 17.1 %copy-start.3 = (f32[2048]{0:T(1024)S(1)}, f32[2048]{0:T(1024)}, u32[]{:S(2)}) copy-start(f32[2048]{0:T(1024)} %param.12) | copy-start | bytes 24580
  135.9 7.3 %copy-start.6 = (f32[1,128,2]{1,2,0:T(2,128)S(1)}, f32[1,128,2]{1,2,0:T(2,128)}, u32[]{:S(2)}) copy-start(f32[1,128,2]{1,2,0:T(2,128)} %param.14) | copy-start | bytes 3076
  135.9 127.0 %all-to-all-start.1 = ((f32[128,6,2048]{2,1,0:T(8,128)}), f32[128,6,2048]{2,1,0:T(8,128)}, u32[]{:S(2)}, u32[]{:S(2)}) async-start(f32[128,6,2048]{2,1,0:T(8,128)} %copy.51), calls=%async_computation.2 | async-start | bytes 16777216 | tf_op jit(solution)/shard_map/all_to_all | solution.py:67
  274.5 8.8 %copy-start.1 = (bf16[1,256,1024]{2,1,0:T(8,128)(2,1)S(1)}, bf16[1,256,1024]{2,1,0:T(8,128)(2,1)}, u32[]{:S(2)}) copy-start(bf16[1,256,1024]{2,1,0:T(8,128)(2,1)} %param.9) | copy-start | bytes 1572868
Sparse Core Ops, SparseCore 0:
  12.5 15.1 reduce-scatter.1
where the time goes:
time: 291 us; the launch traced here: 290 us
  waiting for transfers between devices  132 us (45%)
  blocking collectives  64.6 us (22%)
  matrix products  29.7 us (10%)
  local copies, waits for them, and re-layouts  28.8 us (10%)
  other arithmetic  14.2 us (5%)
  between operations  13.6 us (5%)
  starting transfers between devices  7.31 us (3%)
    all_to_all x1, waiting for transfers between devices, body(): lax.all_to_all(partial_value, ('tp', 'ep'), split_axis=0, concat_axis=0,...  119 us
    all_to_all x1, blocking collectives, body(): lax.all_to_all(doubled, ('tp', 'ep'), split_axis=0, concat_axis=0, tiled=...  64.6 us
    dot_general x1, matrix products, expert_ffn(): jnp.einsum('smf,fd->smd', hidden, weight_out, preferred_element_type=jnp....  24.9 us
    reduce_scatter x1, waiting for transfers between devices, body(): lax.psum_scatter(jnp.dot(local_context, out_weight, preferred_element_typ...  13.1 us
    dot_general x1, local copies, waits for them, and re-layouts, expert_ffn(): jnp.einsum('smf,fd->smd', hidden, weight_out, preferred_element_type=jnp....  10 us
    all_to_all x1, starting transfers between devices, body(): lax.all_to_all(partial_value, ('tp', 'ep'), split_axis=0, concat_axis=0,...  7.28 us
    reduce_sum x1, other arithmetic, body(): jnp.sum(halves_back.reshape(2, expert_count, capacity, feature_count), ax...  5.94 us
  transfers between devices with their start and end apart: 2, of which 2 were waited for; matrix products, arithmetic and copies ran while one was open for 1% of the time, Pallas kernels for 0%

commit v1 on v0

v1 whole, which is shorter than its diff:
```python
import functools

import jax
import jax.numpy as jnp
from jax import lax
from jax.experimental import pallas as pl
from jax.experimental.pallas import tpu as pltpu
from jax.sharding import PartitionSpec as P

SLOT = 6
PACK = 8
F32, BF16 = jnp.float32, jnp.bfloat16
VMEM = pl.BlockSpec(memory_space=pltpu.VMEM)


def dot(a, b):
    return jnp.dot(a, b, preferred_element_type=F32)


def iota(shape, dim):
    return lax.broadcasted_iota(jnp.int32, shape, dim)


def places(ids, keep, experts, along):
    tokens = ids[0].shape[along]
    shape = (experts, tokens) if along == 1 else (tokens, experts)
    member = iota(shape, 1 - along)
    hot = [jnp.where((member == ids[k]) & (keep[k] > 0), 1.0, 0.0) for k in (0, 1)]
    older = (iota((tokens, tokens), 1 - along) < iota((tokens, tokens), along)).astype(F32).astype(BF16)
    out = []
    base = 0.0
    for k in (0, 1):
        sent = hot[k].astype(BF16)
        before = (dot(sent, older) if along == 1 else dot(older, sent)) + base
        rank = jnp.sum(hot[k] * before, axis=1 - along, keepdims=True).astype(jnp.int32)
        base = base + jnp.sum(hot[k], axis=along, keepdims=True)
        late = jnp.where(rank >= SLOT // 2, 1, 0)
        block = rank - (SLOT // 2) * late
        kept = keep[k] > 0
        main = jnp.where(kept, ids[k] * PACK + rank, -1)
        tail = ids[k] * PACK + SLOT + late
        out.append((main, [jnp.where(kept & (block == j), tail, -1) for j in range(3)]))
    return out


def pack_kernel(experts, own_ref, recv_ref, res_ref, gain_ref, ids_ref, keep_ref, stream_ref, packed_ref):
    stream = (res_ref[...].astype(F32) + (own_ref[...] + recv_ref[...])).astype(BF16)
    stream_ref[...] = stream
    value = stream.astype(F32)
    count = value.shape[1]
    centred = value - jnp.sum(value, axis=1, keepdims=True) / count
    variance = jnp.sum(centred * centred, axis=1, keepdims=True) / count
    normed = (centred / jnp.sqrt(variance + 1e-05) * gain_ref[...]).astype(BF16)
    ids = [ids_ref[k : k + 1, :] for k in (0, 1)]
    keep = [keep_ref[k : k + 1, :] for k in (0, 1)]
    (main0, tails0), (main1, tails1) = places(ids, keep, experts, 1)
    rows = iota((experts * PACK, ids[0].shape[1]), 0)

    def choose(a, b):
        return jnp.where((rows == a) | (rows == b), 1.0, 0.0).astype(BF16)

    main = choose(main0, main1)
    wide = count * SLOT // PACK
    part = wide // 3
    for j in range(3):
        packed_ref[:, j * part : (j + 1) * part] = (
            dot(main, normed[:, j * part : (j + 1) * part])
            + dot(choose(tails0[j], tails1[j]), normed[:, wide:])
        ).astype(BF16)


def combine_kernel(experts, packed_ref, stream_ref, ids_ref, keep_ref, gate_ref, out_ref):
    ids = [ids_ref[:, k : k + 1] for k in (0, 1)]
    keep = [keep_ref[:, k : k + 1] for k in (0, 1)]
    (main0, tails0), (main1, tails1) = places(ids, keep, experts, 0)
    tokens = ids[0].shape[0]
    columns = iota((tokens, experts * PACK), 1)

    def choose(a):
        return jnp.where(columns == a, 1.0, 0.0).astype(BF16)

    gates = [gate_ref[:, k : k + 1] for k in (0, 1)]
    wide = packed_ref.shape[1]
    part = wide // 3
    mains = [choose(main0), choose(main1)]
    tails = [[choose(tails0[j]), choose(tails1[j])] for j in range(3)]
    for j in range(3):
        block = packed_ref[:, j * part : (j + 1) * part]
        mixed = gates[0] * dot(mains[0], block) + gates[1] * dot(mains[1], block)
        at = slice(j * part, (j + 1) * part)
        out_ref[:, at] = (stream_ref[:, at].astype(F32) + mixed).astype(BF16)
    mixed = 0.0
    for k in (0, 1):
        mixed += gates[k] * sum(dot(tails[j][k], packed_ref[:, j * part : (j + 1) * part]) for j in range(3))
    out_ref[:, wide:] = (stream_ref[:, wide:].astype(F32) + mixed).astype(BF16)


SOURCES = 32


def unpack_into(packed_ref, rows_ref):
    tall, short = SOURCES * PACK, SOURCES * SLOT
    wide = packed_ref.shape[1]
    part = wide // 3
    row, col = iota((short, tall), 0), iota((short, tall), 1)
    source, at = col >> 3, col & 7
    first = row - SLOT * source
    main = jnp.where((at < SLOT) & (first == at), 1.0, 0.0).astype(BF16)
    tails = [
        jnp.where((at >= SLOT) & (first == (at - SLOT) * 3 + j), 1.0, 0.0).astype(BF16)
        for j in range(3)
    ]
    for g in range(packed_ref.shape[0] // tall):
        block = packed_ref[g * tall : (g + 1) * tall, :]
        at_rows = slice(g * short, (g + 1) * short)
        rows_ref[at_rows, :wide] = dot(main, block).astype(BF16)
        rows_ref[at_rows, wide:] = sum(
            dot(tails[j], block[:, j * part : (j + 1) * part]) for j in range(3)
        ).astype(BF16)


def ffn_kernel(packed_ref, in_ref, out_ref, result_ref, rows_ref, acc_ref):
    step = pl.program_id(0)

    @pl.when(step == 0)
    def _():
        unpack_into(packed_ref, rows_ref)

    hidden = jnp.maximum(dot(rows_ref[...], in_ref[...]), 0.0).astype(BF16)
    term = dot(hidden, out_ref[...])

    @pl.when(step == 0)
    def _():
        acc_ref[...] = term

    @pl.when(step > 0)
    def _():
        acc_ref[...] += term

    @pl.when(step == pl.num_programs(0) - 1)
    def _():
        result_ref[...] = acc_ref[...].astype(result_ref.dtype)


def ffn(packed, weight_in, weight_out, dtype, tile=512):
    rows = packed.shape[0] * SLOT // PACK
    features, units = weight_in.shape
    return pl.pallas_call(
        ffn_kernel,
        grid=(units // tile,),
        in_specs=[
            pl.BlockSpec(packed.shape, lambda f: (0, 0), pipeline_mode=pl.Buffered(1)),
            pl.BlockSpec((features, tile), lambda f: (0, f)),
            pl.BlockSpec((tile, features), lambda f: (f, 0)),
        ],
        out_specs=pl.BlockSpec((rows, features), lambda f: (0, 0)),
        out_shape=jax.ShapeDtypeStruct((rows, features), dtype),
        scratch_shapes=[pltpu.VMEM((rows, features), BF16), pltpu.VMEM((rows, features), F32)],
        compiler_params=pltpu.CompilerParams(vmem_limit_bytes=48 << 20),
        cost_estimate=pl.CostEstimate(
            flops=4 * rows * features * units, bytes_accessed=4 * features * units, transcendentals=0
        ),
        name="ffn",
    )(packed, weight_in, weight_out)


def repack_kernel(own_ref, recv_ref, packed_ref):
    tall, short = SOURCES * PACK, SOURCES * SLOT
    wide = packed_ref.shape[1]
    part = wide // 3
    row, col = iota((tall, short), 1), iota((tall, short), 0)
    source, at = col >> 3, col & 7
    first = row - SLOT * source
    main = jnp.where((at < SLOT) & (first == at), 1.0, 0.0).astype(BF16)
    tails = [
        jnp.where((at >= SLOT) & (first == (at - SLOT) * 3 + j), 1.0, 0.0).astype(BF16)
        for j in range(3)
    ]
    for g in range(packed_ref.shape[0] // tall):
        at_rows = slice(g * short, (g + 1) * short)
        block = (own_ref[at_rows, :] + recv_ref[at_rows, :].astype(F32)).astype(BF16)
        for j in range(3):
            packed_ref[g * tall : (g + 1) * tall, j * part : (j + 1) * part] = (
                dot(main, block[:, j * part : (j + 1) * part]) + dot(tails[j], block[:, wide:])
            ).astype(BF16)


def whole(kernel, out_shape, name, flops, *args):
    return pl.pallas_call(
        kernel,
        in_specs=[VMEM] * len(args),
        out_specs=jax.tree.map(lambda _: VMEM, out_shape),
        out_shape=out_shape,
        compiler_params=pltpu.CompilerParams(vmem_limit_bytes=48 << 20),
        cost_estimate=pl.CostEstimate(
            flops=flops, bytes_accessed=sum(a.size * a.dtype.itemsize for a in args), transcendentals=0
        ),
        name=name,
    )(*args)


SWAP = [(0, 1), (1, 0)]


def body(context, out_weight, residual_in, norm_gain, expert_ids, gate_weights, keep_mask, expert_in, expert_out):
    tokens, features = residual_in.shape[1:]
    experts = lax.axis_size("ep")
    core = lax.axis_index("tp")
    other_half = dot(lax.dynamic_slice_in_dim(context[0], (1 - core) * tokens, tokens), out_weight)
    recv = lax.ppermute(other_half, "tp", SWAP)
    own = dot(lax.dynamic_slice_in_dim(context[0], core * tokens, tokens), out_weight)
    wide = features * SLOT // PACK
    packed_shape = jax.ShapeDtypeStruct((experts * PACK, wide), BF16)
    stream, outgoing = whole(
        functools.partial(pack_kernel, experts),
        (jax.ShapeDtypeStruct((tokens, features), BF16), packed_shape),
        "pack",
        4 * tokens * experts * PACK * wide,
        own, recv, residual_in[0], norm_gain[None, :], expert_ids[0].T, keep_mask[0].T,
    )

    def exchange(packed):
        blocks = packed.reshape(experts, PACK, wide)
        return lax.all_to_all(blocks, "ep", split_axis=0, concat_axis=0, tiled=True).reshape(packed.shape)

    rows = exchange(outgoing)
    rows_other = lax.ppermute(rows, "tp", SWAP)
    part_own = ffn(rows, expert_in[0], expert_out[0], F32)
    part_other = ffn(rows_other, expert_in[0], expert_out[0], BF16)
    part_recv = lax.ppermute(part_other, "tp", SWAP)
    results = whole(
        repack_kernel, packed_shape, "repack", 4 * SOURCES * SLOT * experts * PACK * wide, part_own, part_recv
    )
    returned = exchange(results)
    return whole(
        functools.partial(combine_kernel, experts),
        jax.ShapeDtypeStruct((tokens, features), BF16),
        "combine",
        8 * tokens * experts * PACK * wide,
        returned, stream, expert_ids[0], keep_mask[0], gate_weights[0],
    )[None]


def solution(mesh):
    return jax.shard_map(
        body,
        mesh=mesh,
        in_specs=(
            P("ep", None, "tp"),
            P("tp", None),
            P("ep", "tp", None),
            P(),
            P("ep", "tp", None),
            P("ep", "tp", None),
            P("ep", "tp", None),
            P("ep", None, "tp"),
            P("ep", "tp", None),
        ),
        out_specs=P("ep", "tp", None),
        check_vma=False,
    )
```

time: 291 us -> 112 us (0.38)
  the two profiles are of different devices: /device:TPU:19 before, /device:TPU:0 now
where the time goes in v1:
time: 112 us
  blocking collectives  36.4 us (32%)
  Pallas kernels  31.6 us (28%)
  waiting for transfers between devices  28.3 us (25%)
  matrix products  6.81 us (6%)
  starting transfers between devices  5.54 us (5%)
  local copies, waits for them, and re-layouts  3.14 us (3%)
    all_to_all x1, blocking collectives, exchange(): lax.all_to_all(blocks, 'ep', split_axis=0, concat_axis=0, tiled=True)  36.4 us
    all_to_all x1, waiting for transfers between devices, exchange(): lax.all_to_all(blocks, 'ep', split_axis=0, concat_axis=0, tiled=True)  24.8 us
    pallas_call x2, Pallas kernels, ffn(): pl.pallas_call(ffn_kernel, grid=(units // tile,), in_specs=[pl.BlockSpec(...  23.7 us
    pallas_call x3, Pallas kernels, whole(): pl.pallas_call(kernel, in_specs=[VMEM] * len(args), out_specs=jax.tree.ma...  7.97 us
    dot_general x2, matrix products, dot(): return jnp.dot(a, b, preferred_element_type=F32)  6.81 us
    all_to_all x1, starting transfers between devices, exchange(): lax.all_to_all(blocks, 'ep', split_axis=0, concat_axis=0, tiled=True)  5.32 us
    ppermute x1, waiting for transfers between devices, body(): rows_other = lax.ppermute(rows, 'tp', SWAP)  3.41 us
    unnamed x17, local copies, waits for them, and re-layouts  3.02 us
  transfers between devices with their start and end apart: 4, of which 2 were waited for; matrix products, arithmetic and copies ran while one was open for 3% of the time, Pallas kernels for 11%

profile of v1, /device:TPU:0, one launch (start us, length us, event | category | flops | bytes accessed | tf_op | source)
XLA Modules:
  0.0 111.9 jit_solution(16979232046497126183)
XLA Ops:
  0.0 0.0 copy-start
  0.0 0.0 copy-start.4
  0.0 0.0 copy-start.5
  0.0 1.0 copy-done
  1.0 3.9 %fusion = f32[128,2048]{1,0:T(8,128)} fusion(bf16[1024,2048]{1,0:T(8,128)(2,1)} %param.10, bf16[1,256,1024]{2,1,0:T(8,128)(2,1)S(1)} %copy-done, s32[]{:T(128)S(6)} %select_n.7), kind=kOutput, calls=%fused_computation | convolution fusion | flops 536870912 | bytes 5505028 | tf_op jit(solution)/shard_map/dot_general | solution.py:17
  4.9 0.0 copy-start.2
  4.9 0.0 copy-start.3
  4.9 0.0 collective-permute-start
  4.9 0.0 copy-done.4
  4.9 0.1 copy.10
  5.0 0.1 copy.12.ids_ref
  5.1 0.0 copy-done.5
  5.1 0.1 copy.11
  5.2 0.1 copy.13.keep_ref
  5.3 2.9 %fusion.2.own_ref = f32[128,2048]{1,0:T(8,128)S(1)} fusion(bf16[1024,2048]{1,0:T(8,128)(2,1)} %param.10, bf16[1,256,1024]{2,1,0:T(8,128)(2,1)S(1)} %copy-done, s32[]{:T(128)S(6)} %select_n.6), kind=kOutput, calls=%fused_computation.2 | convolution fusion | flops 536870912 | bytes 5505028 | tf_op jit(solution)/shard_map/dot_general | solution.py:17
  8.2 0.0 collective-permute-done.recv_ref
  8.2 0.0 copy-done.2
  8.3 0.0 copy-done.3
  8.3 1.5 %pack.1 = (bf16[128,2048]{1,0:T(8,128)(2,1)S(1)}, bf16[512,1536]{1,0:T(8,128)(2,1)S(1)}) custom-call(f32[128,2048]{1,0:T(8,128)S(1)} %fusion.2.own_ref, f32[128,2048]{1,0:T(8,128)S(1)} %collective-permute-done.recv_ref, bf16[128,2048]{1,0:T(8,128)(2,1)S(1)} %bitcast.28, f32[1,2048]{1,0:T(1,128)S(1)} %bitcast.34, s32[2,128]{1,0:T(2,128)S(1)} %copy.12.ids_ref, ...), custom_call_target="tpu_custom_call" | custom-call | flops 402653184 | bytes 2631680 | tf_op jit(solution)/shard_map/pack/pallas_call | solution.py:189
  9.8 36.4 %all_to_all.10 = bf16[64,8,1536]{2,1,0:T(8,128)(2,1)S(1)} all-to-all(bf16[64,8,1536]{2,1,0:T(8,128)(2,1)S(1)} %bitcast.27), channel_id=1, replica_groups=mesh['tp'=2,'ep'=64] {'ep'}, dimensions={0} | all-to-all | bytes 3145728 | tf_op jit(solution)/shard_map/all_to_all | solution.py:224
  46.2 0.0 collective-permute-start.1
  46.2 3.4 %collective-permute-done.1.packed_ref = bf16[512,1536]{1,0:T(8,128)(2,1)S(1)} collective-permute-done((bf16[512,1536]{1,0:T(8,128)(2,1)S(1)}, bf16[512,1536]{1,0:T(8,128)(2,1)S(1)}, u32[]{:S(2)}, u32[]{:S(2)}) %collective-permute-start.1) | collective-permute-done | bytes 1572896 | tf_op jit(solution)/shard_map/ppermute | solution.py:227
  49.6 11.8 %ffn.3 = bf16[384,2048]{1,0:T(8,128)(2,1)S(1)} custom-call(bf16[512,1536]{1,0:T(8,128)(2,1)S(1)} %collective-permute-done.1.packed_ref, bf16[2048,2048]{1,0:T(8,128)(2,1)} %bitcast.35, bf16[2048,2048]{1,0:T(8,128)(2,1)} %bitcast.37), custom_call_target="tpu_custom_call" | custom-call | flops 6442450944 | bytes 16777216 | tf_op jit(solution)/shard_map/ffn/pallas_call | solution.py:148
  61.4 0.2 collective-permute-start.2
  61.6 11.9 %ffn.2.own_ref = f32[384,2048]{1,0:T(8,128)S(1)} custom-call(bf16[512,1536]{1,0:T(8,128)(2,1)S(1)} %bitcast.25, bf16[2048,2048]{1,0:T(8,128)(2,1)} %bitcast.36, bf16[2048,2048]{1,0:T(8,128)(2,1)} %bitcast.38), custom_call_target="tpu_custom_call" | custom-call | flops 6442450944 | bytes 16777216 | tf_op jit(solution)/shard_map/ffn/pallas_call | solution.py:148
  73.5 0.0 copy-start.1
  73.5 1.6 %copy-done.1 = f32[384,2048]{1,0:T(8,128)} copy-done((f32[384,2048]{1,0:T(8,128)}, f32[384,2048]{1,0:T(8,128)S(1)}, u32[]{:S(2)}) %copy-start.1) | copy-done | bytes 3145752
  75.1 0.0 copy-start.6
  75.1 0.0 collective-permute-done.2.recv_ref
  75.1 4.1 %repack.1 = bf16[512,1536]{1,0:T(8,128)(2,1)} custom-call(f32[384,2048]{1,0:T(8,128)} %copy-done.1, bf16[384,2048]{1,0:T(8,128)(2,1)S(1)} %collective-permute-done.2.recv_ref), custom_call_target="tpu_custom_call" | custom-call | flops 603979776 | bytes 4718592 | tf_op jit(solution)/shard_map/repack/pallas_call | solution.py:189
  79.2 5.3 %all-to-all-start.1 = ((bf16[64,8,1536]{2,1,0:T(8,128)(2,1)}), bf16[64,8,1536]{2,1,0:T(8,128)(2,1)S(1)}, u32[]{:S(2)}, u32[]{:S(2)}) async-start(bf16[64,8,1536]{2,1,0:T(8,128)(2,1)} %bitcast.12), calls=%async_computation.1 | async-start | bytes 3145728 | tf_op jit(solution)/shard_map/all_to_all | solution.py:224
  84.6 0.0 copy-done.6
  84.6 0.1 copy.14
  84.7 24.8 %all-to-all-done.1 = bf16[64,8,1536]{2,1,0:T(8,128)(2,1)S(1)} async-done(((bf16[64,8,1536]{2,1,0:T(8,128)(2,1)}), bf16[64,8,1536]{2,1,0:T(8,128)(2,1)S(1)}, u32[]{:S(2)}, u32[]{:S(2)}) %all-to-all-start.1) | async-done | bytes 1572896 | tf_op jit(solution)/shard_map/all_to_all | solution.py:224
  109.5 2.4 %combine.1 = bf16[128,2048]{1,0:T(8,128)(2,1)} custom-call(bf16[512,1536]{1,0:T(8,128)(2,1)S(1)} %bitcast.26, bf16[128,2048]{1,0:T(8,128)(2,1)S(1)} %get-tuple-element.8.stream_ref, s32[128,2]{1,0:T(8,128)S(1)} %bitcast.30, s32[128,2]{1,0:T(8,128)S(1)} %bitcast.32, f32[128,2]{1,0:T(8,128)S(1)} %bitcast.33), custom_call_target="tpu_custom_call" | custom-call | flops 805306368 | bytes 2100224 | tf_op jit(solution)/shard_map/combine/pallas_call | solution.py:189
Async XLA Ops:
  0.0 1.0 copy-start
  0.0 4.9 %copy-start.4 = (s32[1,128,2]{1,2,0:T(2,128)S(1)}, s32[1,128,2]{1,2,0:T(2,128)}, u32[]{:S(2)}) copy-start(s32[1,128,2]{1,2,0:T(2,128)} %param.13) | copy-start | bytes 3076
  0.0 5.1 %copy-start.5 = (s32[1,128,2]{1,2,0:T(2,128)S(1)}, s32[1,128,2]{1,2,0:T(2,128)}, u32[]{:S(2)}) copy-start(s32[1,128,2]{1,2,0:T(2,128)} %param.15) | copy-start | bytes 3076
  4.9 3.3 %copy-start.2 = (bf16[1,128,2048]{2,1,0:T(8,128)(2,1)S(1)}, bf16[1,128,2048]{2,1,0:T(8,128)(2,1)}, u32[]{:S(2)}) copy-start(bf16[1,128,2048]{2,1,0:T(8,128)(2,1)} %param.11) | copy-start | bytes 1572868
  4.9 3.3 %copy-start.3 = (f32[2048]{0:T(1024)S(1)}, f32[2048]{0:T(1024)}, u32[]{:S(2)}) copy-start(f32[2048]{0:T(1024)} %param.12) | copy-start | bytes 24580
  4.9 3.3 %collective-permute-start = (f32[128,2048]{1,0:T(8,128)}, f32[128,2048]{1,0:T(8,128)S(1)}, u32[]{:S(2)}, u32[]{:S(2)}) collective-permute-start(f32[128,2048]{1,0:T(8,128)} %fusion), channel_id=1, source_target_pairs={{0,64},{64,0},{1,65},{65,1},{2,66},{66,2},{3,67},{67,3},{4,68},{68... | collective-permute-start | bytes 3145736 | tf_op jit(solution)/shard_map/ppermute | solution.py:210
  46.2 3.4 %collective-permute-start.1 = (bf16[512,1536]{1,0:T(8,128)(2,1)S(1)}, bf16[512,1536]{1,0:T(8,128)(2,1)S(1)}, u32[]{:S(2)}, u32[]{:S(2)}) collective-permute-start(bf16[512,1536]{1,0:T(8,128)(2,1)S(1)} %bitcast.24), channel_id=1, source_target_pairs={{0,64},{64,0},{1,65},{65,1},{2,66},{66,2},{3,67},{67,3},{4,68},{68... | collective-permute-start | bytes 4718600 | tf_op jit(solution)/shard_map/ppermute | solution.py:227
  61.4 13.7 %collective-permute-start.2 = (bf16[384,2048]{1,0:T(8,128)(2,1)S(1)}, bf16[384,2048]{1,0:T(8,128)(2,1)S(1)}, u32[]{:S(2)}, u32[]{:S(2)}) collective-permute-start(bf16[384,2048]{1,0:T(8,128)(2,1)S(1)} %ffn.3), channel_id=1, source_target_pairs={{0,64},{64,0},{1,65},{65,1},{2,66},{66,2},{3,67},{67,3},{4,68},{68... | collective-permute-start | bytes 4718600 | tf_op jit(solution)/shard_map/ppermute | solution.py:230
  73.5 1.6 %copy-start.1 = (f32[384,2048]{1,0:T(8,128)}, f32[384,2048]{1,0:T(8,128)S(1)}, u32[]{:S(2)}) copy-start(f32[384,2048]{1,0:T(8,128)S(1)} %ffn.2.own_ref) | copy-start | bytes 9437188
  75.1 9.4 %copy-start.6 = (f32[1,128,2]{1,2,0:T(2,128)S(1)}, f32[1,128,2]{1,2,0:T(2,128)}, u32[]{:S(2)}) copy-start(f32[1,128,2]{1,2,0:T(2,128)} %param.14) | copy-start | bytes 3076
  79.2 30.3 %all-to-all-start.1 = ((bf16[64,8,1536]{2,1,0:T(8,128)(2,1)}), bf16[64,8,1536]{2,1,0:T(8,128)(2,1)S(1)}, u32[]{:S(2)}, u32[]{:S(2)}) async-start(bf16[64,8,1536]{2,1,0:T(8,128)(2,1)} %bitcast.12), calls=%async_computation.1 | async-start | bytes 3145728 | tf_op jit(solution)/shard_map/all_to_all | solution.py:224

commit v2 on v0

v2 whole, which is shorter than its diff:
```python
import functools

import jax
import jax.numpy as jnp
from jax import lax
from jax.experimental import pallas as pl
from jax.experimental.pallas import tpu as pltpu
from jax.sharding import PartitionSpec as P


PACK = 8
CHUNKS = (4, 2)
SOURCES = 32
LIMIT = 40 << 20
F32, BF16 = jnp.float32, jnp.bfloat16
VMEM = pl.BlockSpec(memory_space=pltpu.VMEM)
HBM = pl.BlockSpec(memory_space=pltpu.HBM)
SWAP = [(0, 1), (1, 0)]
STARTS = [sum(CHUNKS[:c]) for c in range(len(CHUNKS))]


def dot(a, b):
    return jnp.dot(a, b, preferred_element_type=F32)


def iota(shape, dim):
    return lax.broadcasted_iota(jnp.int32, shape, dim)


def where_bf16(condition):
    return jnp.where(condition, 1.0, 0.0).astype(BF16)


def ranks(ids, keep, experts, along):
    tokens = ids[0].shape[along]
    shape = (experts, tokens) if along == 1 else (tokens, experts)
    member = iota(shape, 1 - along)
    hot = [jnp.where((member == ids[k]) & (keep[k] > 0), 1.0, 0.0) for k in (0, 1)]
    older = where_bf16(iota((tokens, tokens), 1 - along) < iota((tokens, tokens), along))
    out = []
    base = 0.0
    for k in (0, 1):
        sent = hot[k].astype(BF16)
        before = (dot(sent, older) if along == 1 else dot(older, sent)) + base
        out.append(jnp.sum(hot[k] * before, axis=1 - along, keepdims=True).astype(jnp.int32))
        base = base + jnp.sum(hot[k], axis=along, keepdims=True)
    return out


def packed_row(ids, keep, rank, chunk, piece):
    slots, slot = CHUNKS[chunk], rank - STARTS[chunk]
    inside = (keep > 0) & (slot >= 0) & (slot < slots)
    return jnp.where(inside, ids * PACK + slots * piece + slot, -1)


def pack_kernel(experts, own_ref, recv_ref, res_ref, gain_ref, ids_ref, keep_ref, stream_ref, *packed_refs):
    stream = (res_ref[...].astype(F32) + (own_ref[...] + recv_ref[...])).astype(BF16)
    stream_ref[...] = stream
    value = stream.astype(F32)
    tokens, features = value.shape
    centred = value - jnp.sum(value, axis=1, keepdims=True) / features
    variance = jnp.sum(centred * centred, axis=1, keepdims=True) / features
    normed = (centred / jnp.sqrt(variance + 1e-05) * gain_ref[...]).astype(BF16)
    ids = [ids_ref[k : k + 1, :] for k in (0, 1)]
    keep = [keep_ref[k : k + 1, :] for k in (0, 1)]
    rank = ranks(ids, keep, experts, 1)
    for chunk, slots in enumerate(CHUNKS):
        pieces = PACK // slots
        wide = features // pieces
        at = [
            jnp.concatenate([packed_row(ids[k], keep[k], rank[k], chunk, h) for h in range(pieces)], axis=1)
            for k in (0, 1)
        ]
        rows = iota((experts * PACK, tokens * pieces), 0)
        stacked = jnp.concatenate([normed[:, h * wide : (h + 1) * wide] for h in range(pieces)], axis=0)
        packed_refs[chunk][...] = dot(where_bf16((rows == at[0]) | (rows == at[1])), stacked).astype(BF16)


def combine_kernel(experts, *refs):
    packed_refs = refs[: len(CHUNKS)]
    stream_ref, ids_ref, keep_ref, gate_ref, out_ref = refs[len(CHUNKS) :]
    ids = [ids_ref[:, k : k + 1] for k in (0, 1)]
    keep = [keep_ref[:, k : k + 1] for k in (0, 1)]
    gate = [gate_ref[:, k : k + 1] for k in (0, 1)]
    rank = ranks(ids, keep, experts, 0)
    tokens, _ = stream_ref.shape
    columns = iota((2 * tokens, experts * PACK), 1)
    total = None
    for chunk, slots in enumerate(CHUNKS):
        pieces = PACK // slots
        packed = packed_refs[chunk][...]
        mixed = []
        for h in range(pieces):
            at = jnp.concatenate([packed_row(ids[k], keep[k], rank[k], chunk, h) for k in (0, 1)], axis=0)
            rows = dot(where_bf16(columns == at), packed)
            mixed.append(gate[0] * rows[:tokens] + gate[1] * rows[tokens:])
        mixed = jnp.concatenate(mixed, axis=1)
        total = mixed if total is None else total + mixed
    out_ref[...] = (stream_ref[...].astype(F32) + total).astype(BF16)


def unpack_matrix(slots, reverse):
    size = SOURCES * PACK
    shift = slots.bit_length() - 1
    row, col = iota((size, size), 1 if reverse else 0), iota((size, size), 0 if reverse else 1)
    source, at = col >> 3, col & 7
    piece, slot = at >> shift, at & (slots - 1)
    return where_bf16(row == piece * (SOURCES * slots) + slots * source + slot)


def ffn_kernel(slots, tile, own_ref, other_ref, in_hbm, out_hbm, own_out, other_out, in_ref, out_ref, rows_ref, hidden_ref, sems):
    _, units = in_hbm.shape
    steps_in, steps_out = units // tile, out_hbm.shape[1] // tile

    def copies(which, i):
        at = pl.ds(pl.multiple_of(i * tile, tile), tile)
        source, target = ((in_hbm, in_ref), (out_hbm, out_ref))[which]
        return pltpu.make_async_copy(source.at[:, at], target.at[:, at], sems.at[which * steps_in + i])

    for i in range(steps_in):
        copies(0, i).start()
    for i in range(steps_out):
        copies(1, i).start()
    tall, short = SOURCES * PACK, SOURCES * slots
    pieces = PACK // slots
    wide = own_ref.shape[1]
    groups = own_ref.shape[0] // tall
    spread = unpack_matrix(slots, False)
    for s, ref in enumerate((own_ref, other_ref)):
        for g in range(groups):
            moved = dot(spread, ref[g * tall : (g + 1) * tall, :]).astype(BF16)
            for h in range(pieces):
                first = (s * groups + g) * short
                rows_ref[first : first + short, h * wide : (h + 1) * wide] = moved[h * short : (h + 1) * short]

    @pl.loop(0, steps_in)
    def _(i):
        copies(0, i).wait()
        at = pl.ds(pl.multiple_of(i * tile, tile), tile)
        hidden_ref[:, at] = jnp.maximum(dot(rows_ref[...], in_ref[:, at]), 0.0).astype(BF16)

    @pl.loop(0, steps_out)
    def _(i):
        copies(1, i).wait()
        at = pl.ds(pl.multiple_of(i * tile, tile), tile)
        rows_ref[:, at] = dot(hidden_ref[...], out_ref[:, at]).astype(BF16)

    gather = unpack_matrix(slots, True)
    for s, ref in enumerate((own_out, other_out)):
        for g in range(groups):
            first = (s * groups + g) * short
            stacked = jnp.concatenate(
                [rows_ref[first : first + short, h * wide : (h + 1) * wide] for h in range(pieces)], axis=0
            )
            ref[g * tall : (g + 1) * tall, :] = dot(gather, stacked).astype(BF16)


def ffn(slots, own, other, weight_in, weight_out, tile=512):
    rows = 2 * own.shape[0] * slots // PACK
    features, units = weight_in.shape
    return pl.pallas_call(
        functools.partial(ffn_kernel, slots, tile),
        in_specs=[VMEM, VMEM, HBM, HBM],
        out_specs=[VMEM, VMEM],
        out_shape=[jax.ShapeDtypeStruct(own.shape, BF16)] * 2,
        scratch_shapes=[
            pltpu.VMEM(weight_in.shape, BF16),
            pltpu.VMEM(weight_out.shape, BF16),
            pltpu.VMEM((rows, features), BF16),
            pltpu.VMEM((rows, units), BF16),
            pltpu.SemaphoreType.DMA((units // tile + features // tile,)),
        ],
        compiler_params=pltpu.CompilerParams(vmem_limit_bytes=LIMIT),
        cost_estimate=pl.CostEstimate(
            flops=4 * rows * features * units, bytes_accessed=4 * features * units, transcendentals=0
        ),
    )(own, other, weight_in, weight_out)


def project_kernel(core_ref, context_ref, weight_ref, own_ref, other_ref):
    both = dot(context_ref[...], weight_ref[...])
    tokens = own_ref.shape[0]
    first = core_ref[0] == 0
    own_ref[...] = jnp.where(first, both[:tokens], both[tokens:])
    other_ref[...] = jnp.where(first, both[tokens:], both[:tokens])


def project(core, context, weight, tile=512):
    tokens, depth = context.shape
    features = weight.shape[1]
    half = jax.ShapeDtypeStruct((tokens // 2, features), F32)
    half_spec = pl.BlockSpec((tokens // 2, tile), lambda f, core: (0, f))
    return pl.pallas_call(
        project_kernel,
        grid_spec=pltpu.PrefetchScalarGridSpec(
            num_scalar_prefetch=1,
            grid=(features // tile,),
            in_specs=[
                pl.BlockSpec((tokens, depth), lambda f, core: (0, 0)),
                pl.BlockSpec((depth, tile), lambda f, core: (0, f)),
            ],
            out_specs=[half_spec, half_spec],
        ),
        out_shape=[half, half],
        compiler_params=pltpu.CompilerParams(vmem_limit_bytes=LIMIT),
        cost_estimate=pl.CostEstimate(
            flops=2 * tokens * depth * features, bytes_accessed=2 * depth * features, transcendentals=0
        ),
        name="project",
    )(core[None], context, weight)


def whole(kernel, out_shape, flops, *args):
    return pl.pallas_call(
        kernel,
        in_specs=[VMEM] * len(args),
        out_specs=jax.tree.map(lambda _: VMEM, out_shape),
        out_shape=out_shape,
        compiler_params=pltpu.CompilerParams(vmem_limit_bytes=16 << 20),
        cost_estimate=pl.CostEstimate(
            flops=flops, bytes_accessed=sum(a.size * a.dtype.itemsize for a in args), transcendentals=0
        ),
    )(*args)


def body(context, out_weight, residual_in, norm_gain, expert_ids, gate_weights, keep_mask, expert_in, expert_out):
    tokens, features = residual_in.shape[1:]
    experts = lax.axis_size("ep")
    own, other = project(
        lax.axis_index("tp"), context[0], pltpu.with_memory_space_constraint(out_weight, pltpu.HBM)
    )
    recv = lax.ppermute(other, "tp", SWAP)
    packed_shapes = [
        jax.ShapeDtypeStruct((experts * PACK, features * slots // PACK), BF16) for slots in CHUNKS
    ]
    flops = sum(2 * tokens * experts * PACK * features for _ in CHUNKS)
    stream, *outgoing = whole(
        functools.partial(pack_kernel, experts),
        [jax.ShapeDtypeStruct((tokens, features), BF16), *packed_shapes],
        flops,
        own, recv, residual_in[0], norm_gain[None, :], expert_ids[0].T, keep_mask[0].T,
    )

    def exchange(packed):
        blocks = packed.reshape(experts, PACK, packed.shape[1])
        return lax.all_to_all(blocks, "ep", split_axis=0, concat_axis=0, tiled=True).reshape(packed.shape)

    weights = [pltpu.with_memory_space_constraint(w[0], pltpu.HBM) for w in (expert_in, expert_out)]
    arrived = []
    for packed in outgoing:
        arrived.append(exchange(packed))
    returned = []
    for slots, rows in zip(CHUNKS, arrived):
        rows_other = lax.ppermute(rows, "tp", SWAP)
        part_own, part_other = ffn(slots, rows, rows_other, *weights)
        part_recv = lax.ppermute(part_other, "tp", SWAP)
        returned.append(exchange((part_own.astype(F32) + part_recv.astype(F32)).astype(BF16)))
    return whole(
        functools.partial(combine_kernel, experts),
        jax.ShapeDtypeStruct((tokens, features), BF16),
        2 * flops,
        *returned, stream, expert_ids[0], keep_mask[0], gate_weights[0],
    )[None]


def solution(mesh):
    return jax.shard_map(
        body,
        mesh=mesh,
        in_specs=(
            P("ep", None, "tp"),
            P("tp", None),
            P("ep", "tp", None),
            P(),
            P("ep", "tp", None),
            P("ep", "tp", None),
            P("ep", "tp", None),
            P("ep", None, "tp"),
            P("ep", "tp", None),
        ),
        out_specs=P("ep", "tp", None),
        check_vma=False,
    )
```

time: 291 us -> 128 us (0.44)
  the two profiles are of different devices: /device:TPU:19 before, /device:TPU:0 now
where the time goes in v2:
time: 128 us
  blocking collectives  49.1 us (38%)
  waiting for transfers between devices  33.6 us (26%)
  Pallas kernels  29.9 us (23%)
  starting transfers between devices  10.1 us (8%)
  other arithmetic  3.56 us (3%)
  local copies, waits for them, and re-layouts  1.57 us (1%)
    all_to_all x2, blocking collectives, exchange(): lax.all_to_all(blocks, 'ep', split_axis=0, concat_axis=0, tiled=True)  49.1 us
    all_to_all x2, waiting for transfers between devices, exchange(): lax.all_to_all(blocks, 'ep', split_axis=0, concat_axis=0, tiled=True)  29.2 us
    pallas_call x2, Pallas kernels, ffn(): pl.pallas_call(functools.partial(ffn_kernel, slots, tile), in_specs=[VMEM...  21 us
    all_to_all x2, starting transfers between devices, exchange(): lax.all_to_all(blocks, 'ep', split_axis=0, concat_axis=0, tiled=True)  9.44 us
    pallas_call x1, Pallas kernels, project(): pl.pallas_call(project_kernel, grid_spec=pltpu.PrefetchScalarGridSpec(num...  4.91 us
    pallas_call x2, Pallas kernels, whole(): pl.pallas_call(kernel, in_specs=[VMEM] * len(args), out_specs=jax.tree.ma...  3.91 us
    reshape x2, other arithmetic, exchange(): blocks = packed.reshape(experts, PACK, packed.shape[1])  3.56 us
  transfers between devices with their start and end apart: 7, of which 4 were waited for; matrix products, arithmetic and copies ran while one was open for 3% of the time, Pallas kernels for 16%

profile of v2, /device:TPU:0, one launch (start us, length us, event | category | flops | bytes accessed | tf_op | source)
XLA Modules:
  0.0 127.9 jit_solution(10123486364967868247)
XLA Ops:
  0.0 0.0 copy-start.3
  0.0 0.0 copy-start.4
  0.0 0.0 copy-start.2
  0.0 0.0 copy-start
  0.0 1.1 copy-done
  1.1 0.0 copy-start.1
  1.1 4.9 %project.1 = (f32[128,2048]{1,0:T(8,128)S(1)}, f32[128,2048]{1,0:T(8,128)}) custom-call(s32[1]{0:T(128)} %bitcast.core_ref, bf16[256,1024]{1,0:T(8,128)(2,1)S(1)} %bitcast.30, bf16[1024,2048]{1,0:T(8,128)(2,1)} %weight_ref.1), custom_call_target="tpu_custom_call" | custom-call | flops 1073741824 | bytes 4194304 | tf_op jit(solution)/shard_map/project/pallas_call | solution.py:193
  6.0 0.0 collective-permute-start
  6.0 0.0 copy-done.3
  6.0 0.1 copy.10
  6.1 0.1 copy.12.ids_ref
  6.2 0.0 copy-done.4
  6.2 0.1 copy.11
  6.3 0.1 copy.13.keep_ref
  6.4 2.5 %collective-permute-done.recv_ref = f32[128,2048]{1,0:T(8,128)S(1)} collective-permute-done((f32[128,2048]{1,0:T(8,128)}, f32[128,2048]{1,0:T(8,128)S(1)}, u32[]{:S(2)}, u32[]{:S(2)}) %collective-permute-start) | collective-permute-done | bytes 1048608 | tf_op jit(solution)/shard_map/ppermute | solution.py:232
  8.9 0.0 copy-done.2
  8.9 0.0 copy-done.1
  8.9 1.2 shard_map.91
  10.1 30.5 %all_to_all.20 = bf16[64,8,1024]{2,1,0:T(8,128)(2,1)S(1)} all-to-all(bf16[64,8,1024]{2,1,0:T(8,128)(2,1)S(1)} %bitcast.29), channel_id=1, replica_groups=mesh['tp'=2,'ep'=64] {'ep'}, dimensions={0} | all-to-all | bytes 2097152 | tf_op jit(solution)/shard_map/all_to_all | solution.py:246
  40.6 0.0 collective-permute-start.1
  40.7 18.6 %all_to_all.21 = bf16[64,8,512]{2,1,0:T(8,128)(2,1)S(1)} all-to-all(bf16[64,8,512]{2,1,0:T(8,128)(2,1)S(1)} %bitcast.32), channel_id=1, replica_groups=mesh['tp'=2,'ep'=64] {'ep'}, dimensions={0} | all-to-all | bytes 1048576 | tf_op jit(solution)/shard_map/all_to_all | solution.py:246
  59.2 0.0 collective-permute-start.3
  59.2 0.0 collective-permute-done.1.other_ref
  59.2 13.0 %shard_map.92 = (bf16[512,1024]{1,0:T(8,128)(2,1)S(1)}, bf16[512,1024]{1,0:T(8,128)(2,1)S(1)}) custom-call(bf16[512,1024]{1,0:T(8,128)(2,1)S(1)} %bitcast.27, bf16[512,1024]{1,0:T(8,128)(2,1)S(1)} %collective-permute-done.1.other_ref, bf16[2048,2048]{1,0:T(8,128)(2,1)} %bitcast.40, bf16[2048,2048]{1,0:T(8,128)(2,1)} %bitcast.42), custom_call_target="tpu_custom_call" | custom-call | flops 8589934592 | bytes 16777216 | tf_op jit(solution)/shard_map/pallas_call | solution.py:161
  72.2 0.6 collective-permute-start.2
  72.8 0.0 collective-permute-done.3.other_ref
  72.8 8.1 %shard_map.93 = (bf16[512,512]{1,0:T(8,128)(2,1)S(1)}, bf16[512,512]{1,0:T(8,128)(2,1)S(1)}) custom-call(bf16[512,512]{1,0:T(8,128)(2,1)S(1)} %bitcast.25, bf16[512,512]{1,0:T(8,128)(2,1)S(1)} %collective-permute-done.3.other_ref, bf16[2048,2048]{1,0:T(8,128)(2,1)} %bitcast.41, bf16[2048,2048]{1,0:T(8,128)(2,1)} %bitcast.43), custom_call_target="tpu_custom_call" | custom-call | flops 4294967296 | bytes 16777216 | tf_op jit(solution)/shard_map/pallas_call | solution.py:161
  80.9 0.0 copy-start.5
  80.9 0.1 collective-permute-start.4
  81.0 1.9 %collective-permute-done.4 = bf16[512,512]{1,0:T(8,128)(2,1)S(1)} collective-permute-done((bf16[512,512]{1,0:T(8,128)(2,1)S(1)}, bf16[512,512]{1,0:T(8,128)(2,1)S(1)}, u32[]{:S(2)}, u32[]{:S(2)}) %collective-permute-start.4) | collective-permute-done | bytes 524320 | tf_op jit(solution)/shard_map/ppermute | solution.py:256
  82.9 0.9 fusion.1
  83.8 4.7 %all-to-all-start.3 = ((bf16[64,8,512]{2,1,0:T(8,128)(2,1)}), bf16[64,8,512]{2,1,0:T(8,128)(2,1)S(1)}, u32[]{:S(2)}, u32[]{:S(2)}) async-start(bf16[64,8,512]{2,1,0:T(8,128)(2,1)} %fusion.1), calls=%async_computation.3 | async-start | bytes 1048576 | tf_op jit(solution)/shard_map/all_to_all | solution.py:246
  88.5 0.0 collective-permute-done.2
  88.5 2.6 %fusion = bf16[64,8,1024]{2,1,0:T(8,128)(2,1)} fusion(bf16[512,1024]{1,0:T(8,128)(2,1)} %collective-permute-done.2, bf16[512,1024]{1,0:T(8,128)(2,1)S(1)} %get-tuple-element.17), kind=kLoop, calls=%fused_computation.1 | loop fusion | flops 2097152 | bytes 3145728 | tf_op jit(solution)/shard_map/reshape | solution.py:245
  91.2 11.2 %all-to-all-done.3 = bf16[64,8,512]{2,1,0:T(8,128)(2,1)S(1)} async-done(((bf16[64,8,512]{2,1,0:T(8,128)(2,1)}), bf16[64,8,512]{2,1,0:T(8,128)(2,1)S(1)}, u32[]{:S(2)}, u32[]{:S(2)}) %all-to-all-start.3) | async-done | bytes 524320 | tf_op jit(solution)/shard_map/all_to_all | solution.py:246
  102.4 4.7 %all-to-all-start.1 = ((bf16[64,8,1024]{2,1,0:T(8,128)(2,1)}), bf16[64,8,1024]{2,1,0:T(8,128)(2,1)S(1)}, u32[]{:S(2)}, u32[]{:S(2)}) async-start(bf16[64,8,1024]{2,1,0:T(8,128)(2,1)} %fusion), calls=%async_computation.1 | async-start | bytes 2097152 | tf_op jit(solution)/shard_map/all_to_all | solution.py:246
  107.1 0.0 copy-done.5
  107.1 0.1 copy.14
  107.3 18.0 %all-to-all-done.1 = bf16[64,8,1024]{2,1,0:T(8,128)(2,1)S(1)} async-done(((bf16[64,8,1024]{2,1,0:T(8,128)(2,1)}), bf16[64,8,1024]{2,1,0:T(8,128)(2,1)S(1)}, u32[]{:S(2)}, u32[]{:S(2)}) %all-to-all-start.1) | async-done | bytes 1048608 | tf_op jit(solution)/shard_map/all_to_all | solution.py:246
  125.2 2.7 %shard_map.94 = bf16[128,2048]{1,0:T(8,128)(2,1)} custom-call(bf16[512,1024]{1,0:T(8,128)(2,1)S(1)} %bitcast.28, bf16[512,512]{1,0:T(8,128)(2,1)S(1)} %bitcast.31, bf16[128,2048]{1,0:T(8,128)(2,1)S(1)} %get-tuple-element.22.refs_2_, s32[128,2]{1,0:T(8,128)S(1)} %bitcast.35, s32[128,2]{1,0:T(8,128)S(1)} %bitcast.37, f32[128,2]{1,0:T(8,128)S(1)} %bitcast.38), custom_call_target="tpu_custom_call" | custom-call | flops 1073741824 | bytes 2100224 | tf_op jit(solution)/shard_map/pallas_call | solution.py:214
Async XLA Ops:
  0.0 6.0 %copy-start.3 = (s32[1,128,2]{1,2,0:T(2,128)S(1)}, s32[1,128,2]{1,2,0:T(2,128)}, u32[]{:S(2)}) copy-start(s32[1,128,2]{1,2,0:T(2,128)} %param.13) | copy-start | bytes 3076
  0.0 6.2 %copy-start.4 = (s32[1,128,2]{1,2,0:T(2,128)S(1)}, s32[1,128,2]{1,2,0:T(2,128)}, u32[]{:S(2)}) copy-start(s32[1,128,2]{1,2,0:T(2,128)} %param.15) | copy-start | bytes 3076
  0.0 8.9 %copy-start.2 = (f32[2048]{0:T(1024)S(1)}, f32[2048]{0:T(1024)}, u32[]{:S(2)}) copy-start(f32[2048]{0:T(1024)} %param.12) | copy-start | bytes 24580
  0.0 1.1 copy-start
  1.1 7.8 %copy-start.1 = (bf16[1,128,2048]{2,1,0:T(8,128)(2,1)S(1)}, bf16[1,128,2048]{2,1,0:T(8,128)(2,1)}, u32[]{:S(2)}) copy-start(bf16[1,128,2048]{2,1,0:T(8,128)(2,1)} %param.11) | copy-start | bytes 1572868
  6.0 2.9 %collective-permute-start = (f32[128,2048]{1,0:T(8,128)}, f32[128,2048]{1,0:T(8,128)S(1)}, u32[]{:S(2)}, u32[]{:S(2)}) collective-permute-start(f32[128,2048]{1,0:T(8,128)} %get-tuple-element.15), channel_id=1, source_target_pairs={{0,64},{64,0},{1,65},{65,1},{2,66},{66,2},{3,67},{67,3},{4,68},{68... | collective-permute-start | bytes 3145736 | tf_op jit(solution)/shard_map/ppermute | solution.py:232
  40.6 18.6 %collective-permute-start.1 = (bf16[512,1024]{1,0:T(8,128)(2,1)S(1)}, bf16[512,1024]{1,0:T(8,128)(2,1)S(1)}, u32[]{:S(2)}, u32[]{:S(2)}) collective-permute-start(bf16[512,1024]{1,0:T(8,128)(2,1)S(1)} %bitcast.26), channel_id=1, source_target_pairs={{0,64},{64,0},{1,65},{65,1},{2,66},{66,2},{3,67},{67,3},{4,68},{68... | collective-permute-start | bytes 3145736 | tf_op jit(solution)/shard_map/ppermute | solution.py:254
  59.2 13.6 %collective-permute-start.3 = (bf16[512,512]{1,0:T(8,128)(2,1)S(1)}, bf16[512,512]{1,0:T(8,128)(2,1)S(1)}, u32[]{:S(2)}, u32[]{:S(2)}) collective-permute-start(bf16[512,512]{1,0:T(8,128)(2,1)S(1)} %bitcast.24), channel_id=1, source_target_pairs={{0,64},{64,0},{1,65},{65,1},{2,66},{66,2},{3,67},{67,3},{4,68},{68... | collective-permute-start | bytes 1572872 | tf_op jit(solution)/shard_map/ppermute | solution.py:254
  72.2 16.3 %collective-permute-start.2 = (bf16[512,1024]{1,0:T(8,128)(2,1)S(1)}, bf16[512,1024]{1,0:T(8,128)(2,1)}, u32[]{:S(2)}, u32[]{:S(2)}) collective-permute-start(bf16[512,1024]{1,0:T(8,128)(2,1)S(1)} %get-tuple-element.18), channel_id=1, source_target_pairs={{0,64},{64,0},{1,65},{65,1},{2,66},{66,2},{3,67},{67,3},{4,68},{68... | collective-permute-start | bytes 3145736 | tf_op jit(solution)/shard_map/ppermute | solution.py:256
  80.9 26.3 %copy-start.5 = (f32[1,128,2]{1,2,0:T(2,128)S(1)}, f32[1,128,2]{1,2,0:T(2,128)}, u32[]{:S(2)}) copy-start(f32[1,128,2]{1,2,0:T(2,128)} %param.14) | copy-start | bytes 3076
  80.9 2.0 %collective-permute-start.4 = (bf16[512,512]{1,0:T(8,128)(2,1)S(1)}, bf16[512,512]{1,0:T(8,128)(2,1)S(1)}, u32[]{:S(2)}, u32[]{:S(2)}) collective-permute-start(bf16[512,512]{1,0:T(8,128)(2,1)S(1)} %get-tuple-element.21), channel_id=1, source_target_pairs={{0,64},{64,0},{1,65},{65,1},{2,66},{66,2},{3,67},{67,3},{4,68},{68... | collective-permute-start | bytes 1572872 | tf_op jit(solution)/shard_map/ppermute | solution.py:256
  83.8 18.6 %all-to-all-start.3 = ((bf16[64,8,512]{2,1,0:T(8,128)(2,1)}), bf16[64,8,512]{2,1,0:T(8,128)(2,1)S(1)}, u32[]{:S(2)}, u32[]{:S(2)}) async-start(bf16[64,8,512]{2,1,0:T(8,128)(2,1)} %fusion.1), calls=%async_computation.3 | async-start | bytes 1048576 | tf_op jit(solution)/shard_map/all_to_all | solution.py:246
  102.4 22.8 %all-to-all-start.1 = ((bf16[64,8,1024]{2,1,0:T(8,128)(2,1)}), bf16[64,8,1024]{2,1,0:T(8,128)(2,1)S(1)}, u32[]{:S(2)}, u32[]{:S(2)}) async-start(bf16[64,8,1024]{2,1,0:T(8,128)(2,1)} %fusion), calls=%async_computation.1 | async-start | bytes 2097152 | tf_op jit(solution)/shard_map/all_to_all | solution.py:246

commit v3 on v1

v3 whole, which is shorter than its diff:
```python
import functools

import jax
import jax.numpy as jnp
from jax import lax
from jax.experimental import pallas as pl
from jax.experimental.pallas import tpu as pltpu
from jax.sharding import PartitionSpec as P


SLOT = 6
PACK = 8
TAIL = 3
SOURCES = 32
TILE = 512
LIMIT = 32 << 20
F32, BF16 = jnp.float32, jnp.bfloat16
VMEM = pl.BlockSpec(memory_space=pltpu.VMEM)
SMEM = pl.BlockSpec(memory_space=pltpu.SMEM)
HBM = pl.BlockSpec(memory_space=pltpu.HBM)
SWAP = [(0, 1), (1, 0)]


def dot(a, b):
    return jnp.dot(a, b, preferred_element_type=F32)


def iota(shape, dim):
    return lax.broadcasted_iota(jnp.int32, shape, dim)


def ones_where(condition):
    return jnp.where(condition, 1.0, 0.0).astype(BF16)


def parts_of(width):
    return [slice(j * (width // TAIL), (j + 1) * (width // TAIL)) for j in range(TAIL)]


def places(ids, keep, experts, along):
    tokens = ids[0].shape[along]
    shape = (experts, tokens) if along == 1 else (tokens, experts)
    member = iota(shape, 1 - along)
    hot = [jnp.where((member == ids[k]) & (keep[k] > 0), 1.0, 0.0) for k in (0, 1)]
    older = ones_where(iota((tokens, tokens), 1 - along) < iota((tokens, tokens), along))
    out = []
    base = 0.0
    for k in (0, 1):
        sent = hot[k].astype(BF16)
        before = (dot(sent, older) if along == 1 else dot(older, sent)) + base
        rank = jnp.sum(hot[k] * before, axis=1 - along, keepdims=True).astype(jnp.int32)
        base = base + jnp.sum(hot[k], axis=along, keepdims=True)
        late = jnp.where(rank >= TAIL, 1, 0)
        kept = keep[k] > 0
        tail = ids[k] * PACK + SLOT + late
        out.append(
            (
                jnp.where(kept, ids[k] * PACK + rank, -1),
                [jnp.where(kept & (rank - TAIL * late == j), tail, -1) for j in range(TAIL)],
            )
        )
    return out


def pack_kernel(experts, own_ref, recv_ref, res_ref, gain_ref, ids_ref, keep_ref, stream_ref, packed_ref):
    attended = own_ref[...] + recv_ref[...].astype(F32)
    stream = (res_ref[...].astype(F32) + attended).astype(BF16)
    stream_ref[...] = stream
    value = stream.astype(F32)
    tokens, features = value.shape
    centred = value - jnp.sum(value, axis=1, keepdims=True) / features
    variance = jnp.sum(centred * centred, axis=1, keepdims=True) / features
    normed = (centred / jnp.sqrt(variance + 1e-05) * gain_ref[...]).astype(BF16)
    ids = [ids_ref[k : k + 1, :] for k in (0, 1)]
    keep = [keep_ref[k : k + 1, :] for k in (0, 1)]
    first, second = places(ids, keep, experts, 1)
    rows = iota((experts * PACK, tokens), 0)
    main = ones_where((rows == first[0]) | (rows == second[0]))
    wide = packed_ref.shape[1]
    for j, part in enumerate(parts_of(wide)):
        tail = ones_where((rows == first[1][j]) | (rows == second[1][j]))
        packed_ref[:, part] = dot(
            jnp.concatenate([main, tail], axis=1), jnp.concatenate([normed[:, part], normed[:, wide:]], axis=0)
        ).astype(BF16)


def combine_kernel(experts, packed_ref, stream_ref, ids_ref, keep_ref, gate_ref, out_ref):
    ids = [ids_ref[:, k : k + 1] for k in (0, 1)]
    keep = [keep_ref[:, k : k + 1] for k in (0, 1)]
    first, second = places(ids, keep, experts, 0)
    tokens = ids[0].shape[0]
    columns = iota((2 * tokens, experts * PACK), 1)
    gate = [gate_ref[:, k : k + 1] for k in (0, 1)]
    wide = packed_ref.shape[1]
    parts = parts_of(wide)

    def finish(at, rows):
        mixed = gate[0] * rows[:tokens] + gate[1] * rows[tokens:]
        out_ref[:, at] = (stream_ref[:, at].astype(F32) + mixed).astype(BF16)

    main = ones_where(columns == jnp.concatenate([first[0], second[0]], axis=0))
    for part in parts:
        finish(part, dot(main, packed_ref[:, part]))
    tails = [ones_where(columns == jnp.concatenate([first[1][j], second[1][j]], axis=0)) for j in range(TAIL)]
    finish(
        slice(wide, None),
        dot(jnp.concatenate(tails, axis=1), jnp.concatenate([packed_ref[:, part] for part in parts], axis=0)),
    )


def movers(reverse):
    tall, short = SOURCES * PACK, SOURCES * SLOT
    shape = (tall, short) if reverse else (short, tall)
    row, col = iota(shape, 1 if reverse else 0), iota(shape, 0 if reverse else 1)
    at = col & (PACK - 1)
    slot = row - SLOT * (col >> 3)
    main = ones_where((at < SLOT) & (slot == at))
    return main, [ones_where((at >= SLOT) & (slot == (at - SLOT) * TAIL + j)) for j in range(TAIL)]


def unpack_into(packed_ref, rows_ref):
    tall, short = SOURCES * PACK, SOURCES * SLOT
    wide = packed_ref.shape[1]
    main, tails = movers(False)
    tails = jnp.concatenate(tails, axis=1)
    for g in range(packed_ref.shape[0] // tall):
        block = packed_ref[g * tall : (g + 1) * tall, :]
        at = slice(g * short, (g + 1) * short)
        rows_ref[at, :wide] = dot(main, block).astype(BF16)
        stacked = jnp.concatenate([block[:, part] for part in parts_of(wide)], axis=0)
        rows_ref[at, wide:] = dot(tails, stacked).astype(BF16)


def tile_copy(hbm_ref, vmem_ref, sems, i):
    at = pl.ds(pl.multiple_of(i * TILE, TILE), TILE)
    return pltpu.make_async_copy(hbm_ref.at[:, at], vmem_ref.at[:, at], sems.at[i])


def start_copies(hbm_ref, vmem_ref, sems):
    for i in range(hbm_ref.shape[1] // TILE):
        tile_copy(hbm_ref, vmem_ref, sems, i).start()


def tiled(hbm_ref, vmem_ref, sems, step):
    @pl.loop(0, hbm_ref.shape[1] // TILE)
    def _(i):
        tile_copy(hbm_ref, vmem_ref, sems, i).wait()
        step(pl.ds(pl.multiple_of(i * TILE, TILE), TILE))


def hidden_kernel(packed_ref, in_hbm, hidden_ref, in_ref, rows_ref, sems):
    start_copies(in_hbm, in_ref, sems)
    unpack_into(packed_ref, rows_ref)

    def step(at):
        hidden_ref[:, at] = jnp.maximum(dot(rows_ref[...], in_ref[:, at]), 0.0).astype(BF16)

    tiled(in_hbm, in_ref, sems, step)


def result_kernel(hidden_ref, out_hbm, result_ref, out_ref, sems):
    start_copies(out_hbm, out_ref, sems)

    def step(at):
        result_ref[:, at] = dot(hidden_ref[...], out_ref[:, at]).astype(result_ref.dtype)

    tiled(out_hbm, out_ref, sems, step)


def both_kernel(packed_ref, in_hbm, out_hbm, result_ref, in_ref, rows_ref, hidden_ref, out_ref, in_sems, out_sems):
    start_copies(in_hbm, in_ref, in_sems)
    start_copies(out_hbm, out_ref, out_sems)
    unpack_into(packed_ref, rows_ref)

    def step_in(at):
        hidden_ref[:, at] = jnp.maximum(dot(rows_ref[...], in_ref[:, at]), 0.0).astype(BF16)

    def step_out(at):
        result_ref[:, at] = dot(hidden_ref[...], out_ref[:, at]).astype(result_ref.dtype)

    tiled(in_hbm, in_ref, in_sems, step_in)
    tiled(out_hbm, out_ref, out_sems, step_out)


def add_kernel(own_ref, recv_ref, packed_ref):
    tall, short = SOURCES * PACK, SOURCES * SLOT
    wide = packed_ref.shape[1]
    main, tails = movers(True)
    for g in range(packed_ref.shape[0] // tall):
        at = slice(g * short, (g + 1) * short)
        block = (own_ref[at, :] + recv_ref[at, :].astype(F32)).astype(BF16)
        for j, part in enumerate(parts_of(wide)):
            packed_ref[g * tall : (g + 1) * tall, part] = dot(
                jnp.concatenate([main, tails[j]], axis=1),
                jnp.concatenate([block[:, part], block[:, wide:]], axis=0),
            ).astype(BF16)


def project_kernel(core_ref, context_hbm, weight_hbm, own_ref, other_ref, context_ref, weight_ref, sem, sems):
    load = pltpu.make_async_copy(context_hbm, context_ref, sem)
    load.start()
    start_copies(weight_hbm, weight_ref, sems)
    load.wait()
    tokens = own_ref.shape[0]
    first = core_ref[0] == 0

    def step(at):
        both = dot(context_ref[...], weight_ref[:, at])
        own_ref[:, at] = jnp.where(first, both[:tokens], both[tokens:])
        other_ref[:, at] = jnp.where(first, both[tokens:], both[:tokens]).astype(BF16)

    tiled(weight_hbm, weight_ref, sems, step)


def call(kernel, flops, out_shape, args, specs=None, scratch=(), limit=LIMIT):
    return pl.pallas_call(
        kernel,
        in_specs=specs or [VMEM] * len(args),
        out_specs=jax.tree.map(lambda _: VMEM, out_shape),
        out_shape=out_shape,
        scratch_shapes=scratch,
        compiler_params=pltpu.CompilerParams(vmem_limit_bytes=limit),
        cost_estimate=pl.CostEstimate(
            flops=flops, bytes_accessed=sum(a.size * a.dtype.itemsize for a in args), transcendentals=0
        ),
    )(*args)


def shape(*dims, dtype=BF16):
    return jax.ShapeDtypeStruct(dims, dtype)


def sems(weight):
    return pltpu.SemaphoreType.DMA((weight.shape[1] // TILE,))


def vmem(a):
    return pltpu.VMEM(a.shape, a.dtype)


def body(context, out_weight, residual_in, norm_gain, expert_ids, gate_weights, keep_mask, expert_in, expert_out):
    tokens, features = residual_in.shape[1:]
    experts = lax.axis_size("ep")
    units = expert_in.shape[2]

    def in_hbm(a):
        return pltpu.with_memory_space_constraint(a, pltpu.HBM)

    context, out_weight = in_hbm(context[0]), in_hbm(out_weight)
    weight_in, weight_out = in_hbm(expert_in[0]), in_hbm(expert_out[0])
    own, other = call(
        project_kernel,
        2 * context.size * features,
        [shape(tokens, features, dtype=F32), shape(tokens, features)],
        (lax.axis_index("tp")[None], context, out_weight),
        specs=[SMEM, HBM, HBM],
        scratch=[vmem(context), vmem(out_weight), pltpu.SemaphoreType.DMA(()), sems(out_weight)],
    )
    recv = lax.ppermute(other, "tp", SWAP)
    packed_shape = shape(experts * PACK, features * SLOT // PACK)
    rows_shape = shape(experts * SLOT, features)
    moving = 4 * tokens * experts * PACK * features
    stream, outgoing = call(
        functools.partial(pack_kernel, experts),
        moving,
        [shape(tokens, features), packed_shape],
        (own, recv, residual_in[0], norm_gain[None, :], expert_ids[0].T, keep_mask[0].T),
    )

    def exchange(packed):
        blocks = packed.reshape(experts, PACK, packed.shape[1])
        return lax.all_to_all(blocks, "ep", split_axis=0, concat_axis=0, tiled=True).reshape(packed.shape)

    rows = exchange(outgoing)
    rows_other = lax.ppermute(rows, "tp", SWAP)
    half = 2 * experts * SLOT * features * units
    row_buffer, hidden_shape = vmem(rows_shape), shape(experts * SLOT, units)
    hidden = call(
        hidden_kernel, half, hidden_shape, (rows, weight_in), specs=[VMEM, HBM],
        scratch=[vmem(weight_in), row_buffer, sems(weight_in)],
    )
    part_other = call(
        both_kernel, 2 * half, rows_shape, (rows_other, weight_in, weight_out), specs=[VMEM, HBM, HBM],
        scratch=[vmem(weight_in), row_buffer, vmem(hidden_shape), vmem(weight_out), sems(weight_in), sems(weight_out)],
    )
    part_recv = lax.ppermute(part_other, "tp", SWAP)
    part_own = call(
        result_kernel, half, shape(*rows_shape.shape, dtype=F32), (hidden, weight_out),
        specs=[VMEM, HBM], scratch=[vmem(weight_out), sems(weight_out)],
    )
    results = call(add_kernel, moving, packed_shape, (part_own, part_recv))
    returned = exchange(results)
    return call(
        functools.partial(combine_kernel, experts),
        2 * moving,
        shape(tokens, features),
        (returned, stream, expert_ids[0], keep_mask[0], gate_weights[0]),
    )[None]


def solution(mesh):
    return jax.shard_map(
        body,
        mesh=mesh,
        in_specs=(
            P("ep", None, "tp"),
            P("tp", None),
            P("ep", "tp", None),
            P(),
            P("ep", "tp", None),
            P("ep", "tp", None),
            P("ep", "tp", None),
            P("ep", None, "tp"),
            P("ep", "tp", None),
        ),
        out_specs=P("ep", "tp", None),
        check_vma=False,
    )
```

time: 112 us -> 105 us (0.938)
  matrix products: 6.81 us -> 0 us
  local copies, waits for them, and re-layouts: 3.14 us -> 0.49 us
  waiting for transfers between devices: 28.3 us -> 29.8 us
    dot_general x2 -> x0, matrix products: 6.81 us -> none  [dot(): return jnp.dot(a, b, preferred_element_type=F32)]
    unnamed x17 -> x13, local copies, waits for them, and re-layouts: 3.02 us -> 0.37 us
    ppermute x1, waiting for transfers between devices: 0.01 us -> 1.52 us  [body(): recv = lax.ppermute(other, 'tp', SWAP)]
    pallas_call x5 -> x7, Pallas kernels: 31.6 us -> 32.4 us  [call(): pl.pallas_call(kernel, in_specs=specs or [VMEM] * len(args), out_specs=ja...]
  transfers between devices with their start and end apart: 4 -> 4, of which waited for: 2 -> 3; matrix products, arithmetic and copies ran while one was open for 3% -> 0% of each run, Pallas kernels for 11% -> 11%
where the time goes in v3:
time: 105 us
  blocking collectives  36.1 us (34%)
  Pallas kernels  32.4 us (31%)
  waiting for transfers between devices  29.8 us (28%)
  starting transfers between devices  5.73 us (5%)
    all_to_all x1, blocking collectives, exchange(): lax.all_to_all(blocks, 'ep', split_axis=0, concat_axis=0, tiled=True)  36.1 us
    pallas_call x7, Pallas kernels, call(): pl.pallas_call(kernel, in_specs=specs or [VMEM] * len(args), out_specs=ja...  32.4 us
    all_to_all x1, waiting for transfers between devices, exchange(): lax.all_to_all(blocks, 'ep', split_axis=0, concat_axis=0, tiled=True)  24.8 us
    all_to_all x1, starting transfers between devices, exchange(): lax.all_to_all(blocks, 'ep', split_axis=0, concat_axis=0, tiled=True)  5.42 us
    ppermute x1, waiting for transfers between devices, body(): rows_other = lax.ppermute(rows, 'tp', SWAP)  3.41 us
  transfers between devices with their start and end apart: 4, of which 3 were waited for; matrix products, arithmetic and copies ran while one was open for 0% of the time, Pallas kernels for 11%

profile of v3, /device:TPU:0, one launch (start us, length us, event | category | flops | bytes accessed | tf_op | source)
XLA Modules:
  0.0 104.6 jit_solution(13673444508631032271)
XLA Ops:
  0.0 0.0 copy-start.2
  0.0 0.0 copy-start.3
  0.0 0.0 copy-start
  0.0 0.0 copy-start.1
  0.0 3.9 %shard_map.91 = (f32[128,2048]{1,0:T(8,128)S(1)}, bf16[128,2048]{1,0:T(8,128)(2,1)S(1)}) custom-call(s32[1]{0:T(128)} %bitcast.core_ref, bf16[256,1024]{1,0:T(8,128)(2,1)} %bitcast.31, bf16[1024,2048]{1,0:T(8,128)(2,1)} %weight_hbm.1), custom_call_target="tpu_custom_call" | custom-call | flops 1073741824 | bytes 4718596 | tf_op jit(solution)/shard_map/pallas_call | solution.py:216
  3.9 0.1 collective-permute-start
  4.0 0.0 copy-done.2
  4.0 0.1 copy.10
  4.1 0.1 copy.12.ids_ref
  4.2 0.0 copy-done.3
  4.2 0.1 copy.11
  4.3 0.1 copy.13.keep_ref
  4.4 1.5 %collective-permute-done.recv_ref = bf16[128,2048]{1,0:T(8,128)(2,1)S(1)} collective-permute-done((bf16[128,2048]{1,0:T(8,128)(2,1)S(1)}, bf16[128,2048]{1,0:T(8,128)(2,1)S(1)}, u32[]{:S(2)}, u32[]{:S(2)}) %collective-permute-start) | collective-permute-done | bytes 524320 | tf_op jit(solution)/shard_map/ppermute | solution.py:259
  5.9 0.0 copy-done
  5.9 0.0 copy-done.1
  5.9 1.1 %shard_map.92 = (bf16[128,2048]{1,0:T(8,128)(2,1)S(1)}, bf16[512,1536]{1,0:T(8,128)(2,1)S(1)}) custom-call(f32[128,2048]{1,0:T(8,128)S(1)} %get-tuple-element.9.own_ref, bf16[128,2048]{1,0:T(8,128)(2,1)S(1)} %collective-permute-done.recv_ref, bf16[128,2048]{1,0:T(8,128)(2,1)S(1)} %bitcast.22, f32[1,2048]{1,0:T(1,128)S(1)} %bitcast.28, ...), custom_call_target="tpu_custom_call" | custom-call | flops 536870912 | bytes 2107392 | tf_op jit(solution)/shard_map/pallas_call | solution.py:216
  7.0 36.1 %all_to_all.10 = bf16[64,8,1536]{2,1,0:T(8,128)(2,1)S(1)} all-to-all(bf16[64,8,1536]{2,1,0:T(8,128)(2,1)S(1)} %bitcast.21), channel_id=1, replica_groups=mesh['tp'=2,'ep'=64] {'ep'}, dimensions={0} | all-to-all | bytes 3145728 | tf_op jit(solution)/shard_map/all_to_all | solution.py:272
  43.1 0.0 collective-permute-start.1
  43.1 3.4 %collective-permute-done.1.packed_ref = bf16[512,1536]{1,0:T(8,128)(2,1)S(1)} collective-permute-done((bf16[512,1536]{1,0:T(8,128)(2,1)S(1)}, bf16[512,1536]{1,0:T(8,128)(2,1)S(1)}, u32[]{:S(2)}, u32[]{:S(2)}) %collective-permute-start.1) | collective-permute-done | bytes 1572896 | tf_op jit(solution)/shard_map/ppermute | solution.py:275
  46.5 11.0 %shard_map.95 = bf16[384,2048]{1,0:T(8,128)(2,1)S(1)} custom-call(bf16[512,1536]{1,0:T(8,128)(2,1)S(1)} %collective-permute-done.1.packed_ref, bf16[2048,2048]{1,0:T(8,128)(2,1)} %bitcast.32, bf16[2048,2048]{1,0:T(8,128)(2,1)} %bitcast.29), custom_call_target="tpu_custom_call" | custom-call | flops 6442450944 | bytes 18350080 | tf_op jit(solution)/shard_map/pallas_call | solution.py:216
  57.6 0.2 collective-permute-start.2
  57.8 6.2 %shard_map.93.hidden_ref = bf16[384,2048]{1,0:T(8,128)(2,1)S(1)} custom-call(bf16[512,1536]{1,0:T(8,128)(2,1)S(1)} %bitcast.19, bf16[2048,2048]{1,0:T(8,128)(2,1)} %bitcast.33), custom_call_target="tpu_custom_call" | custom-call | flops 3221225472 | bytes 9961472 | tf_op jit(solution)/shard_map/pallas_call | solution.py:216
  64.0 5.6 %shard_map.94.own_ref = f32[384,2048]{1,0:T(8,128)S(1)} custom-call(bf16[384,2048]{1,0:T(8,128)(2,1)S(1)} %shard_map.93.hidden_ref, bf16[2048,2048]{1,0:T(8,128)(2,1)} %bitcast.30), custom_call_target="tpu_custom_call" | custom-call | flops 3221225472 | bytes 9961472 | tf_op jit(solution)/shard_map/pallas_call | solution.py:216
  69.5 0.0 collective-permute-done.2.recv_ref
  69.6 2.3 %shard_map.96 = bf16[512,1536]{1,0:T(8,128)(2,1)} custom-call(f32[384,2048]{1,0:T(8,128)S(1)} %shard_map.94.own_ref, bf16[384,2048]{1,0:T(8,128)(2,1)S(1)} %collective-permute-done.2.recv_ref), custom_call_target="tpu_custom_call" | custom-call | flops 536870912 | bytes 4718592 | tf_op jit(solution)/shard_map/pallas_call | solution.py:216
  71.8 0.0 copy-start.4
  71.8 5.4 %all-to-all-start.1 = ((bf16[64,8,1536]{2,1,0:T(8,128)(2,1)}), bf16[64,8,1536]{2,1,0:T(8,128)(2,1)S(1)}, u32[]{:S(2)}, u32[]{:S(2)}) async-start(bf16[64,8,1536]{2,1,0:T(8,128)(2,1)} %bitcast.12), calls=%async_computation.1 | async-start | bytes 3145728 | tf_op jit(solution)/shard_map/all_to_all | solution.py:272
  77.3 0.0 copy-done.4
  77.3 0.1 copy.14
  77.4 24.8 %all-to-all-done.1 = bf16[64,8,1536]{2,1,0:T(8,128)(2,1)S(1)} async-done(((bf16[64,8,1536]{2,1,0:T(8,128)(2,1)}), bf16[64,8,1536]{2,1,0:T(8,128)(2,1)S(1)}, u32[]{:S(2)}, u32[]{:S(2)}) %all-to-all-start.1) | async-done | bytes 1572896 | tf_op jit(solution)/shard_map/all_to_all | solution.py:272
  102.2 2.3 %shard_map.97 = bf16[128,2048]{1,0:T(8,128)(2,1)} custom-call(bf16[512,1536]{1,0:T(8,128)(2,1)S(1)} %bitcast.20, bf16[128,2048]{1,0:T(8,128)(2,1)S(1)} %get-tuple-element.12.stream_ref, s32[128,2]{1,0:T(8,128)S(1)} %bitcast.24, s32[128,2]{1,0:T(8,128)S(1)} %bitcast.26, f32[128,2]{1,0:T(8,128)S(1)} %bitcast.27), custom_call_target="tpu_custom_call" | custom-call | flops 1073741824 | bytes 2100224 | tf_op jit(solution)/shard_map/pallas_call | solution.py:216
Async XLA Ops:
  0.0 4.0 %copy-start.2 = (s32[1,128,2]{1,2,0:T(2,128)S(1)}, s32[1,128,2]{1,2,0:T(2,128)}, u32[]{:S(2)}) copy-start(s32[1,128,2]{1,2,0:T(2,128)} %param.13) | copy-start | bytes 3076
  0.0 4.2 %copy-start.3 = (s32[1,128,2]{1,2,0:T(2,128)S(1)}, s32[1,128,2]{1,2,0:T(2,128)}, u32[]{:S(2)}) copy-start(s32[1,128,2]{1,2,0:T(2,128)} %param.15) | copy-start | bytes 3076
  0.0 5.9 %copy-start = (bf16[1,128,2048]{2,1,0:T(8,128)(2,1)S(1)}, bf16[1,128,2048]{2,1,0:T(8,128)(2,1)}, u32[]{:S(2)}) copy-start(bf16[1,128,2048]{2,1,0:T(8,128)(2,1)} %param.11) | copy-start | bytes 1572868
  0.0 5.9 %copy-start.1 = (f32[2048]{0:T(1024)S(1)}, f32[2048]{0:T(1024)}, u32[]{:S(2)}) copy-start(f32[2048]{0:T(1024)} %param.12) | copy-start | bytes 24580
  3.9 2.0 %collective-permute-start = (bf16[128,2048]{1,0:T(8,128)(2,1)S(1)}, bf16[128,2048]{1,0:T(8,128)(2,1)S(1)}, u32[]{:S(2)}, u32[]{:S(2)}) collective-permute-start(bf16[128,2048]{1,0:T(8,128)(2,1)S(1)} %get-tuple-element.10), channel_id=1, source_target_pairs={{0,64},{64,0},{1,65},{65,1},{2,66},{66,2},{3,67},{67,3},{4,68},{68... | collective-permute-start | bytes 1572872 | tf_op jit(solution)/shard_map/ppermute | solution.py:259
  43.1 3.4 %collective-permute-start.1 = (bf16[512,1536]{1,0:T(8,128)(2,1)S(1)}, bf16[512,1536]{1,0:T(8,128)(2,1)S(1)}, u32[]{:S(2)}, u32[]{:S(2)}) collective-permute-start(bf16[512,1536]{1,0:T(8,128)(2,1)S(1)} %bitcast.18), channel_id=1, source_target_pairs={{0,64},{64,0},{1,65},{65,1},{2,66},{66,2},{3,67},{67,3},{4,68},{68... | collective-permute-start | bytes 4718600 | tf_op jit(solution)/shard_map/ppermute | solution.py:275
  57.6 12.0 %collective-permute-start.2 = (bf16[384,2048]{1,0:T(8,128)(2,1)S(1)}, bf16[384,2048]{1,0:T(8,128)(2,1)S(1)}, u32[]{:S(2)}, u32[]{:S(2)}) collective-permute-start(bf16[384,2048]{1,0:T(8,128)(2,1)S(1)} %shard_map.95), channel_id=1, source_target_pairs={{0,64},{64,0},{1,65},{65,1},{2,66},{66,2},{3,67},{67,3},{4,68},{68... | collective-permute-start | bytes 4718600 | tf_op jit(solution)/shard_map/ppermute | solution.py:286
  71.8 5.4 %copy-start.4 = (f32[1,128,2]{1,2,0:T(2,128)S(1)}, f32[1,128,2]{1,2,0:T(2,128)}, u32[]{:S(2)}) copy-start(f32[1,128,2]{1,2,0:T(2,128)} %param.14) | copy-start | bytes 3076
  71.8 30.4 %all-to-all-start.1 = ((bf16[64,8,1536]{2,1,0:T(8,128)(2,1)}), bf16[64,8,1536]{2,1,0:T(8,128)(2,1)S(1)}, u32[]{:S(2)}, u32[]{:S(2)}) async-start(bf16[64,8,1536]{2,1,0:T(8,128)(2,1)} %bitcast.12), calls=%async_computation.1 | async-start | bytes 3145728 | tf_op jit(solution)/shard_map/all_to_all | solution.py:272

commit v4 on v3

--- a/solution.py
+++ b/solution.py
@@ -13,7 +13,8 @@
 TAIL = 3
 SOURCES = 32
 TILE = 512
-LIMIT = 32 << 20
+PIECE = 256
+LIMIT = 16 << 20
 F32, BF16 = jnp.float32, jnp.bfloat16
 VMEM = pl.BlockSpec(memory_space=pltpu.VMEM)
 SMEM = pl.BlockSpec(memory_space=pltpu.SMEM)
@@ -62,7 +63,22 @@
     return out
 
 
-def pack_kernel(experts, own_ref, recv_ref, res_ref, gain_ref, ids_ref, keep_ref, stream_ref, packed_ref):
+def select_kernel(experts, ids_ref, keep_ref, ids_t_ref, keep_t_ref, gate_ref, at_ref, choice_ref, gates_ref):
+    places_t = places(
+        [ids_t_ref[k : k + 1, :] for k in (0, 1)], [keep_t_ref[k : k + 1, :] for k in (0, 1)], experts, 1
+    )
+    at_ref[...] = jnp.concatenate([row for main, tails in places_t for row in (main, *tails)], axis=0)
+    first, second = places(
+        [ids_ref[:, k : k + 1] for k in (0, 1)], [keep_ref[:, k : k + 1] for k in (0, 1)], experts, 0
+    )
+    size = experts * PACK
+    columns = iota((choice_ref.shape[0], size), 1)
+    for j, (a, b) in enumerate(zip([first[0], *first[1]], [second[0], *second[1]])):
+        choice_ref[:, j * size : (j + 1) * size] = ones_where(columns == jnp.concatenate([a, b], axis=0))
+    gates_ref[...] = gate_ref[...]
+
+
+def pack_kernel(own_ref, recv_ref, res_ref, gain_ref, at_ref, stream_ref, packed_ref):
     attended = own_ref[...] + recv_ref[...].astype(F32)
     stream = (res_ref[...].astype(F32) + attended).astype(BF16)
     stream_ref[...] = stream
@@ -71,40 +87,35 @@
     centred = value - jnp.sum(value, axis=1, keepdims=True) / features
     variance = jnp.sum(centred * centred, axis=1, keepdims=True) / features
     normed = (centred / jnp.sqrt(variance + 1e-05) * gain_ref[...]).astype(BF16)
-    ids = [ids_ref[k : k + 1, :] for k in (0, 1)]
-    keep = [keep_ref[k : k + 1, :] for k in (0, 1)]
-    first, second = places(ids, keep, experts, 1)
-    rows = iota((experts * PACK, tokens), 0)
-    main = ones_where((rows == first[0]) | (rows == second[0]))
-    wide = packed_ref.shape[1]
+    size, wide = packed_ref.shape
+    rows = iota((size, tokens), 0)
+
+    def chosen(j):
+        return ones_where((rows == at_ref[j : j + 1, :]) | (rows == at_ref[j + 1 + TAIL : j + 2 + TAIL, :]))
+
+    main = chosen(0)
     for j, part in enumerate(parts_of(wide)):
-        tail = ones_where((rows == first[1][j]) | (rows == second[1][j]))
         packed_ref[:, part] = dot(
-            jnp.concatenate([main, tail], axis=1), jnp.concatenate([normed[:, part], normed[:, wide:]], axis=0)
+            jnp.concatenate([main, chosen(1 + j)], axis=1),
+            jnp.concatenate([normed[:, part], normed[:, wide:]], axis=0),
         ).astype(BF16)
 
 
-def combine_kernel(experts, packed_ref, stream_ref, ids_ref, keep_ref, gate_ref, out_ref):
-    ids = [ids_ref[:, k : k + 1] for k in (0, 1)]
-    keep = [keep_ref[:, k : k + 1] for k in (0, 1)]
-    first, second = places(ids, keep, experts, 0)
-    tokens = ids[0].shape[0]
-    columns = iota((2 * tokens, experts * PACK), 1)
+def combine_kernel(packed_ref, stream_ref, choice_ref, gate_ref, out_ref):
+    size, wide = packed_ref.shape
+    tokens = out_ref.shape[0]
     gate = [gate_ref[:, k : k + 1] for k in (0, 1)]
-    wide = packed_ref.shape[1]
     parts = parts_of(wide)
 
     def finish(at, rows):
         mixed = gate[0] * rows[:tokens] + gate[1] * rows[tokens:]
         out_ref[:, at] = (stream_ref[:, at].astype(F32) + mixed).astype(BF16)
 
-    main = ones_where(columns == jnp.concatenate([first[0], second[0]], axis=0))
     for part in parts:
-        finish(part, dot(main, packed_ref[:, part]))
-    tails = [ones_where(columns == jnp.concatenate([first[1][j], second[1][j]], axis=0)) for j in range(TAIL)]
+        finish(part, dot(choice_ref[:, :size], packed_ref[:, part]))
     finish(
         slice(wide, None),
-        dot(jnp.concatenate(tails, axis=1), jnp.concatenate([packed_ref[:, part] for part in parts], axis=0)),
+        dot(choice_ref[:, size:], jnp.concatenate([packed_ref[:, part] for part in parts], axis=0)),
     )
 
 
@@ -132,19 +143,32 @@
 
 
 def tile_copy(hbm_ref, vmem_ref, sems, i):
-    at = pl.ds(pl.multiple_of(i * TILE, TILE), TILE)
+    at = pl.ds(pl.multiple_of(i * PIECE, PIECE), PIECE)
     return pltpu.make_async_copy(hbm_ref.at[:, at], vmem_ref.at[:, at], sems.at[i])
 
 
 def start_copies(hbm_ref, vmem_ref, sems):
-    for i in range(hbm_ref.shape[1] // TILE):
+    for i in range(hbm_ref.shape[1] // PIECE):
         tile_copy(hbm_ref, vmem_ref, sems, i).start()
 
 
-def tiled(hbm_ref, vmem_ref, sems, step):
-    @pl.loop(0, hbm_ref.shape[1] // TILE)
+def tiled(width, step, copies=None):
+    def wait(i):
+        if copies is not None:
+            tile_copy(*copies, i).wait()
+
+    pieces = TILE // PIECE
+    first = 0
+    if copies is not None:
+        first = 1
+        for i in range(pieces):
+            wait(i)
+            step(slice(i * PIECE, (i + 1) * PIECE))
+
+    @pl.loop(first, width // TILE)
     def _(i):
-        tile_copy(hbm_ref, vmem_ref, sems, i).wait()
+        for p in range(pieces):
+            wait(i * pieces + p)
         step(pl.ds(pl.multiple_of(i * TILE, TILE), TILE))
 
 
@@ -155,31 +179,30 @@
     def step(at):
         hidden_ref[:, at] = jnp.maximum(dot(rows_ref[...], in_ref[:, at]), 0.0).astype(BF16)
 
-    tiled(in_hbm, in_ref, sems, step)
-
-
-def result_kernel(hidden_ref, out_hbm, result_ref, out_ref, sems):
+    tiled(in_ref.shape[1], step, (in_hbm, in_ref, sems))
+
+
+def both_kernel(packed_ref, in_ref, out_hbm, result_ref, out_ref, rows_ref, hidden_ref, sems):
     start_copies(out_hbm, out_ref, sems)
-
+    unpack_into(packed_ref, rows_ref)
+
+    def step_in(at):
+        hidden_ref[:, at] = jnp.maximum(dot(rows_ref[...], in_ref[:, at]), 0.0).astype(BF16)
+
+    def step_out(at):
+        result_ref[:, at] = dot(hidden_ref[...], out_ref[:, at]).astype(result_ref.dtype)
+
+    tiled(in_ref.shape[1], step_in)
+    for i in range(out_hbm.shape[1] // PIECE):
+        tile_copy(out_hbm, out_ref, sems, i).wait()
+    tiled(out_ref.shape[1], step_out)
+
+
+def result_kernel(hidden_ref, out_ref, result_ref):
     def step(at):
         result_ref[:, at] = dot(hidden_ref[...], out_ref[:, at]).astype(result_ref.dtype)
 
-    tiled(out_hbm, out_ref, sems, step)
-
-
-def both_kernel(packed_ref, in_hbm, out_hbm, result_ref, in_ref, rows_ref, hidden_ref, out_ref, in_sems, out_sems):
-    start_copies(in_hbm, in_ref, in_sems)
-    start_copies(out_hbm, out_ref, out_sems)
-    unpack_into(packed_ref, rows_ref)
-
-    def step_in(at):
-        hidden_ref[:, at] = jnp.maximum(dot(rows_ref[...], in_ref[:, at]), 0.0).astype(BF16)
-
-    def step_out(at):
-        result_ref[:, at] = dot(hidden_ref[...], out_ref[:, at]).astype(result_ref.dtype)
-
-    tiled(in_hbm, in_ref, in_sems, step_in)
-    tiled(out_hbm, out_ref, out_sems, step_out)
+    tiled(out_ref.shape[1], step)
 
 
 def add_kernel(own_ref, recv_ref, packed_ref):
@@ -209,7 +232,7 @@
         own_ref[:, at] = jnp.where(first, both[:tokens], both[tokens:])
         other_ref[:, at] = jnp.where(first, both[tokens:], both[:tokens]).astype(BF16)
 
-    tiled(weight_hbm, weight_ref, sems, step)
+    tiled(weight_ref.shape[1], step, (weight_hbm, weight_ref, sems))
 
 
 def call(kernel, flops, out_shape, args, specs=None, scratch=(), limit=LIMIT):
@@ -231,7 +254,7 @@
 
 
 def sems(weight):
-    return pltpu.SemaphoreType.DMA((weight.shape[1] // TILE,))
+    return pltpu.SemaphoreType.DMA((weight.shape[1] // PIECE,))
 
 
 def vmem(a):
@@ -257,14 +280,25 @@
         scratch=[vmem(context), vmem(out_weight), pltpu.SemaphoreType.DMA(()), sems(out_weight)],
     )
     recv = lax.ppermute(other, "tp", SWAP)
+    ids, keep = expert_ids[0], keep_mask[0]
+    at, choice, gates = call(
+        functools.partial(select_kernel, experts),
+        tokens * tokens * experts * PACK,
+        [
+            shape(2 + 2 * TAIL, tokens, dtype=jnp.int32),
+            shape(2 * tokens, (1 + TAIL) * experts * PACK),
+            shape(tokens, 2, dtype=F32),
+        ],
+        (ids, keep, ids.T, keep.T, gate_weights[0]),
+    )
     packed_shape = shape(experts * PACK, features * SLOT // PACK)
     rows_shape = shape(experts * SLOT, features)
     moving = 4 * tokens * experts * PACK * features
     stream, outgoing = call(
-        functools.partial(pack_kernel, experts),
+        pack_kernel,
         moving,
         [shape(tokens, features), packed_shape],
-        (own, recv, residual_in[0], norm_gain[None, :], expert_ids[0].T, keep_mask[0].T),
+        (own, recv, residual_in[0], norm_gain[None, :], at),
     )
 
     def exchange(packed):
@@ -275,27 +309,19 @@
     rows_other = lax.ppermute(rows, "tp", SWAP)
     half = 2 * experts * SLOT * features * units
     row_buffer, hidden_shape = vmem(rows_shape), shape(experts * SLOT, units)
-    hidden = call(
-        hidden_kernel, half, hidden_shape, (rows, weight_in), specs=[VMEM, HBM],
-        scratch=[vmem(weight_in), row_buffer, sems(weight_in)],
-    )
-    part_other = call(
-        both_kernel, 2 * half, rows_shape, (rows_other, weight_in, weight_out), specs=[VMEM, HBM, HBM],
-        scratch=[vmem(weight_in), row_buffer, vmem(hidden_shape), vmem(weight_out), sems(weight_in), sems(weight_out)],
+    hidden, weight_in = call(
+        hidden_kernel, half, [hidden_shape, vmem(weight_in)], (rows, weight_in), specs=[VMEM, HBM],
+        scratch=[row_buffer, sems(weight_in)],
+    )
+    part_other, weight_out = call(
+        both_kernel, 2 * half, [rows_shape, vmem(weight_out)], (rows_other, weight_in, weight_out),
+        specs=[VMEM, VMEM, HBM], scratch=[row_buffer, vmem(hidden_shape), sems(weight_out)],
     )
     part_recv = lax.ppermute(part_other, "tp", SWAP)
-    part_own = call(
-        result_kernel, half, shape(*rows_shape.shape, dtype=F32), (hidden, weight_out),
-        specs=[VMEM, HBM], scratch=[vmem(weight_out), sems(weight_out)],
-    )
+    part_own = call(result_kernel, half, shape(*rows_shape.shape, dtype=F32), (hidden, weight_out))
     results = call(add_kernel, moving, packed_shape, (part_own, part_recv))
     returned = exchange(results)
-    return call(
-        functools.partial(combine_kernel, experts),
-        2 * moving,
-        shape(tokens, features),
-        (returned, stream, expert_ids[0], keep_mask[0], gate_weights[0]),
-    )[None]
+    return call(combine_kernel, 2 * moving, shape(tokens, features), (returned, stream, choice, gates))[None]
 
 
 def solution(mesh):

time: 105 us -> 96.1 us (0.915)
  blocking collectives: 36.1 us -> 65.8 us
  waiting for transfers between devices: 29.8 us -> 0.81 us
  starting transfers between devices: 5.73 us -> 0.68 us
  Pallas kernels: 32.4 us -> 28.2 us
    all_to_all x1 -> x2, blocking collectives: 36.1 us -> 65.8 us  [exchange(): lax.all_to_all(blocks, 'ep', split_axis=0, concat_axis=0, tiled=True)]
    all_to_all x1 -> x0, waiting for transfers between devices: 24.8 us -> none  [exchange(): lax.all_to_all(blocks, 'ep', split_axis=0, concat_axis=0, tiled=True)]
    all_to_all x1 -> x0, starting transfers between devices: 5.42 us -> none  [exchange(): lax.all_to_all(blocks, 'ep', split_axis=0, concat_axis=0, tiled=True)]
    pallas_call x7 -> x8, Pallas kernels: 32.4 us -> 28.2 us  [call(): pl.pallas_call(kernel, in_specs=specs or [VMEM] * len(args), out_specs=ja...]
    ppermute x1, waiting for transfers between devices: 3.41 us -> 0.01 us  [body(): rows_other = lax.ppermute(rows, 'tp', SWAP)]
  transfers between devices with their start and end apart: 4 -> 3, of which waited for: 3 -> 1; matrix products, arithmetic and copies ran while one was open for 0% -> 0% of each run, Pallas kernels for 11% -> 11%
where the time goes in v4:
time: 96.1 us; the launch traced here: 95.9 us
  blocking collectives  65.8 us (68%)
  Pallas kernels  28.2 us (29%)
    all_to_all x2, blocking collectives, exchange(): lax.all_to_all(blocks, 'ep', split_axis=0, concat_axis=0, tiled=True)  65.8 us
    pallas_call x8, Pallas kernels, call(): pl.pallas_call(kernel, in_specs=specs or [VMEM] * len(args), out_specs=ja...  28.2 us
  transfers between devices with their start and end apart: 3, of which 1 were waited for; matrix products, arithmetic and copies ran while one was open for 0% of the time, Pallas kernels for 11%

profile of v4, /device:TPU:0, one launch (start us, length us, event | category | flops | bytes accessed | tf_op | source)
XLA Modules:
  0.0 95.9 jit_solution(3938274371475640010)
XLA Ops:
  0.0 0.0 copy-start.4
  0.0 0.0 copy-start.3
  0.0 0.0 copy-start.2
  0.0 0.0 copy-start
  0.0 0.0 copy-start.1
  0.0 4.5 %shard_map.91 = (f32[128,2048]{1,0:T(8,128)S(1)}, bf16[128,2048]{1,0:T(8,128)(2,1)S(1)}) custom-call(s32[1]{0:T(128)} %bitcast.core_ref, bf16[256,1024]{1,0:T(8,128)(2,1)} %bitcast.30, bf16[1024,2048]{1,0:T(8,128)(2,1)} %weight_hbm.1), custom_call_target="tpu_custom_call" | custom-call | flops 1073741824 | bytes 4718596 | tf_op jit(solution)/shard_map/pallas_call | solution.py:239
  4.5 0.1 collective-permute-start
  4.6 0.0 copy-done.4
  4.7 0.1 copy.10
  4.8 0.0 copy-done.3
  4.8 0.1 copy.12.keep_ref
  4.9 0.0 copy-done.2
  4.9 0.1 copy.11.ids_ref
  5.0 0.7 shard_map.92
  5.7 0.8 collective-permute-done.recv_ref
  6.5 0.0 copy-done
  6.5 0.0 copy-done.1
  6.5 1.1 %shard_map.93 = (bf16[128,2048]{1,0:T(8,128)(2,1)S(1)}, bf16[512,1536]{1,0:T(8,128)(2,1)S(1)}) custom-call(f32[128,2048]{1,0:T(8,128)S(1)} %get-tuple-element.16.own_ref, bf16[128,2048]{1,0:T(8,128)(2,1)S(1)} %collective-permute-done.recv_ref, bf16[128,2048]{1,0:T(8,128)(2,1)S(1)} %bitcast.23, f32[1,2048]{1,0:T(1,128)S(1)} %bitcast.25, ...), custom_call_target="tpu_custom_call" | custom-call | flops 536870912 | bytes 2109440 | tf_op jit(solution)/shard_map/pallas_call | solution.py:239
  7.7 36.1 %all_to_all.10 = bf16[64,8,1536]{2,1,0:T(8,128)(2,1)S(1)} all-to-all(bf16[64,8,1536]{2,1,0:T(8,128)(2,1)S(1)} %bitcast.22), channel_id=1, replica_groups=mesh['tp'=2,'ep'=64] {'ep'}, dimensions={0} | all-to-all | bytes 3145728 | tf_op jit(solution)/shard_map/all_to_all | solution.py:306
  43.7 0.0 collective-permute-start.1
  43.7 6.2 %shard_map.94 = (bf16[384,2048]{1,0:T(8,128)(2,1)S(1)}, bf16[2048,2048]{1,0:T(8,128)(2,1)S(1)}) custom-call(bf16[512,1536]{1,0:T(8,128)(2,1)S(1)} %bitcast.20, bf16[2048,2048]{1,0:T(8,128)(2,1)} %bitcast.31), custom_call_target="tpu_custom_call" | custom-call | flops 3221225472 | bytes 9961472 | tf_op jit(solution)/shard_map/pallas_call | solution.py:239
  49.9 0.0 collective-permute-done.1.packed_ref
  50.0 8.8 %shard_map.95 = (bf16[384,2048]{1,0:T(8,128)(2,1)S(1)}, bf16[2048,2048]{1,0:T(8,128)(2,1)S(1)}) custom-call(bf16[512,1536]{1,0:T(8,128)(2,1)S(1)} %collective-permute-done.1.packed_ref, bf16[2048,2048]{1,0:T(8,128)(2,1)S(1)} %get-tuple-element.21.in_ref, bf16[2048,2048]{1,0:T(8,128)(2,1)} %bitcast.32), custom_call_target="tpu_custom_call" | custom-call | flops 6442450944 | bytes 18350080 | tf_op jit(solution)/shard_map/pallas_call | solution.py:239
  58.7 0.6 collective-permute-start.2
  59.3 3.9 %shard_map.96.own_ref = f32[384,2048]{1,0:T(8,128)S(1)} custom-call(bf16[384,2048]{1,0:T(8,128)(2,1)S(1)} %get-tuple-element.20.hidden_ref, bf16[2048,2048]{1,0:T(8,128)(2,1)S(1)} %get-tuple-element.22.out_ref), custom_call_target="tpu_custom_call" | custom-call | flops 3221225472 | bytes 9961472 | tf_op jit(solution)/shard_map/pallas_call | solution.py:239
  63.3 0.0 collective-permute-done.2.recv_ref
  63.3 1.1 %shard_map.97 = bf16[512,1536]{1,0:T(8,128)(2,1)S(1)} custom-call(f32[384,2048]{1,0:T(8,128)S(1)} %shard_map.96.own_ref, bf16[384,2048]{1,0:T(8,128)(2,1)S(1)} %collective-permute-done.2.recv_ref), custom_call_target="tpu_custom_call" | custom-call | flops 536870912 | bytes 4718592 | tf_op jit(solution)/shard_map/pallas_call | solution.py:239
  64.4 29.7 %all_to_all.11 = bf16[64,8,1536]{2,1,0:T(8,128)(2,1)S(1)} all-to-all(bf16[64,8,1536]{2,1,0:T(8,128)(2,1)S(1)} %bitcast.18), channel_id=1, replica_groups=mesh['tp'=2,'ep'=64] {'ep'}, dimensions={0} | all-to-all | bytes 3145728 | tf_op jit(solution)/shard_map/all_to_all | solution.py:306
  94.1 1.8 %shard_map.98 = bf16[128,2048]{1,0:T(8,128)(2,1)} custom-call(bf16[512,1536]{1,0:T(8,128)(2,1)S(1)} %bitcast.21, bf16[128,2048]{1,0:T(8,128)(2,1)S(1)} %get-tuple-element.24.stream_ref, bf16[256,2048]{1,0:T(8,128)(2,1)S(1)} %get-tuple-element.25.choice_ref, f32[128,2]{1,0:T(8,128)S(1)} %get-tuple-element.26.gate_ref), custom_call_target="tpu_custom_call" | custom-call | flops 1073741824 | bytes 3146752 | tf_op jit(solution)/shard_map/pallas_call | solution.py:239
Async XLA Ops:
  0.0 4.6 %copy-start.4 = (f32[1,128,2]{1,2,0:T(2,128)S(1)}, f32[1,128,2]{1,2,0:T(2,128)}, u32[]{:S(2)}) copy-start(f32[1,128,2]{1,2,0:T(2,128)} %param.14) | copy-start | bytes 3076
  0.0 4.8 %copy-start.3 = (s32[1,128,2]{1,2,0:T(2,128)S(1)}, s32[1,128,2]{1,2,0:T(2,128)}, u32[]{:S(2)}) copy-start(s32[1,128,2]{1,2,0:T(2,128)} %param.15) | copy-start | bytes 3076
  0.0 4.9 %copy-start.2 = (s32[1,128,2]{1,2,0:T(2,128)S(1)}, s32[1,128,2]{1,2,0:T(2,128)}, u32[]{:S(2)}) copy-start(s32[1,128,2]{1,2,0:T(2,128)} %param.13) | copy-start | bytes 3076
  0.0 6.5 %copy-start = (bf16[1,128,2048]{2,1,0:T(8,128)(2,1)S(1)}, bf16[1,128,2048]{2,1,0:T(8,128)(2,1)}, u32[]{:S(2)}) copy-start(bf16[1,128,2048]{2,1,0:T(8,128)(2,1)} %param.11) | copy-start | bytes 1572868
  0.0 6.5 %copy-start.1 = (f32[2048]{0:T(1024)S(1)}, f32[2048]{0:T(1024)}, u32[]{:S(2)}) copy-start(f32[2048]{0:T(1024)} %param.12) | copy-start | bytes 24580
  4.5 2.0 %collective-permute-start = (bf16[128,2048]{1,0:T(8,128)(2,1)S(1)}, bf16[128,2048]{1,0:T(8,128)(2,1)S(1)}, u32[]{:S(2)}, u32[]{:S(2)}) collective-permute-start(bf16[128,2048]{1,0:T(8,128)(2,1)S(1)} %get-tuple-element.17), channel_id=1, source_target_pairs={{0,64},{64,0},{1,65},{65,1},{2,66},{66,2},{3,67},{67,3},{4,68},{68... | collective-permute-start | bytes 1572872 | tf_op jit(solution)/shard_map/ppermute | solution.py:282
  43.7 6.2 %collective-permute-start.1 = (bf16[512,1536]{1,0:T(8,128)(2,1)S(1)}, bf16[512,1536]{1,0:T(8,128)(2,1)S(1)}, u32[]{:S(2)}, u32[]{:S(2)}) collective-permute-start(bf16[512,1536]{1,0:T(8,128)(2,1)S(1)} %bitcast.19), channel_id=1, source_target_pairs={{0,64},{64,0},{1,65},{65,1},{2,66},{66,2},{3,67},{67,3},{4,68},{68... | collective-permute-start | bytes 4718600 | tf_op jit(solution)/shard_map/ppermute | solution.py:309
  58.7 4.5 %collective-permute-start.2 = (bf16[384,2048]{1,0:T(8,128)(2,1)S(1)}, bf16[384,2048]{1,0:T(8,128)(2,1)S(1)}, u32[]{:S(2)}, u32[]{:S(2)}) collective-permute-start(bf16[384,2048]{1,0:T(8,128)(2,1)S(1)} %get-tuple-element.23), channel_id=1, source_target_pairs={{0,64},{64,0},{1,65},{65,1},{2,66},{66,2},{3,67},{67,3},{4,68},{68... | collective-permute-start | bytes 4718600 | tf_op jit(solution)/shard_map/ppermute | solution.py:320

commit v5 on v3

v5 whole, which is shorter than its diff:
```python
import functools

import jax
import jax.numpy as jnp
from jax import lax
from jax.experimental import pallas as pl
from jax.experimental.pallas import tpu as pltpu
from jax.sharding import PartitionSpec as P


SLOT = 6
PACK = 8
SPLIT = (4, 2)
FIRST = (0, 4)
SOURCES = 32
TILE = 512
LIMIT = 16 << 20
F32, BF16 = jnp.float32, jnp.bfloat16
VMEM = pl.BlockSpec(memory_space=pltpu.VMEM)
SMEM = pl.BlockSpec(memory_space=pltpu.SMEM)
HBM = pl.BlockSpec(memory_space=pltpu.HBM)
SWAP = [(0, 1), (1, 0)]


def dot(a, b):
    return jnp.dot(a, b, preferred_element_type=F32)


def iota(shape, dim):
    return lax.broadcasted_iota(jnp.int32, shape, dim)


def ones_where(condition):
    return jnp.where(condition, 1.0, 0.0).astype(BF16)


def kinds(features):
    start = 0
    for kind, slots in enumerate(SPLIT):
        pieces = PACK // slots
        wide = features // pieces
        yield kind, slots, pieces, wide, slice(start, start + wide)
        start += wide


def ranks(ids, keep, experts):
    tokens = ids[0].shape[1]
    member = iota((experts, tokens), 0)
    hot = [jnp.where((member == ids[k]) & (keep[k] > 0), 1.0, 0.0) for k in (0, 1)]
    older = ones_where(iota((tokens, tokens), 0) < iota((tokens, tokens), 1))
    out = []
    base = 0.0
    for k in (0, 1):
        before = dot(hot[k].astype(BF16), older) + base
        out.append(jnp.sum(hot[k] * before, axis=0, keepdims=True).astype(jnp.int32))
        base = base + jnp.sum(hot[k], axis=1, keepdims=True)
    return out


def packed_row(ids, keep, rank, kind, piece):
    slot = rank - FIRST[kind]
    inside = (keep > 0) & (slot >= 0) & (slot < SPLIT[kind])
    return jnp.where(inside, ids * PACK + SPLIT[kind] * piece + slot, -1)


def upright(row):
    size = row.shape[1]
    return jnp.sum(
        jnp.where(iota((size, size), 0) == iota((size, size), 1), row, jnp.zeros((), row.dtype)), axis=1, keepdims=True
    )


def select_kernel(experts, ids_ref, keep_ref, gate_ref, send_ref, take_ref, gates_ref):
    size, tokens = experts * PACK, ids_ref.shape[1]
    ids = [ids_ref[k : k + 1, :] for k in (0, 1)]
    keep = [keep_ref[k : k + 1, :] for k in (0, 1)]
    rank = ranks(ids, keep, experts)
    start = 0
    for kind, slots in enumerate(SPLIT):
        pieces = PACK // slots
        rows = iota((size, pieces * tokens), 0)
        a, b = (
            jnp.concatenate([packed_row(ids[k], keep[k], rank[k], kind, h) for h in range(pieces)], axis=1)
            for k in (0, 1)
        )
        send_ref[:, start : start + pieces * tokens] = ones_where((rows == a) | (rows == b))
        start += pieces * tokens
    ids, keep, rank = ([upright(row) for row in rows] for rows in (ids, keep, rank))
    columns = iota((tokens, size), 1)
    start = 0
    for kind, slots in enumerate(SPLIT):
        for h in range(PACK // slots):
            for k in (0, 1):
                take_ref[start : start + tokens, :] = ones_where(
                    columns == packed_row(ids[k], keep[k], rank[k], kind, h)
                )
                start += tokens
    for k in (0, 1):
        gates_ref[:, k : k + 1] = upright(gate_ref[k : k + 1, :])


def stack_pieces(rows, pieces, wide):
    return jnp.concatenate([rows[:, h * wide : (h + 1) * wide] for h in range(pieces)], axis=0)


def pack_kernel(own_ref, recv_ref, res_ref, gain_ref, send_ref, stream_ref, packed_ref):
    attended = own_ref[...] + recv_ref[...].astype(F32)
    stream = (res_ref[...].astype(F32) + attended).astype(BF16)
    stream_ref[...] = stream
    value = stream.astype(F32)
    tokens, features = value.shape
    centred = value - jnp.sum(value, axis=1, keepdims=True) / features
    variance = jnp.sum(centred * centred, axis=1, keepdims=True) / features
    normed = (centred / jnp.sqrt(variance + 1e-05) * gain_ref[...]).astype(BF16)
    start = 0
    for _, _, pieces, wide, columns in kinds(features):
        send = send_ref[:, start : start + pieces * tokens]
        packed_ref[:, columns] = dot(send, stack_pieces(normed, pieces, wide)).astype(BF16)
        start += pieces * tokens


def combine_kernel(packed_ref, stream_ref, take_ref, gate_ref, out_ref):
    tokens, features = out_ref.shape
    gate = [gate_ref[:, k : k + 1] for k in (0, 1)]
    start = 0
    total = None
    for _, _, pieces, wide, columns in kinds(features):
        count = 2 * pieces * tokens
        rows = dot(take_ref[start : start + count, :], packed_ref[:, columns])
        start += count
        mixed = []
        for h in range(pieces):
            at = 2 * h * tokens
            mixed.append(gate[0] * rows[at : at + tokens] + gate[1] * rows[at + tokens : at + 2 * tokens])
        mixed = jnp.concatenate(mixed, axis=1)
        total = mixed if total is None else total + mixed
    out_ref[...] = (stream_ref[...].astype(F32) + total).astype(BF16)


def mover(slots, reverse):
    size = SOURCES * PACK
    row, col = iota((size, size), 1 if reverse else 0), iota((size, size), 0 if reverse else 1)
    source, at = col >> 3, col & (PACK - 1)
    piece, slot = at >> (slots.bit_length() - 1), at & (slots - 1)
    return ones_where(row == piece * (SOURCES * slots) + slots * source + slot)


def blocks(packed_rows, features):
    tall = SOURCES * PACK
    for g in range(packed_rows // tall):
        start = g * SOURCES * SLOT
        for kind, slots, pieces, wide, columns in kinds(features):
            yield kind, slice(g * tall, (g + 1) * tall), columns, start, SOURCES * slots, pieces, wide
            start += SOURCES * slots


def unpack_into(packed_ref, rows_ref):
    movers = [mover(slots, False) for slots in SPLIT]
    for kind, at, columns, start, count, pieces, wide in blocks(packed_ref.shape[0], rows_ref.shape[1]):
        moved = dot(movers[kind], packed_ref[at, columns]).astype(BF16)
        for h in range(pieces):
            rows_ref[start : start + count, h * wide : (h + 1) * wide] = moved[h * count : (h + 1) * count]


def columns_of(i):
    return pl.ds(pl.multiple_of(i * TILE, TILE), TILE)


def tile_copy(hbm_ref, vmem_ref, sems, i, skip=0):
    return pltpu.make_async_copy(hbm_ref.at[:, columns_of(i + skip)], vmem_ref.at[:, columns_of(i)], sems.at[i])


def start_copies(hbm_ref, vmem_ref, sems, skip=0):
    for i in range(vmem_ref.shape[1] // TILE):
        tile_copy(hbm_ref, vmem_ref, sems, i, skip).start()


def hidden_kernel(packed_ref, first_ref, in_hbm, hidden_ref, rest_ref, rows_ref, sems):
    start_copies(in_hbm, rest_ref, sems, 1)
    unpack_into(packed_ref, rows_ref)
    hidden_ref[:, :TILE] = jnp.maximum(dot(rows_ref[...], first_ref[...]), 0.0).astype(BF16)

    @pl.loop(0, rest_ref.shape[1] // TILE)
    def _(i):
        tile_copy(in_hbm, rest_ref, sems, i, 1).wait()
        hidden_ref[:, columns_of(i + 1)] = jnp.maximum(dot(rows_ref[...], rest_ref[:, columns_of(i)]), 0.0).astype(BF16)


def both_kernel(packed_ref, first_ref, rest_ref, out_hbm, result_ref, out_ref, rows_ref, hidden_ref, sems):
    start_copies(out_hbm, out_ref, sems)
    unpack_into(packed_ref, rows_ref)
    hidden_ref[:, :TILE] = jnp.maximum(dot(rows_ref[...], first_ref[...]), 0.0).astype(BF16)

    @pl.loop(0, rest_ref.shape[1] // TILE)
    def _(i):
        hidden_ref[:, columns_of(i + 1)] = jnp.maximum(dot(rows_ref[...], rest_ref[:, columns_of(i)]), 0.0).astype(BF16)

    @pl.loop(0, out_ref.shape[1] // TILE)
    def _(i):
        tile_copy(out_hbm, out_ref, sems, i).wait()
        result_ref[:, columns_of(i)] = dot(hidden_ref[...], out_ref[:, columns_of(i)]).astype(BF16)


def result_kernel(hidden_ref, out_ref, result_ref):
    @pl.loop(0, out_ref.shape[1] // TILE)
    def _(i):
        result_ref[:, columns_of(i)] = dot(hidden_ref[...], out_ref[:, columns_of(i)])


def add_kernel(own_ref, recv_ref, packed_ref):
    movers = [mover(slots, True) for slots in SPLIT]
    for kind, at, columns, start, count, pieces, wide in blocks(packed_ref.shape[0], own_ref.shape[1]):
        rows = slice(start, start + count)
        block = (own_ref[rows, :] + recv_ref[rows, :].astype(F32)).astype(BF16)
        packed_ref[at, columns] = dot(movers[kind], stack_pieces(block, pieces, wide)).astype(BF16)


def project_kernel(
    core_ref, context_hbm, weight_hbm, in_hbm, own_ref, other_ref, first_ref, context_ref, weight_ref, sem, sems, first_sem
):
    load = pltpu.make_async_copy(context_hbm, context_ref, sem)
    load.start()
    start_copies(weight_hbm, weight_ref, sems)
    start_copies(in_hbm, first_ref, first_sem)
    load.wait()
    tokens = own_ref.shape[0]
    first = core_ref[0] == 0

    @pl.loop(0, weight_ref.shape[1] // TILE)
    def _(i):
        tile_copy(weight_hbm, weight_ref, sems, i).wait()
        at = columns_of(i)
        both = dot(context_ref[...], weight_ref[:, at])
        own_ref[:, at] = jnp.where(first, both[:tokens], both[tokens:])
        other_ref[:, at] = jnp.where(first, both[tokens:], both[:tokens]).astype(BF16)

    tile_copy(in_hbm, first_ref, first_sem, 0).wait()


def call(kernel, flops, out_shape, args, specs=None, scratch=(), limit=LIMIT):
    return pl.pallas_call(
        kernel,
        in_specs=specs or [VMEM] * len(args),
        out_specs=jax.tree.map(lambda _: VMEM, out_shape),
        out_shape=out_shape,
        scratch_shapes=scratch,
        compiler_params=pltpu.CompilerParams(vmem_limit_bytes=limit),
        cost_estimate=pl.CostEstimate(
            flops=flops, bytes_accessed=sum(a.size * a.dtype.itemsize for a in args), transcendentals=0
        ),
    )(*args)


def shape(*dims, dtype=BF16):
    return jax.ShapeDtypeStruct(dims, dtype)


def sems(columns):
    return pltpu.SemaphoreType.DMA((columns // TILE,))


def vmem(a):
    return pltpu.VMEM(a.shape, a.dtype)


def body(context, out_weight, residual_in, norm_gain, expert_ids, gate_weights, keep_mask, expert_in, expert_out):
    tokens, features = residual_in.shape[1:]
    experts = lax.axis_size("ep")
    units = expert_in.shape[2]

    def in_hbm(a):
        return pltpu.with_memory_space_constraint(a, pltpu.HBM)

    context, out_weight = in_hbm(context[0]), in_hbm(out_weight)
    weight_in, weight_out = in_hbm(expert_in[0]), in_hbm(expert_out[0])
    own, other, in_first = call(
        project_kernel,
        2 * context.size * features,
        [shape(tokens, features, dtype=F32), shape(tokens, features), pltpu.VMEM((features, TILE), BF16)],
        (lax.axis_index("tp")[None], context, out_weight, weight_in),
        specs=[SMEM, HBM, HBM, HBM],
        scratch=[vmem(context), vmem(out_weight), pltpu.SemaphoreType.DMA(()), sems(features), sems(TILE)],
    )
    recv = lax.ppermute(other, "tp", SWAP)
    size = experts * PACK
    pieces = sum(PACK // slots for slots in SPLIT)
    send, take, gates = call(
        functools.partial(select_kernel, experts),
        tokens * tokens * size,
        [shape(size, pieces * tokens), shape(2 * pieces * tokens, size), shape(tokens, 2, dtype=F32)],
        (expert_ids[0].T, keep_mask[0].T, gate_weights[0].T),
    )
    packed_shape = shape(experts * PACK, features * SLOT // PACK)
    rows_shape = shape(experts * SLOT, features)
    moving = 4 * tokens * experts * PACK * features
    stream, outgoing = call(
        pack_kernel,
        moving,
        [shape(tokens, features), packed_shape],
        (own, recv, residual_in[0], norm_gain[None, :], send),
    )

    def exchange(packed):
        blocks = packed.reshape(experts, PACK, packed.shape[1])
        return lax.all_to_all(blocks, "ep", split_axis=0, concat_axis=0, tiled=True).reshape(packed.shape)

    rows = exchange(outgoing)
    rows_other = lax.ppermute(rows, "tp", SWAP)
    half = 2 * experts * SLOT * features * units
    row_buffer, hidden_shape = vmem(rows_shape), shape(experts * SLOT, units)
    hidden, in_rest = call(
        hidden_kernel, half, [hidden_shape, pltpu.VMEM((features, units - TILE), BF16)],
        (rows, in_first, weight_in), specs=[VMEM, VMEM, HBM], scratch=[row_buffer, sems(units - TILE)],
    )
    part_other, weight_out = call(
        both_kernel, 2 * half, [rows_shape, vmem(weight_out)],
        (rows_other, in_first, in_rest, weight_out), specs=[VMEM, VMEM, VMEM, HBM],
        scratch=[row_buffer, vmem(hidden_shape), sems(features)],
    )
    part_recv = lax.ppermute(part_other, "tp", SWAP)
    part_own = call(result_kernel, half, shape(*rows_shape.shape, dtype=F32), (hidden, weight_out))
    results = call(add_kernel, moving, packed_shape, (part_own, part_recv))
    returned = exchange(results)
    return call(combine_kernel, 2 * moving, shape(tokens, features), (returned, stream, take, gates))[None]


def solution(mesh):
    return jax.shard_map(
        body,
        mesh=mesh,
        in_specs=(
            P("ep", None, "tp"),
            P("tp", None),
            P("ep", "tp", None),
            P(),
            P("ep", "tp", None),
            P("ep", "tp", None),
            P("ep", "tp", None),
            P("ep", None, "tp"),
            P("ep", "tp", None),
        ),
        out_specs=P("ep", "tp", None),
        check_vma=False,
    )
```

time: 105 us -> 93.3 us (0.89)
  blocking collectives: 36.1 us -> 65.8 us
  waiting for transfers between devices: 29.8 us -> 0.76 us
  Pallas kernels: 32.4 us -> 25.8 us
  starting transfers between devices: 5.73 us -> 0.67 us
    all_to_all x1 -> x2, blocking collectives: 36.1 us -> 65.8 us  [exchange(): lax.all_to_all(blocks, 'ep', split_axis=0, concat_axis=0, tiled=True)]
    all_to_all x1 -> x0, waiting for transfers between devices: 24.8 us -> none  [exchange(): lax.all_to_all(blocks, 'ep', split_axis=0, concat_axis=0, tiled=True)]
    pallas_call x7 -> x8, Pallas kernels: 32.4 us -> 25.8 us  [call(): pl.pallas_call(kernel, in_specs=specs or [VMEM] * len(args), out_specs=ja...]
    all_to_all x1 -> x0, starting transfers between devices: 5.42 us -> none  [exchange(): lax.all_to_all(blocks, 'ep', split_axis=0, concat_axis=0, tiled=True)]
    ppermute x1, waiting for transfers between devices: 3.41 us -> 0.01 us  [body(): rows_other = lax.ppermute(rows, 'tp', SWAP)]
  transfers between devices with their start and end apart: 4 -> 3, of which waited for: 3 -> 1; matrix products, arithmetic and copies ran while one was open for 0% -> 0% of each run, Pallas kernels for 11% -> 10%
where the time goes in v5:
time: 93.3 us; the launch traced here: 93.2 us
  blocking collectives  65.8 us (71%)
  Pallas kernels  25.8 us (28%)
    all_to_all x2, blocking collectives, exchange(): lax.all_to_all(blocks, 'ep', split_axis=0, concat_axis=0, tiled=True)  65.8 us
    pallas_call x8, Pallas kernels, call(): pl.pallas_call(kernel, in_specs=specs or [VMEM] * len(args), out_specs=ja...  25.8 us
  transfers between devices with their start and end apart: 3, of which 1 were waited for; matrix products, arithmetic and copies ran while one was open for 0% of the time, Pallas kernels for 10%

profile of v5, /device:TPU:0, one launch (start us, length us, event | category | flops | bytes accessed | tf_op | source)
XLA Modules:
  0.0 93.2 jit_solution(10809478222274431506)
XLA Ops:
  0.0 0.0 copy-start.2
  0.0 0.0 copy-start.3
  0.0 0.0 copy-start.4
  0.0 0.0 copy-start
  0.0 0.0 copy-start.1
  0.0 3.9 %shard_map.91 = (f32[128,2048]{1,0:T(8,128)S(1)}, bf16[128,2048]{1,0:T(8,128)(2,1)S(1)}, bf16[2048,512]{1,0:T(8,128)(2,1)S(1)}) custom-call(s32[1]{0:T(128)} %bitcast.core_ref, bf16[256,1024]{1,0:T(8,128)(2,1)} %bitcast.32, bf16[1024,2048]{1,0:T(8,128)(2,1)} %weight_hbm.1, bf16[2048,2048]{1,0:T(8,128)(2,1)} %bitcast.30), custom_call_target="tpu_custom_call" | custom-call | flops 1073741824 | bytes 13107204 | tf_op jit(solution)/shard_map/pallas_call | solution.py:241
  3.9 0.1 collective-permute-start
  4.0 0.0 copy-done.2
  4.0 0.0 copy-done.3
  4.0 0.0 copy-done.4
  4.1 1.1 %shard_map.92 = (bf16[512,768]{1,0:T(8,128)(2,1)S(1)}, bf16[1536,512]{1,0:T(8,128)(2,1)S(1)}, f32[128,2]{1,0:T(8,128)S(1)}) custom-call(s32[2,128]{1,0:T(2,128)S(1)} %bitcast.27, s32[2,128]{1,0:T(2,128)S(1)} %bitcast.28, f32[2,128]{1,0:T(2,128)S(1)} %bitcast.29), custom_call_target="tpu_custom_call" | custom-call | flops 8388608 | bytes 3072 | tf_op jit(solution)/shard_map/pallas_call | solution.py:241
  5.2 0.8 collective-permute-done.recv_ref
  5.9 0.0 copy-done
  5.9 0.0 copy-done.1
  5.9 1.2 %shard_map.93 = (bf16[128,2048]{1,0:T(8,128)(2,1)S(1)}, bf16[512,1536]{1,0:T(8,128)(2,1)S(1)}) custom-call(f32[128,2048]{1,0:T(8,128)S(1)} %get-tuple-element.17.own_ref, bf16[128,2048]{1,0:T(8,128)(2,1)S(1)} %collective-permute-done.recv_ref, bf16[128,2048]{1,0:T(8,128)(2,1)S(1)} %bitcast.25, f32[1,2048]{1,0:T(1,128)S(1)} %bitcast.26, ...), custom_call_target="tpu_custom_call" | custom-call | flops 536870912 | bytes 2891776 | tf_op jit(solution)/shard_map/pallas_call | solution.py:241
  7.2 36.1 %all_to_all.10 = bf16[64,8,1536]{2,1,0:T(8,128)(2,1)S(1)} all-to-all(bf16[64,8,1536]{2,1,0:T(8,128)(2,1)S(1)} %bitcast.24), channel_id=1, replica_groups=mesh['tp'=2,'ep'=64] {'ep'}, dimensions={0} | all-to-all | bytes 3145728 | tf_op jit(solution)/shard_map/all_to_all | solution.py:305
  43.2 0.0 collective-permute-start.1
  43.2 4.6 %shard_map.94 = (bf16[384,2048]{1,0:T(8,128)(2,1)S(1)}, bf16[2048,1536]{1,0:T(8,128)(2,1)S(1)}) custom-call(bf16[512,1536]{1,0:T(8,128)(2,1)S(1)} %bitcast.23, bf16[2048,512]{1,0:T(8,128)(2,1)S(1)} %get-tuple-element.21.first_ref, bf16[2048,2048]{1,0:T(8,128)(2,1)} %bitcast.31), custom_call_target="tpu_custom_call" | custom-call | flops 3221225472 | bytes 12058624 | tf_op jit(solution)/shard_map/pallas_call | solution.py:241
  47.8 0.0 collective-permute-done.1.packed_ref
  47.8 8.3 %shard_map.95 = (bf16[384,2048]{1,0:T(8,128)(2,1)S(1)}, bf16[2048,2048]{1,0:T(8,128)(2,1)S(1)}) custom-call(bf16[512,1536]{1,0:T(8,128)(2,1)S(1)} %collective-permute-done.1.packed_ref, bf16[2048,512]{1,0:T(8,128)(2,1)S(1)} %get-tuple-element.21.first_ref, bf16[2048,1536]{1,0:T(8,128)(2,1)S(1)} %get-tuple-element.23.rest_ref, bf16[2048,2048]{1,0:T(8,128)(2,1)} %bitcast.33), custom_call_target="tpu_custom_call" | custom-call | flops 6442450944 | bytes 18350080 | tf_op jit(solution)/shard_map/pallas_call | solution.py:241
  56.2 0.6 collective-permute-start.2
  56.7 3.9 %shard_map.96.own_ref = f32[384,2048]{1,0:T(8,128)S(1)} custom-call(bf16[384,2048]{1,0:T(8,128)(2,1)S(1)} %get-tuple-element.22.hidden_ref, bf16[2048,2048]{1,0:T(8,128)(2,1)S(1)} %get-tuple-element.24.out_ref), custom_call_target="tpu_custom_call" | custom-call | flops 3221225472 | bytes 9961472 | tf_op jit(solution)/shard_map/pallas_call | solution.py:241
  60.7 0.0 collective-permute-done.2.recv_ref
  60.7 0.7 shard_map.97
  61.4 29.7 %all_to_all.11 = bf16[64,8,1536]{2,1,0:T(8,128)(2,1)S(1)} all-to-all(bf16[64,8,1536]{2,1,0:T(8,128)(2,1)S(1)} %bitcast.21), channel_id=1, replica_groups=mesh['tp'=2,'ep'=64] {'ep'}, dimensions={0} | all-to-all | bytes 3145728 | tf_op jit(solution)/shard_map/all_to_all | solution.py:305
  91.1 2.1 %shard_map.98 = bf16[128,2048]{1,0:T(8,128)(2,1)} custom-call(bf16[512,1536]{1,0:T(8,128)(2,1)S(1)} %bitcast.20, bf16[128,2048]{1,0:T(8,128)(2,1)S(1)} %get-tuple-element.26.stream_ref, bf16[1536,512]{1,0:T(8,128)(2,1)S(1)} %get-tuple-element.27.take_ref, f32[128,2]{1,0:T(8,128)S(1)} %get-tuple-element.28.gate_ref), custom_call_target="tpu_custom_call" | custom-call | flops 1073741824 | bytes 3671040 | tf_op jit(solution)/shard_map/pallas_call | solution.py:241
Async XLA Ops:
  0.0 4.0 %copy-start.2 = (s32[1,128,2]{1,2,0:T(2,128)S(1)}, s32[1,128,2]{1,2,0:T(2,128)}, u32[]{:S(2)}) copy-start(s32[1,128,2]{1,2,0:T(2,128)} %param.13) | copy-start | bytes 3076
  0.0 4.0 %copy-start.3 = (s32[1,128,2]{1,2,0:T(2,128)S(1)}, s32[1,128,2]{1,2,0:T(2,128)}, u32[]{:S(2)}) copy-start(s32[1,128,2]{1,2,0:T(2,128)} %param.15) | copy-start | bytes 3076
  0.0 4.0 %copy-start.4 = (f32[1,128,2]{1,2,0:T(2,128)S(1)}, f32[1,128,2]{1,2,0:T(2,128)}, u32[]{:S(2)}) copy-start(f32[1,128,2]{1,2,0:T(2,128)} %param.14) | copy-start | bytes 3076
  0.0 5.9 %copy-start = (bf16[1,128,2048]{2,1,0:T(8,128)(2,1)S(1)}, bf16[1,128,2048]{2,1,0:T(8,128)(2,1)}, u32[]{:S(2)}) copy-start(bf16[1,128,2048]{2,1,0:T(8,128)(2,1)} %param.11) | copy-start | bytes 1572868
  0.0 5.9 %copy-start.1 = (f32[2048]{0:T(1024)S(1)}, f32[2048]{0:T(1024)}, u32[]{:S(2)}) copy-start(f32[2048]{0:T(1024)} %param.12) | copy-start | bytes 24580
  3.9 2.0 %collective-permute-start = (bf16[128,2048]{1,0:T(8,128)(2,1)S(1)}, bf16[128,2048]{1,0:T(8,128)(2,1)S(1)}, u32[]{:S(2)}, u32[]{:S(2)}) collective-permute-start(bf16[128,2048]{1,0:T(8,128)(2,1)S(1)} %get-tuple-element.18), channel_id=1, source_target_pairs={{0,64},{64,0},{1,65},{65,1},{2,66},{66,2},{3,67},{67,3},{4,68},{68... | collective-permute-start | bytes 1572872 | tf_op jit(solution)/shard_map/ppermute | solution.py:284
  43.2 4.6 %collective-permute-start.1 = (bf16[512,1536]{1,0:T(8,128)(2,1)S(1)}, bf16[512,1536]{1,0:T(8,128)(2,1)S(1)}, u32[]{:S(2)}, u32[]{:S(2)}) collective-permute-start(bf16[512,1536]{1,0:T(8,128)(2,1)S(1)} %bitcast.22), channel_id=1, source_target_pairs={{0,64},{64,0},{1,65},{65,1},{2,66},{66,2},{3,67},{67,3},{4,68},{68... | collective-permute-start | bytes 4718600 | tf_op jit(solution)/shard_map/ppermute | solution.py:308
  56.2 4.5 %collective-permute-start.2 = (bf16[384,2048]{1,0:T(8,128)(2,1)S(1)}, bf16[384,2048]{1,0:T(8,128)(2,1)S(1)}, u32[]{:S(2)}, u32[]{:S(2)}) collective-permute-start(bf16[384,2048]{1,0:T(8,128)(2,1)S(1)} %get-tuple-element.25), channel_id=1, source_target_pairs={{0,64},{64,0},{1,65},{65,1},{2,66},{66,2},{3,67},{67,3},{4,68},{68... | collective-permute-start | bytes 4718600 | tf_op jit(solution)/shard_map/ppermute | solution.py:320

commit v6 on v5

--- a/solution.py
+++ b/solution.py
@@ -119,22 +119,32 @@
         start += pieces * tokens
 
 
-def combine_kernel(packed_ref, stream_ref, take_ref, gate_ref, out_ref):
+def combine_kernel(packed_ref, stream_ref, take_ref, gate_ref, out_hbm, out_ref, sems):
     tokens, features = out_ref.shape
     gate = [gate_ref[:, k : k + 1] for k in (0, 1)]
     start = 0
-    total = None
+    taken = []
     for _, _, pieces, wide, columns in kinds(features):
         count = 2 * pieces * tokens
-        rows = dot(take_ref[start : start + count, :], packed_ref[:, columns])
+        taken.append((wide, dot(take_ref[start : start + count, :], packed_ref[:, columns])))
         start += count
-        mixed = []
-        for h in range(pieces):
-            at = 2 * h * tokens
-            mixed.append(gate[0] * rows[at : at + tokens] + gate[1] * rows[at + tokens : at + 2 * tokens])
-        mixed = jnp.concatenate(mixed, axis=1)
-        total = mixed if total is None else total + mixed
-    out_ref[...] = (stream_ref[...].astype(F32) + total).astype(BF16)
+    part = min(wide for wide, _ in taken)
+    copies = []
+    for q in range(features // part):
+        rows = []
+        for k in (0, 1):
+            found = []
+            for wide, values in taken:
+                h, column = q * part // wide, q * part % wide
+                found.append(values[(2 * h + k) * tokens : (2 * h + k + 1) * tokens, column : column + part])
+            rows.append(sum(found[1:], found[0]))
+        at = slice(q * part, (q + 1) * part)
+        mixed = gate[0] * rows[0] + gate[1] * rows[1]
+        out_ref[:, at] = (stream_ref[:, at].astype(F32) + mixed).astype(BF16)
+        copies.append(pltpu.make_async_copy(out_ref.at[:, at], out_hbm.at[:, at], sems.at[q]))
+        copies[-1].start()
+    for copy in copies:
+        copy.wait()
 
 
 def mover(slots, reverse):
@@ -163,6 +173,8 @@
 
 
 def columns_of(i):
+    if isinstance(i, int):
+        return slice(i * TILE, (i + 1) * TILE)
     return pl.ds(pl.multiple_of(i * TILE, TILE), TILE)
 
 
@@ -179,9 +191,7 @@
     start_copies(in_hbm, rest_ref, sems, 1)
     unpack_into(packed_ref, rows_ref)
     hidden_ref[:, :TILE] = jnp.maximum(dot(rows_ref[...], first_ref[...]), 0.0).astype(BF16)
-
-    @pl.loop(0, rest_ref.shape[1] // TILE)
-    def _(i):
+    for i in range(rest_ref.shape[1] // TILE):
         tile_copy(in_hbm, rest_ref, sems, i, 1).wait()
         hidden_ref[:, columns_of(i + 1)] = jnp.maximum(dot(rows_ref[...], rest_ref[:, columns_of(i)]), 0.0).astype(BF16)
 
@@ -190,20 +200,16 @@
     start_copies(out_hbm, out_ref, sems)
     unpack_into(packed_ref, rows_ref)
     hidden_ref[:, :TILE] = jnp.maximum(dot(rows_ref[...], first_ref[...]), 0.0).astype(BF16)
-
-    @pl.loop(0, rest_ref.shape[1] // TILE)
-    def _(i):
+    for i in range(rest_ref.shape[1] // TILE):
         hidden_ref[:, columns_of(i + 1)] = jnp.maximum(dot(rows_ref[...], rest_ref[:, columns_of(i)]), 0.0).astype(BF16)
-
-    @pl.loop(0, out_ref.shape[1] // TILE)
-    def _(i):
+    for i in range(out_ref.shape[1] // TILE):
         tile_copy(out_hbm, out_ref, sems, i).wait()
+    for i in range(out_ref.shape[1] // TILE):
         result_ref[:, columns_of(i)] = dot(hidden_ref[...], out_ref[:, columns_of(i)]).astype(BF16)
 
 
 def result_kernel(hidden_ref, out_ref, result_ref):
-    @pl.loop(0, out_ref.shape[1] // TILE)
-    def _(i):
+    for i in range(out_ref.shape[1] // TILE):
         result_ref[:, columns_of(i)] = dot(hidden_ref[...], out_ref[:, columns_of(i)])
 
 
@@ -237,14 +243,14 @@
     tile_copy(in_hbm, first_ref, first_sem, 0).wait()
 
 
-def call(kernel, flops, out_shape, args, specs=None, scratch=(), limit=LIMIT):
+def call(kernel, flops, out_shape, args, specs=None, out_specs=None, scratch=()):
     return pl.pallas_call(
         kernel,
         in_specs=specs or [VMEM] * len(args),
-        out_specs=jax.tree.map(lambda _: VMEM, out_shape),
+        out_specs=out_specs or jax.tree.map(lambda _: VMEM, out_shape),
         out_shape=out_shape,
         scratch_shapes=scratch,
-        compiler_params=pltpu.CompilerParams(vmem_limit_bytes=limit),
+        compiler_params=pltpu.CompilerParams(vmem_limit_bytes=LIMIT),
         cost_estimate=pl.CostEstimate(
             flops=flops, bytes_accessed=sum(a.size * a.dtype.itemsize for a in args), transcendentals=0
         ),
@@ -321,7 +327,15 @@
     part_own = call(result_kernel, half, shape(*rows_shape.shape, dtype=F32), (hidden, weight_out))
     results = call(add_kernel, moving, packed_shape, (part_own, part_recv))
     returned = exchange(results)
-    return call(combine_kernel, 2 * moving, shape(tokens, features), (returned, stream, take, gates))[None]
+    out_shape = shape(tokens, features)
+    return call(
+        combine_kernel,
+        2 * moving,
+        out_shape,
+        (returned, stream, take, gates),
+        out_specs=HBM,
+        scratch=[vmem(out_shape), pltpu.SemaphoreType.DMA((max(PACK // slots for slots in SPLIT),))],
+    )[None]
 
 
 def solution(mesh):

time: 93.3 us -> 92 us (0.986)
  Pallas kernels: 25.8 us -> 24.1 us
    pallas_call x8, Pallas kernels: 25.8 us -> 24.1 us  [call(): pl.pallas_call(kernel, in_specs=specs or [VMEM] * len(args), out_specs=ou...]
where the time goes in v6:
time: 92 us; the launch traced here: 91.8 us
  blocking collectives  65.8 us (72%)
  Pallas kernels  24.1 us (26%)
    all_to_all x2, blocking collectives, exchange(): lax.all_to_all(blocks, 'ep', split_axis=0, concat_axis=0, tiled=True)  65.8 us
    pallas_call x8, Pallas kernels, call(): pl.pallas_call(kernel, in_specs=specs or [VMEM] * len(args), out_specs=ou...  24.1 us
  transfers between devices with their start and end apart: 3, of which 1 were waited for; matrix products, arithmetic and copies ran while one was open for 0% of the time, Pallas kernels for 10%

profile of v6, /device:TPU:0, one launch (start us, length us, event | category | flops | bytes accessed | tf_op | source)
XLA Modules:
  0.0 91.8 jit_solution(4003731540951144336)
XLA Ops:
  0.0 0.0 copy-start.2
  0.0 0.0 copy-start.3
  0.0 0.0 copy-start.4
  0.0 0.0 copy-start
  0.0 0.0 copy-start.1
  0.0 3.9 %shard_map.91 = (f32[128,2048]{1,0:T(8,128)S(1)}, bf16[128,2048]{1,0:T(8,128)(2,1)S(1)}, bf16[2048,512]{1,0:T(8,128)(2,1)S(1)}) custom-call(s32[1]{0:T(128)} %bitcast.core_ref, bf16[256,1024]{1,0:T(8,128)(2,1)} %bitcast.32, bf16[1024,2048]{1,0:T(8,128)(2,1)} %weight_hbm.1, bf16[2048,2048]{1,0:T(8,128)(2,1)} %bitcast.30), custom_call_target="tpu_custom_call" | custom-call | flops 1073741824 | bytes 13107204 | tf_op jit(solution)/shard_map/pallas_call | solution.py:247
  3.9 0.1 collective-permute-start
  4.0 0.0 copy-done.2
  4.0 0.0 copy-done.3
  4.0 0.0 copy-done.4
  4.1 1.1 %shard_map.92 = (bf16[512,768]{1,0:T(8,128)(2,1)S(1)}, bf16[1536,512]{1,0:T(8,128)(2,1)S(1)}, f32[128,2]{1,0:T(8,128)S(1)}) custom-call(s32[2,128]{1,0:T(2,128)S(1)} %bitcast.27, s32[2,128]{1,0:T(2,128)S(1)} %bitcast.28, f32[2,128]{1,0:T(2,128)S(1)} %bitcast.29), custom_call_target="tpu_custom_call" | custom-call | flops 8388608 | bytes 3072 | tf_op jit(solution)/shard_map/pallas_call | solution.py:247
  5.2 0.8 collective-permute-done.recv_ref
  5.9 0.0 copy-done
  5.9 0.0 copy-done.1
  5.9 1.2 %shard_map.93 = (bf16[128,2048]{1,0:T(8,128)(2,1)S(1)}, bf16[512,1536]{1,0:T(8,128)(2,1)S(1)}) custom-call(f32[128,2048]{1,0:T(8,128)S(1)} %get-tuple-element.17.own_ref, bf16[128,2048]{1,0:T(8,128)(2,1)S(1)} %collective-permute-done.recv_ref, bf16[128,2048]{1,0:T(8,128)(2,1)S(1)} %bitcast.25, f32[1,2048]{1,0:T(1,128)S(1)} %bitcast.26, ...), custom_call_target="tpu_custom_call" | custom-call | flops 536870912 | bytes 2891776 | tf_op jit(solution)/shard_map/pallas_call | solution.py:247
  7.2 36.1 %all_to_all.10 = bf16[64,8,1536]{2,1,0:T(8,128)(2,1)S(1)} all-to-all(bf16[64,8,1536]{2,1,0:T(8,128)(2,1)S(1)} %bitcast.24), channel_id=1, replica_groups=mesh['tp'=2,'ep'=64] {'ep'}, dimensions={0} | all-to-all | bytes 3145728 | tf_op jit(solution)/shard_map/all_to_all | solution.py:311
  43.2 0.0 collective-permute-start.1
  43.2 4.6 %shard_map.94 = (bf16[384,2048]{1,0:T(8,128)(2,1)S(1)}, bf16[2048,1536]{1,0:T(8,128)(2,1)S(1)}) custom-call(bf16[512,1536]{1,0:T(8,128)(2,1)S(1)} %bitcast.23, bf16[2048,512]{1,0:T(8,128)(2,1)S(1)} %get-tuple-element.21.first_ref, bf16[2048,2048]{1,0:T(8,128)(2,1)} %bitcast.31), custom_call_target="tpu_custom_call" | custom-call | flops 3221225472 | bytes 12058624 | tf_op jit(solution)/shard_map/pallas_call | solution.py:247
  47.8 0.0 collective-permute-done.1.packed_ref
  47.8 7.3 %shard_map.95 = (bf16[384,2048]{1,0:T(8,128)(2,1)S(1)}, bf16[2048,2048]{1,0:T(8,128)(2,1)S(1)}) custom-call(bf16[512,1536]{1,0:T(8,128)(2,1)S(1)} %collective-permute-done.1.packed_ref, bf16[2048,512]{1,0:T(8,128)(2,1)S(1)} %get-tuple-element.21.first_ref, bf16[2048,1536]{1,0:T(8,128)(2,1)S(1)} %get-tuple-element.23.rest_ref, bf16[2048,2048]{1,0:T(8,128)(2,1)} %bitcast.33), custom_call_target="tpu_custom_call" | custom-call | flops 6442450944 | bytes 18350080 | tf_op jit(solution)/shard_map/pallas_call | solution.py:247
  55.1 0.8 collective-permute-start.2
  55.9 3.4 %shard_map.96.own_ref = f32[384,2048]{1,0:T(8,128)S(1)} custom-call(bf16[384,2048]{1,0:T(8,128)(2,1)S(1)} %get-tuple-element.22.hidden_ref, bf16[2048,2048]{1,0:T(8,128)(2,1)S(1)} %get-tuple-element.24.out_ref), custom_call_target="tpu_custom_call" | custom-call | flops 3221225472 | bytes 9961472 | tf_op jit(solution)/shard_map/pallas_call | solution.py:247
  59.3 0.0 collective-permute-done.2.recv_ref
  59.3 0.7 shard_map.97
  60.0 29.7 %all_to_all.11 = bf16[64,8,1536]{2,1,0:T(8,128)(2,1)S(1)} all-to-all(bf16[64,8,1536]{2,1,0:T(8,128)(2,1)S(1)} %bitcast.21), channel_id=1, replica_groups=mesh['tp'=2,'ep'=64] {'ep'}, dimensions={0} | all-to-all | bytes 3145728 | tf_op jit(solution)/shard_map/all_to_all | solution.py:311
  89.7 2.0 %shard_map.98 = bf16[128,2048]{1,0:T(8,128)(2,1)} custom-call(bf16[512,1536]{1,0:T(8,128)(2,1)S(1)} %bitcast.20, bf16[128,2048]{1,0:T(8,128)(2,1)S(1)} %get-tuple-element.26.stream_ref, bf16[1536,512]{1,0:T(8,128)(2,1)S(1)} %get-tuple-element.27.take_ref, f32[128,2]{1,0:T(8,128)S(1)} %get-tuple-element.28.gate_ref), custom_call_target="tpu_custom_call" | custom-call | flops 1073741824 | bytes 3671040 | tf_op jit(solution)/shard_map/pallas_call | solution.py:247
Async XLA Ops:
  0.0 4.0 %copy-start.2 = (s32[1,128,2]{1,2,0:T(2,128)S(1)}, s32[1,128,2]{1,2,0:T(2,128)}, u32[]{:S(2)}) copy-start(s32[1,128,2]{1,2,0:T(2,128)} %param.13) | copy-start | bytes 3076
  0.0 4.0 %copy-start.3 = (s32[1,128,2]{1,2,0:T(2,128)S(1)}, s32[1,128,2]{1,2,0:T(2,128)}, u32[]{:S(2)}) copy-start(s32[1,128,2]{1,2,0:T(2,128)} %param.15) | copy-start | bytes 3076
  0.0 4.0 %copy-start.4 = (f32[1,128,2]{1,2,0:T(2,128)S(1)}, f32[1,128,2]{1,2,0:T(2,128)}, u32[]{:S(2)}) copy-start(f32[1,128,2]{1,2,0:T(2,128)} %param.14) | copy-start | bytes 3076
  0.0 5.9 %copy-start = (bf16[1,128,2048]{2,1,0:T(8,128)(2,1)S(1)}, bf16[1,128,2048]{2,1,0:T(8,128)(2,1)}, u32[]{:S(2)}) copy-start(bf16[1,128,2048]{2,1,0:T(8,128)(2,1)} %param.11) | copy-start | bytes 1572868
  0.0 5.9 %copy-start.1 = (f32[2048]{0:T(1024)S(1)}, f32[2048]{0:T(1024)}, u32[]{:S(2)}) copy-start(f32[2048]{0:T(1024)} %param.12) | copy-start | bytes 24580
  3.9 2.0 %collective-permute-start = (bf16[128,2048]{1,0:T(8,128)(2,1)S(1)}, bf16[128,2048]{1,0:T(8,128)(2,1)S(1)}, u32[]{:S(2)}, u32[]{:S(2)}) collective-permute-start(bf16[128,2048]{1,0:T(8,128)(2,1)S(1)} %get-tuple-element.18), channel_id=1, source_target_pairs={{0,64},{64,0},{1,65},{65,1},{2,66},{66,2},{3,67},{67,3},{4,68},{68... | collective-permute-start | bytes 1572872 | tf_op jit(solution)/shard_map/ppermute | solution.py:290
  43.2 4.6 %collective-permute-start.1 = (bf16[512,1536]{1,0:T(8,128)(2,1)S(1)}, bf16[512,1536]{1,0:T(8,128)(2,1)S(1)}, u32[]{:S(2)}, u32[]{:S(2)}) collective-permute-start(bf16[512,1536]{1,0:T(8,128)(2,1)S(1)} %bitcast.22), channel_id=1, source_target_pairs={{0,64},{64,0},{1,65},{65,1},{2,66},{66,2},{3,67},{67,3},{4,68},{68... | collective-permute-start | bytes 4718600 | tf_op jit(solution)/shard_map/ppermute | solution.py:314
  55.1 4.2 %collective-permute-start.2 = (bf16[384,2048]{1,0:T(8,128)(2,1)S(1)}, bf16[384,2048]{1,0:T(8,128)(2,1)S(1)}, u32[]{:S(2)}, u32[]{:S(2)}) collective-permute-start(bf16[384,2048]{1,0:T(8,128)(2,1)S(1)} %get-tuple-element.25), channel_id=1, source_target_pairs={{0,64},{64,0},{1,65},{65,1},{2,66},{66,2},{3,67},{67,3},{4,68},{68... | collective-permute-start | bytes 4718600 | tf_op jit(solution)/shard_map/ppermute | solution.py:326

commit v7 on v6

--- a/solution.py
+++ b/solution.py
@@ -173,44 +173,35 @@
 
 
 def columns_of(i):
-    if isinstance(i, int):
-        return slice(i * TILE, (i + 1) * TILE)
-    return pl.ds(pl.multiple_of(i * TILE, TILE), TILE)
-
-
-def tile_copy(hbm_ref, vmem_ref, sems, i, skip=0):
-    return pltpu.make_async_copy(hbm_ref.at[:, columns_of(i + skip)], vmem_ref.at[:, columns_of(i)], sems.at[i])
-
-
-def start_copies(hbm_ref, vmem_ref, sems, skip=0):
+    return slice(i * TILE, (i + 1) * TILE)
+
+
+def tile_copy(hbm_ref, vmem_ref, sems, i):
+    return pltpu.make_async_copy(hbm_ref.at[:, columns_of(i)], vmem_ref.at[:, columns_of(i)], sems.at[i])
+
+
+def start_copies(hbm_ref, vmem_ref, sems):
     for i in range(vmem_ref.shape[1] // TILE):
-        tile_copy(hbm_ref, vmem_ref, sems, i, skip).start()
-
-
-def hidden_kernel(packed_ref, first_ref, in_hbm, hidden_ref, rest_ref, rows_ref, sems):
-    start_copies(in_hbm, rest_ref, sems, 1)
+        tile_copy(hbm_ref, vmem_ref, sems, i).start()
+
+
+def hidden_kernel(packed_ref, in_ref, hidden_ref, rows_ref):
     unpack_into(packed_ref, rows_ref)
-    hidden_ref[:, :TILE] = jnp.maximum(dot(rows_ref[...], first_ref[...]), 0.0).astype(BF16)
-    for i in range(rest_ref.shape[1] // TILE):
-        tile_copy(in_hbm, rest_ref, sems, i, 1).wait()
-        hidden_ref[:, columns_of(i + 1)] = jnp.maximum(dot(rows_ref[...], rest_ref[:, columns_of(i)]), 0.0).astype(BF16)
-
-
-def both_kernel(packed_ref, first_ref, rest_ref, out_hbm, result_ref, out_ref, rows_ref, hidden_ref, sems):
+    for i in range(in_ref.shape[1] // TILE):
+        hidden_ref[:, columns_of(i)] = jnp.maximum(dot(rows_ref[...], in_ref[:, columns_of(i)]), 0.0).astype(BF16)
+
+
+def both_kernel(packed_ref, in_ref, out_hbm, result_ref, out_ref, rows_ref, hidden_ref, sems):
     start_copies(out_hbm, out_ref, sems)
-    unpack_into(packed_ref, rows_ref)
-    hidden_ref[:, :TILE] = jnp.maximum(dot(rows_ref[...], first_ref[...]), 0.0).astype(BF16)
-    for i in range(rest_ref.shape[1] // TILE):
-        hidden_ref[:, columns_of(i + 1)] = jnp.maximum(dot(rows_ref[...], rest_ref[:, columns_of(i)]), 0.0).astype(BF16)
+    hidden_kernel(packed_ref, in_ref, hidden_ref, rows_ref)
     for i in range(out_ref.shape[1] // TILE):
         tile_copy(out_hbm, out_ref, sems, i).wait()
-    for i in range(out_ref.shape[1] // TILE):
-        result_ref[:, columns_of(i)] = dot(hidden_ref[...], out_ref[:, columns_of(i)]).astype(BF16)
+    result_kernel(hidden_ref, out_ref, result_ref)
 
 
 def result_kernel(hidden_ref, out_ref, result_ref):
     for i in range(out_ref.shape[1] // TILE):
-        result_ref[:, columns_of(i)] = dot(hidden_ref[...], out_ref[:, columns_of(i)])
+        result_ref[:, columns_of(i)] = dot(hidden_ref[...], out_ref[:, columns_of(i)]).astype(result_ref.dtype)
 
 
 def add_kernel(own_ref, recv_ref, packed_ref):
@@ -221,36 +212,29 @@
         packed_ref[at, columns] = dot(movers[kind], stack_pieces(block, pieces, wide)).astype(BF16)
 
 
-def project_kernel(
-    core_ref, context_hbm, weight_hbm, in_hbm, own_ref, other_ref, first_ref, context_ref, weight_ref, sem, sems, first_sem
-):
+def project_kernel(core_ref, context_hbm, weight_hbm, own_ref, other_ref, context_ref, weight_ref, sem, sems):
     load = pltpu.make_async_copy(context_hbm, context_ref, sem)
     load.start()
     start_copies(weight_hbm, weight_ref, sems)
-    start_copies(in_hbm, first_ref, first_sem)
     load.wait()
     tokens = own_ref.shape[0]
     first = core_ref[0] == 0
-
-    @pl.loop(0, weight_ref.shape[1] // TILE)
-    def _(i):
+    for i in range(weight_ref.shape[1] // TILE):
         tile_copy(weight_hbm, weight_ref, sems, i).wait()
         at = columns_of(i)
         both = dot(context_ref[...], weight_ref[:, at])
         own_ref[:, at] = jnp.where(first, both[:tokens], both[tokens:])
         other_ref[:, at] = jnp.where(first, both[tokens:], both[:tokens]).astype(BF16)
 
-    tile_copy(in_hbm, first_ref, first_sem, 0).wait()
-
-
-def call(kernel, flops, out_shape, args, specs=None, out_specs=None, scratch=()):
+
+def call(kernel, flops, out_shape, args, specs=None, out_specs=None, scratch=(), limit=LIMIT):
     return pl.pallas_call(
         kernel,
         in_specs=specs or [VMEM] * len(args),
         out_specs=out_specs or jax.tree.map(lambda _: VMEM, out_shape),
         out_shape=out_shape,
         scratch_shapes=scratch,
-        compiler_params=pltpu.CompilerParams(vmem_limit_bytes=LIMIT),
+        compiler_params=pltpu.CompilerParams(vmem_limit_bytes=limit),
         cost_estimate=pl.CostEstimate(
             flops=flops, bytes_accessed=sum(a.size * a.dtype.itemsize for a in args), transcendentals=0
         ),
@@ -278,14 +262,15 @@
         return pltpu.with_memory_space_constraint(a, pltpu.HBM)
 
     context, out_weight = in_hbm(context[0]), in_hbm(out_weight)
-    weight_in, weight_out = in_hbm(expert_in[0]), in_hbm(expert_out[0])
-    own, other, in_first = call(
+    weight_in, weight_out = expert_in[0], in_hbm(expert_out[0])
+    own, other = call(
         project_kernel,
         2 * context.size * features,
-        [shape(tokens, features, dtype=F32), shape(tokens, features), pltpu.VMEM((features, TILE), BF16)],
-        (lax.axis_index("tp")[None], context, out_weight, weight_in),
-        specs=[SMEM, HBM, HBM, HBM],
-        scratch=[vmem(context), vmem(out_weight), pltpu.SemaphoreType.DMA(()), sems(features), sems(TILE)],
+        [pltpu.VMEM((tokens, features), F32), pltpu.VMEM((tokens, features), BF16)],
+        (lax.axis_index("tp")[None], context, out_weight),
+        specs=[SMEM, HBM, HBM],
+        scratch=[vmem(context), vmem(out_weight), pltpu.SemaphoreType.DMA(()), sems(features)],
+        limit=60 << 20,
     )
     recv = lax.ppermute(other, "tp", SWAP)
     size = experts * PACK
@@ -301,7 +286,7 @@
     moving = 4 * tokens * experts * PACK * features
     stream, outgoing = call(
         pack_kernel,
-        moving,
+        8 * moving,
         [shape(tokens, features), packed_shape],
         (own, recv, residual_in[0], norm_gain[None, :], send),
     )
@@ -314,14 +299,10 @@
     rows_other = lax.ppermute(rows, "tp", SWAP)
     half = 2 * experts * SLOT * features * units
     row_buffer, hidden_shape = vmem(rows_shape), shape(experts * SLOT, units)
-    hidden, in_rest = call(
-        hidden_kernel, half, [hidden_shape, pltpu.VMEM((features, units - TILE), BF16)],
-        (rows, in_first, weight_in), specs=[VMEM, VMEM, HBM], scratch=[row_buffer, sems(units - TILE)],
-    )
+    hidden = call(hidden_kernel, half, hidden_shape, (rows, weight_in), scratch=[row_buffer])
     part_other, weight_out = call(
-        both_kernel, 2 * half, [rows_shape, vmem(weight_out)],
-        (rows_other, in_first, in_rest, weight_out), specs=[VMEM, VMEM, VMEM, HBM],
-        scratch=[row_buffer, vmem(hidden_shape), sems(features)],
+        both_kernel, 2 * half, [rows_shape, vmem(weight_out)], (rows_other, weight_in, weight_out),
+        specs=[VMEM, VMEM, HBM], scratch=[row_buffer, vmem(hidden_shape), sems(features)],
     )
     part_recv = lax.ppermute(part_other, "tp", SWAP)
     part_own = call(result_kernel, half, shape(*rows_shape.shape, dtype=F32), (hidden, weight_out))

time: 92 us -> 94.8 us (1.030)
  waiting for transfers between devices: 0.76 us -> 4.16 us
    ppermute x1, waiting for transfers between devices: 0.01 us -> 3.41 us  [body(): rows_other = lax.ppermute(rows, 'tp', SWAP)]
  transfers between devices with their start and end apart: 3 -> 3, of which waited for: 1 -> 2; matrix products, arithmetic and copies ran while one was open for 0% -> 0% of each run, Pallas kernels for 10% -> 9%
where the time goes in v7:
time: 94.8 us; the launch traced here: 94.7 us
  blocking collectives  66.4 us (70%)
  Pallas kernels  23.3 us (25%)
  waiting for transfers between devices  4.16 us (4%)
    all_to_all x2, blocking collectives, exchange(): lax.all_to_all(blocks, 'ep', split_axis=0, concat_axis=0, tiled=True)  66.4 us
    pallas_call x8, Pallas kernels, call(): pl.pallas_call(kernel, in_specs=specs or [VMEM] * len(args), out_specs=ou...  23.3 us
    ppermute x1, waiting for transfers between devices, body(): rows_other = lax.ppermute(rows, 'tp', SWAP)  3.41 us
  transfers between devices with their start and end apart: 3, of which 2 were waited for; matrix products, arithmetic and copies ran while one was open for 0% of the time, Pallas kernels for 9%

profile of v7, /device:TPU:0, one launch (start us, length us, event | category | flops | bytes accessed | tf_op | source)
XLA Modules:
  0.0 94.7 jit_solution(9346945339526263095)
XLA Ops:
  0.0 0.0 copy-start.3
  0.0 0.0 copy-start.4
  0.0 0.0 copy-start.5
  0.0 0.0 copy-start.1
  0.0 0.0 copy-start.2
  0.0 3.9 %shard_map.91 = (f32[128,2048]{1,0:T(8,128)S(1)}, bf16[128,2048]{1,0:T(8,128)(2,1)S(1)}) custom-call(s32[1]{0:T(128)} %bitcast.core_ref, bf16[256,1024]{1,0:T(8,128)(2,1)} %bitcast.32, bf16[1024,2048]{1,0:T(8,128)(2,1)} %weight_hbm.1), custom_call_target="tpu_custom_call" | custom-call | flops 1073741824 | bytes 4718596 | tf_op jit(solution)/shard_map/pallas_call | solution.py:231
  3.9 0.1 collective-permute-start
  4.0 0.0 copy-done.3
  4.0 0.0 copy-done.4
  4.0 0.0 copy-done.5
  4.0 1.1 %shard_map.92 = (bf16[512,768]{1,0:T(8,128)(2,1)S(1)}, bf16[1536,512]{1,0:T(8,128)(2,1)S(1)}, f32[128,2]{1,0:T(8,128)S(1)}) custom-call(s32[2,128]{1,0:T(2,128)S(1)} %bitcast.29, s32[2,128]{1,0:T(2,128)S(1)} %bitcast.30, f32[2,128]{1,0:T(2,128)S(1)} %bitcast.31), custom_call_target="tpu_custom_call" | custom-call | flops 8388608 | bytes 3072 | tf_op jit(solution)/shard_map/pallas_call | solution.py:231
  5.1 0.8 collective-permute-done.recv_ref
  5.9 0.0 copy-done.1
  5.9 0.0 copy-done.2
  5.9 0.0 copy-start
  5.9 1.2 %shard_map.93 = (bf16[128,2048]{1,0:T(8,128)(2,1)S(1)}, bf16[512,1536]{1,0:T(8,128)(2,1)S(1)}) custom-call(f32[128,2048]{1,0:T(8,128)S(1)} %get-tuple-element.14.own_ref, bf16[128,2048]{1,0:T(8,128)(2,1)S(1)} %collective-permute-done.recv_ref, bf16[128,2048]{1,0:T(8,128)(2,1)S(1)} %bitcast.27, f32[1,2048]{1,0:T(1,128)S(1)} %bitcast.28, ...), custom_call_target="tpu_custom_call" | custom-call | flops 4294967296 | bytes 2891776 | tf_op jit(solution)/shard_map/pallas_call | solution.py:231
  7.1 36.3 %all_to_all.10 = bf16[64,8,1536]{2,1,0:T(8,128)(2,1)S(1)} all-to-all(bf16[64,8,1536]{2,1,0:T(8,128)(2,1)S(1)} %bitcast.24), channel_id=1, replica_groups=mesh['tp'=2,'ep'=64] {'ep'}, dimensions={0} | all-to-all | bytes 3145728 | tf_op jit(solution)/shard_map/all_to_all | solution.py:296
  43.5 0.0 collective-permute-start.1
  43.5 3.4 %collective-permute-done.1.packed_ref = bf16[512,1536]{1,0:T(8,128)(2,1)S(1)} collective-permute-done((bf16[512,1536]{1,0:T(8,128)(2,1)S(1)}, bf16[512,1536]{1,0:T(8,128)(2,1)S(1)}, u32[]{:S(2)}, u32[]{:S(2)}) %collective-permute-start.1) | collective-permute-done | bytes 1572896 | tf_op jit(solution)/shard_map/ppermute | solution.py:299
  46.9 0.0 copy-done
  46.9 7.3 %shard_map.95 = (bf16[384,2048]{1,0:T(8,128)(2,1)S(1)}, bf16[2048,2048]{1,0:T(8,128)(2,1)S(1)}) custom-call(bf16[512,1536]{1,0:T(8,128)(2,1)S(1)} %collective-permute-done.1.packed_ref, bf16[2048,2048]{1,0:T(8,128)(2,1)S(1)} %bitcast.25, bf16[2048,2048]{1,0:T(8,128)(2,1)} %bitcast.33), custom_call_target="tpu_custom_call" | custom-call | flops 6442450944 | bytes 18350080 | tf_op jit(solution)/shard_map/pallas_call | solution.py:231
  54.2 0.4 collective-permute-start.2
  54.6 3.8 %shard_map.94.hidden_ref = bf16[384,2048]{1,0:T(8,128)(2,1)S(1)} custom-call(bf16[512,1536]{1,0:T(8,128)(2,1)S(1)} %bitcast.23, bf16[2048,2048]{1,0:T(8,128)(2,1)S(1)} %bitcast.26), custom_call_target="tpu_custom_call" | custom-call | flops 3221225472 | bytes 9961472 | tf_op jit(solution)/shard_map/pallas_call | solution.py:231
  58.4 3.4 %shard_map.96.own_ref = f32[384,2048]{1,0:T(8,128)S(1)} custom-call(bf16[384,2048]{1,0:T(8,128)(2,1)S(1)} %shard_map.94.hidden_ref, bf16[2048,2048]{1,0:T(8,128)(2,1)S(1)} %get-tuple-element.18.out_ref), custom_call_target="tpu_custom_call" | custom-call | flops 3221225472 | bytes 9961472 | tf_op jit(solution)/shard_map/pallas_call | solution.py:231
  61.8 0.0 collective-permute-done.2.recv_ref
  61.8 0.7 shard_map.97
  62.5 30.1 %all_to_all.11 = bf16[64,8,1536]{2,1,0:T(8,128)(2,1)S(1)} all-to-all(bf16[64,8,1536]{2,1,0:T(8,128)(2,1)S(1)} %bitcast.21), channel_id=1, replica_groups=mesh['tp'=2,'ep'=64] {'ep'}, dimensions={0} | all-to-all | bytes 3145728 | tf_op jit(solution)/shard_map/all_to_all | solution.py:296
  92.5 2.0 %shard_map.98 = bf16[128,2048]{1,0:T(8,128)(2,1)} custom-call(bf16[512,1536]{1,0:T(8,128)(2,1)S(1)} %bitcast.20, bf16[128,2048]{1,0:T(8,128)(2,1)S(1)} %get-tuple-element.20.stream_ref, bf16[1536,512]{1,0:T(8,128)(2,1)S(1)} %get-tuple-element.21.take_ref, f32[128,2]{1,0:T(8,128)S(1)} %get-tuple-element.22.gate_ref), custom_call_target="tpu_custom_call" | custom-call | flops 1073741824 | bytes 3671040 | tf_op jit(solution)/shard_map/pallas_call | solution.py:231
Async XLA Ops:
  0.0 4.0 %copy-start.3 = (s32[1,128,2]{1,2,0:T(2,128)S(1)}, s32[1,128,2]{1,2,0:T(2,128)}, u32[]{:S(2)}) copy-start(s32[1,128,2]{1,2,0:T(2,128)} %param.13) | copy-start | bytes 3076
  0.0 4.0 %copy-start.4 = (s32[1,128,2]{1,2,0:T(2,128)S(1)}, s32[1,128,2]{1,2,0:T(2,128)}, u32[]{:S(2)}) copy-start(s32[1,128,2]{1,2,0:T(2,128)} %param.15) | copy-start | bytes 3076
  0.0 4.0 %copy-start.5 = (f32[1,128,2]{1,2,0:T(2,128)S(1)}, f32[1,128,2]{1,2,0:T(2,128)}, u32[]{:S(2)}) copy-start(f32[1,128,2]{1,2,0:T(2,128)} %param.14) | copy-start | bytes 3076
  0.0 5.9 %copy-start.1 = (bf16[1,128,2048]{2,1,0:T(8,128)(2,1)S(1)}, bf16[1,128,2048]{2,1,0:T(8,128)(2,1)}, u32[]{:S(2)}) copy-start(bf16[1,128,2048]{2,1,0:T(8,128)(2,1)} %param.11) | copy-start | bytes 1572868
  0.0 5.9 %copy-start.2 = (f32[2048]{0:T(1024)S(1)}, f32[2048]{0:T(1024)}, u32[]{:S(2)}) copy-start(f32[2048]{0:T(1024)} %param.12) | copy-start | bytes 24580
  3.9 2.0 %collective-permute-start = (bf16[128,2048]{1,0:T(8,128)(2,1)S(1)}, bf16[128,2048]{1,0:T(8,128)(2,1)S(1)}, u32[]{:S(2)}, u32[]{:S(2)}) collective-permute-start(bf16[128,2048]{1,0:T(8,128)(2,1)S(1)} %get-tuple-element.15), channel_id=1, source_target_pairs={{0,64},{64,0},{1,65},{65,1},{2,66},{66,2},{3,67},{67,3},{4,68},{68... | collective-permute-start | bytes 1572872 | tf_op jit(solution)/shard_map/ppermute | solution.py:275
  5.9 41.0 %copy-start = (bf16[1,2048,2048]{2,1,0:T(8,128)(2,1)S(1)}, bf16[1,2048,2048]{2,1,0:T(8,128)(2,1)}, u32[]{:S(2)}) copy-start(bf16[1,2048,2048]{2,1,0:T(8,128)(2,1)} %param.16) | copy-start | bytes 25165828
  43.5 3.4 %collective-permute-start.1 = (bf16[512,1536]{1,0:T(8,128)(2,1)S(1)}, bf16[512,1536]{1,0:T(8,128)(2,1)S(1)}, u32[]{:S(2)}, u32[]{:S(2)}) collective-permute-start(bf16[512,1536]{1,0:T(8,128)(2,1)S(1)} %bitcast.22), channel_id=1, source_target_pairs={{0,64},{64,0},{1,65},{65,1},{2,66},{66,2},{3,67},{67,3},{4,68},{68... | collective-permute-start | bytes 4718600 | tf_op jit(solution)/shard_map/ppermute | solution.py:299
  54.2 7.6 %collective-permute-start.2 = (bf16[384,2048]{1,0:T(8,128)(2,1)S(1)}, bf16[384,2048]{1,0:T(8,128)(2,1)S(1)}, u32[]{:S(2)}, u32[]{:S(2)}) collective-permute-start(bf16[384,2048]{1,0:T(8,128)(2,1)S(1)} %get-tuple-element.19), channel_id=1, source_target_pairs={{0,64},{64,0},{1,65},{65,1},{2,66},{66,2},{3,67},{67,3},{4,68},{68... | collective-permute-start | bytes 4718600 | tf_op jit(solution)/shard_map/ppermute | solution.py:307

commit v8 on v7

--- a/solution.py
+++ b/solution.py
@@ -111,7 +111,7 @@
     tokens, features = value.shape
     centred = value - jnp.sum(value, axis=1, keepdims=True) / features
     variance = jnp.sum(centred * centred, axis=1, keepdims=True) / features
-    normed = (centred / jnp.sqrt(variance + 1e-05) * gain_ref[...]).astype(BF16)
+    normed = (centred * (1.0 / jnp.sqrt(variance + 1e-05)) * gain_ref[...]).astype(BF16)
     start = 0
     for _, _, pieces, wide, columns in kinds(features):
         send = send_ref[:, start : start + pieces * tokens]
@@ -212,16 +212,25 @@
         packed_ref[at, columns] = dot(movers[kind], stack_pieces(block, pieces, wide)).astype(BF16)
 
 
+def project_tiles(width):
+    edges = [*range(0, width, TILE), width - TILE // 2, width]
+    return [slice(a, b) for a, b in zip(edges, edges[1:])]
+
+
 def project_kernel(core_ref, context_hbm, weight_hbm, own_ref, other_ref, context_ref, weight_ref, sem, sems):
     load = pltpu.make_async_copy(context_hbm, context_ref, sem)
     load.start()
-    start_copies(weight_hbm, weight_ref, sems)
+    tiles = project_tiles(weight_ref.shape[1])
+    copies = [
+        pltpu.make_async_copy(weight_hbm.at[:, at], weight_ref.at[:, at], sems.at[i]) for i, at in enumerate(tiles)
+    ]
+    for copy in copies:
+        copy.start()
     load.wait()
     tokens = own_ref.shape[0]
     first = core_ref[0] == 0
-    for i in range(weight_ref.shape[1] // TILE):
-        tile_copy(weight_hbm, weight_ref, sems, i).wait()
-        at = columns_of(i)
+    for copy, at in zip(copies, tiles):
+        copy.wait()
         both = dot(context_ref[...], weight_ref[:, at])
         own_ref[:, at] = jnp.where(first, both[:tokens], both[tokens:])
         other_ref[:, at] = jnp.where(first, both[tokens:], both[:tokens]).astype(BF16)
@@ -269,7 +278,7 @@
         [pltpu.VMEM((tokens, features), F32), pltpu.VMEM((tokens, features), BF16)],
         (lax.axis_index("tp")[None], context, out_weight),
         specs=[SMEM, HBM, HBM],
-        scratch=[vmem(context), vmem(out_weight), pltpu.SemaphoreType.DMA(()), sems(features)],
+        scratch=[vmem(context), vmem(out_weight), pltpu.SemaphoreType.DMA(()), sems(features + TILE)],
         limit=60 << 20,
     )
     recv = lax.ppermute(other, "tp", SWAP)

time: 94.8 us -> 95.4 us (level)
  no operation moved by 1% of the time
where the time goes in v8:
time: 95.4 us; the launch traced here: 95.2 us
  blocking collectives  66.4 us (70%)
  Pallas kernels  23.9 us (25%)
  waiting for transfers between devices  4.16 us (4%)
    all_to_all x2, blocking collectives, exchange(): lax.all_to_all(blocks, 'ep', split_axis=0, concat_axis=0, tiled=True)  66.4 us
    pallas_call x8, Pallas kernels, call(): pl.pallas_call(kernel, in_specs=specs or [VMEM] * len(args), out_specs=ou...  23.9 us
    ppermute x1, waiting for transfers between devices, body(): rows_other = lax.ppermute(rows, 'tp', SWAP)  3.41 us
  transfers between devices with their start and end apart: 3, of which 2 were waited for; matrix products, arithmetic and copies ran while one was open for 0% of the time, Pallas kernels for 9%

profile of v8, /device:TPU:0, one launch (start us, length us, event | category | flops | bytes accessed | tf_op | source)
XLA Modules:
  0.0 95.2 jit_solution(896432911872276216)
XLA Ops:
  0.0 0.0 copy-start.3
  0.0 0.0 copy-start.4
  0.0 0.0 copy-start.5
  0.0 0.0 copy-start.1
  0.0 0.0 copy-start.2
  0.0 4.5 %shard_map.91 = (f32[128,2048]{1,0:T(8,128)S(1)}, bf16[128,2048]{1,0:T(8,128)(2,1)S(1)}) custom-call(s32[1]{0:T(128)} %bitcast.core_ref, bf16[256,1024]{1,0:T(8,128)(2,1)} %bitcast.32, bf16[1024,2048]{1,0:T(8,128)(2,1)} %weight_hbm.1), custom_call_target="tpu_custom_call" | custom-call | flops 1073741824 | bytes 4718596 | tf_op jit(solution)/shard_map/pallas_call | solution.py:240
  4.5 0.1 collective-permute-start
  4.6 0.0 copy-done.3
  4.6 0.0 copy-done.4
  4.6 0.0 copy-done.5
  4.6 1.1 %shard_map.92 = (bf16[512,768]{1,0:T(8,128)(2,1)S(1)}, bf16[1536,512]{1,0:T(8,128)(2,1)S(1)}, f32[128,2]{1,0:T(8,128)S(1)}) custom-call(s32[2,128]{1,0:T(2,128)S(1)} %bitcast.29, s32[2,128]{1,0:T(2,128)S(1)} %bitcast.30, f32[2,128]{1,0:T(2,128)S(1)} %bitcast.31), custom_call_target="tpu_custom_call" | custom-call | flops 8388608 | bytes 3072 | tf_op jit(solution)/shard_map/pallas_call | solution.py:240
  5.7 0.8 collective-permute-done.recv_ref
  6.5 0.0 copy-done.1
  6.5 0.0 copy-done.2
  6.5 0.0 copy-start
  6.5 1.2 %shard_map.93 = (bf16[128,2048]{1,0:T(8,128)(2,1)S(1)}, bf16[512,1536]{1,0:T(8,128)(2,1)S(1)}) custom-call(f32[128,2048]{1,0:T(8,128)S(1)} %get-tuple-element.14.own_ref, bf16[128,2048]{1,0:T(8,128)(2,1)S(1)} %collective-permute-done.recv_ref, bf16[128,2048]{1,0:T(8,128)(2,1)S(1)} %bitcast.27, f32[1,2048]{1,0:T(1,128)S(1)} %bitcast.28, ...), custom_call_target="tpu_custom_call" | custom-call | flops 4294967296 | bytes 2891776 | tf_op jit(solution)/shard_map/pallas_call | solution.py:240
  7.7 36.3 %all_to_all.10 = bf16[64,8,1536]{2,1,0:T(8,128)(2,1)S(1)} all-to-all(bf16[64,8,1536]{2,1,0:T(8,128)(2,1)S(1)} %bitcast.24), channel_id=1, replica_groups=mesh['tp'=2,'ep'=64] {'ep'}, dimensions={0} | all-to-all | bytes 3145728 | tf_op jit(solution)/shard_map/all_to_all | solution.py:305
  44.0 0.0 collective-permute-start.1
  44.0 3.4 %collective-permute-done.1.packed_ref = bf16[512,1536]{1,0:T(8,128)(2,1)S(1)} collective-permute-done((bf16[512,1536]{1,0:T(8,128)(2,1)S(1)}, bf16[512,1536]{1,0:T(8,128)(2,1)S(1)}, u32[]{:S(2)}, u32[]{:S(2)}) %collective-permute-start.1) | collective-permute-done | bytes 1572896 | tf_op jit(solution)/shard_map/ppermute | solution.py:308
  47.5 0.0 copy-done
  47.5 7.3 %shard_map.95 = (bf16[384,2048]{1,0:T(8,128)(2,1)S(1)}, bf16[2048,2048]{1,0:T(8,128)(2,1)S(1)}) custom-call(bf16[512,1536]{1,0:T(8,128)(2,1)S(1)} %collective-permute-done.1.packed_ref, bf16[2048,2048]{1,0:T(8,128)(2,1)S(1)} %bitcast.25, bf16[2048,2048]{1,0:T(8,128)(2,1)} %bitcast.33), custom_call_target="tpu_custom_call" | custom-call | flops 6442450944 | bytes 18350080 | tf_op jit(solution)/shard_map/pallas_call | solution.py:240
  54.7 0.4 collective-permute-start.2
  55.1 3.8 %shard_map.94.hidden_ref = bf16[384,2048]{1,0:T(8,128)(2,1)S(1)} custom-call(bf16[512,1536]{1,0:T(8,128)(2,1)S(1)} %bitcast.23, bf16[2048,2048]{1,0:T(8,128)(2,1)S(1)} %bitcast.26), custom_call_target="tpu_custom_call" | custom-call | flops 3221225472 | bytes 9961472 | tf_op jit(solution)/shard_map/pallas_call | solution.py:240
  59.0 3.4 %shard_map.96.own_ref = f32[384,2048]{1,0:T(8,128)S(1)} custom-call(bf16[384,2048]{1,0:T(8,128)(2,1)S(1)} %shard_map.94.hidden_ref, bf16[2048,2048]{1,0:T(8,128)(2,1)S(1)} %get-tuple-element.18.out_ref), custom_call_target="tpu_custom_call" | custom-call | flops 3221225472 | bytes 9961472 | tf_op jit(solution)/shard_map/pallas_call | solution.py:240
  62.4 0.0 collective-permute-done.2.recv_ref
  62.4 0.7 shard_map.97
  63.0 30.1 %all_to_all.11 = bf16[64,8,1536]{2,1,0:T(8,128)(2,1)S(1)} all-to-all(bf16[64,8,1536]{2,1,0:T(8,128)(2,1)S(1)} %bitcast.21), channel_id=1, replica_groups=mesh['tp'=2,'ep'=64] {'ep'}, dimensions={0} | all-to-all | bytes 3145728 | tf_op jit(solution)/shard_map/all_to_all | solution.py:305
  93.1 2.0 %shard_map.98 = bf16[128,2048]{1,0:T(8,128)(2,1)} custom-call(bf16[512,1536]{1,0:T(8,128)(2,1)S(1)} %bitcast.20, bf16[128,2048]{1,0:T(8,128)(2,1)S(1)} %get-tuple-element.20.stream_ref, bf16[1536,512]{1,0:T(8,128)(2,1)S(1)} %get-tuple-element.21.take_ref, f32[128,2]{1,0:T(8,128)S(1)} %get-tuple-element.22.gate_ref), custom_call_target="tpu_custom_call" | custom-call | flops 1073741824 | bytes 3671040 | tf_op jit(solution)/shard_map/pallas_call | solution.py:240
Async XLA Ops:
  0.0 4.6 %copy-start.3 = (s32[1,128,2]{1,2,0:T(2,128)S(1)}, s32[1,128,2]{1,2,0:T(2,128)}, u32[]{:S(2)}) copy-start(s32[1,128,2]{1,2,0:T(2,128)} %param.13) | copy-start | bytes 3076
  0.0 4.6 %copy-start.4 = (s32[1,128,2]{1,2,0:T(2,128)S(1)}, s32[1,128,2]{1,2,0:T(2,128)}, u32[]{:S(2)}) copy-start(s32[1,128,2]{1,2,0:T(2,128)} %param.15) | copy-start | bytes 3076
  0.0 4.6 %copy-start.5 = (f32[1,128,2]{1,2,0:T(2,128)S(1)}, f32[1,128,2]{1,2,0:T(2,128)}, u32[]{:S(2)}) copy-start(f32[1,128,2]{1,2,0:T(2,128)} %param.14) | copy-start | bytes 3076
  0.0 6.5 %copy-start.1 = (bf16[1,128,2048]{2,1,0:T(8,128)(2,1)S(1)}, bf16[1,128,2048]{2,1,0:T(8,128)(2,1)}, u32[]{:S(2)}) copy-start(bf16[1,128,2048]{2,1,0:T(8,128)(2,1)} %param.11) | copy-start | bytes 1572868
  0.0 6.5 %copy-start.2 = (f32[2048]{0:T(1024)S(1)}, f32[2048]{0:T(1024)}, u32[]{:S(2)}) copy-start(f32[2048]{0:T(1024)} %param.12) | copy-start | bytes 24580
  4.5 2.0 %collective-permute-start = (bf16[128,2048]{1,0:T(8,128)(2,1)S(1)}, bf16[128,2048]{1,0:T(8,128)(2,1)S(1)}, u32[]{:S(2)}, u32[]{:S(2)}) collective-permute-start(bf16[128,2048]{1,0:T(8,128)(2,1)S(1)} %get-tuple-element.15), channel_id=1, source_target_pairs={{0,64},{64,0},{1,65},{65,1},{2,66},{66,2},{3,67},{67,3},{4,68},{68... | collective-permute-start | bytes 1572872 | tf_op jit(solution)/shard_map/ppermute | solution.py:284
  6.5 41.0 %copy-start = (bf16[1,2048,2048]{2,1,0:T(8,128)(2,1)S(1)}, bf16[1,2048,2048]{2,1,0:T(8,128)(2,1)}, u32[]{:S(2)}) copy-start(bf16[1,2048,2048]{2,1,0:T(8,128)(2,1)} %param.16) | copy-start | bytes 25165828
  44.0 3.4 %collective-permute-start.1 = (bf16[512,1536]{1,0:T(8,128)(2,1)S(1)}, bf16[512,1536]{1,0:T(8,128)(2,1)S(1)}, u32[]{:S(2)}, u32[]{:S(2)}) collective-permute-start(bf16[512,1536]{1,0:T(8,128)(2,1)S(1)} %bitcast.22), channel_id=1, source_target_pairs={{0,64},{64,0},{1,65},{65,1},{2,66},{66,2},{3,67},{67,3},{4,68},{68... | collective-permute-start | bytes 4718600 | tf_op jit(solution)/shard_map/ppermute | solution.py:308
  54.7 7.6 %collective-permute-start.2 = (bf16[384,2048]{1,0:T(8,128)(2,1)S(1)}, bf16[384,2048]{1,0:T(8,128)(2,1)S(1)}, u32[]{:S(2)}, u32[]{:S(2)}) collective-permute-start(bf16[384,2048]{1,0:T(8,128)(2,1)S(1)} %get-tuple-element.19), channel_id=1, source_target_pairs={{0,64},{64,0},{1,65},{65,1},{2,66},{66,2},{3,67},{67,3},{4,68},{68... | collective-permute-start | bytes 4718600 | tf_op jit(solution)/shard_map/ppermute | solution.py:316

commit v9 on v7

--- a/solution.py
+++ b/solution.py
@@ -212,19 +212,34 @@
         packed_ref[at, columns] = dot(movers[kind], stack_pieces(block, pieces, wide)).astype(BF16)
 
 
-def project_kernel(core_ref, context_hbm, weight_hbm, own_ref, other_ref, context_ref, weight_ref, sem, sems):
-    load = pltpu.make_async_copy(context_hbm, context_ref, sem)
-    load.start()
+def half_of(context_ref, half):
+    tokens = context_ref.shape[0] // 2
+    return context_ref[pl.ds(pl.multiple_of(half * tokens, tokens), tokens), :]
+
+
+def project_kernel(experts, core_ref, context_hbm, weight_hbm, *refs):
+    small_hbm, refs = refs[:3], refs[3:]
+    other_ref, context_ref, weight_ref, *chosen = refs[:6]
+    small_refs, (small_sems, sem, sems) = refs[6:9], refs[9:]
+    loads = [pltpu.make_async_copy(a, b, small_sems.at[i]) for i, (a, b) in enumerate(zip(small_hbm, small_refs))]
+    loads.append(pltpu.make_async_copy(context_hbm, context_ref, sem))
+    for load in loads:
+        load.start()
     start_copies(weight_hbm, weight_ref, sems)
-    load.wait()
-    tokens = own_ref.shape[0]
-    first = core_ref[0] == 0
+    for load in loads[:3]:
+        load.wait()
+    select_kernel(experts, *small_refs, *chosen)
+    loads[3].wait()
+    rows = half_of(context_ref, 1 - core_ref[0])
     for i in range(weight_ref.shape[1] // TILE):
         tile_copy(weight_hbm, weight_ref, sems, i).wait()
-        at = columns_of(i)
-        both = dot(context_ref[...], weight_ref[:, at])
-        own_ref[:, at] = jnp.where(first, both[:tokens], both[tokens:])
-        other_ref[:, at] = jnp.where(first, both[tokens:], both[:tokens]).astype(BF16)
+        other_ref[:, columns_of(i)] = dot(rows, weight_ref[:, columns_of(i)]).astype(BF16)
+
+
+def own_kernel(core_ref, context_ref, weight_ref, own_ref):
+    rows = half_of(context_ref, core_ref[0])
+    for i in range(weight_ref.shape[1] // TILE):
+        own_ref[:, columns_of(i)] = dot(rows, weight_ref[:, columns_of(i)])
 
 
 def call(kernel, flops, out_shape, args, specs=None, out_specs=None, scratch=(), limit=LIMIT):
@@ -263,23 +278,30 @@
 
     context, out_weight = in_hbm(context[0]), in_hbm(out_weight)
     weight_in, weight_out = expert_in[0], in_hbm(expert_out[0])
-    own, other = call(
-        project_kernel,
-        2 * context.size * features,
-        [pltpu.VMEM((tokens, features), F32), pltpu.VMEM((tokens, features), BF16)],
-        (lax.axis_index("tp")[None], context, out_weight),
-        specs=[SMEM, HBM, HBM],
-        scratch=[vmem(context), vmem(out_weight), pltpu.SemaphoreType.DMA(()), sems(features)],
-        limit=60 << 20,
-    )
-    recv = lax.ppermute(other, "tp", SWAP)
     size = experts * PACK
     pieces = sum(PACK // slots for slots in SPLIT)
-    send, take, gates = call(
-        functools.partial(select_kernel, experts),
-        tokens * tokens * size,
-        [shape(size, pieces * tokens), shape(2 * pieces * tokens, size), shape(tokens, 2, dtype=F32)],
-        (expert_ids[0].T, keep_mask[0].T, gate_weights[0].T),
+    core = lax.axis_index("tp")[None]
+    small = [in_hbm(a[0].T) for a in (expert_ids, keep_mask, gate_weights)]
+    other, context, out_weight, send, take, gates = call(
+        functools.partial(project_kernel, experts),
+        context.size * features,
+        [
+            pltpu.VMEM((tokens, features), BF16),
+            vmem(context),
+            vmem(out_weight),
+            pltpu.VMEM((size, pieces * tokens), BF16),
+            pltpu.VMEM((2 * pieces * tokens, size), BF16),
+            pltpu.VMEM((tokens, 2), F32),
+        ],
+        (core, context, out_weight, *small),
+        specs=[SMEM] + [HBM] * 5,
+        scratch=[*map(vmem, small), pltpu.SemaphoreType.DMA((3,)), pltpu.SemaphoreType.DMA(()), sems(features)],
+        limit=54 << 20,
+    )
+    recv = lax.ppermute(other, "tp", SWAP)
+    own = call(
+        own_kernel, context.size * features, shape(tokens, features, dtype=F32), (core, context, out_weight),
+        specs=[SMEM, VMEM, VMEM],
     )
     packed_shape = shape(experts * PACK, features * SLOT // PACK)
     rows_shape = shape(experts * SLOT, features)

time: 94.8 us -> 94.8 us (level)
  transfers between devices with their start and end apart: 3 -> 3, of which waited for: 2 -> 2; matrix products, arithmetic and copies ran while one was open for 0% -> 0% of each run, Pallas kernels for 9% -> 8%
where the time goes in v9:
time: 94.8 us; the launch traced here: 94.7 us
  blocking collectives  66.1 us (70%)
  Pallas kernels  23.3 us (25%)
  waiting for transfers between devices  4.54 us (5%)
    all_to_all x2, blocking collectives, exchange(): lax.all_to_all(blocks, 'ep', split_axis=0, concat_axis=0, tiled=True)  66.1 us
    pallas_call x8, Pallas kernels, call(): pl.pallas_call(kernel, in_specs=specs or [VMEM] * len(args), out_specs=ou...  23.3 us
    ppermute x1, waiting for transfers between devices, body(): rows_other = lax.ppermute(rows, 'tp', SWAP)  3.41 us
  transfers between devices with their start and end apart: 3, of which 2 were waited for; matrix products, arithmetic and copies ran while one was open for 0% of the time, Pallas kernels for 8%

profile of v9, /device:TPU:0, one launch (start us, length us, event | category | flops | bytes accessed | tf_op | source)
XLA Modules:
  0.0 94.7 jit_solution(2447298475327096127)
XLA Ops:
  0.0 4.2 %shard_map.91 = (bf16[128,2048]{1,0:T(8,128)(2,1)S(1)}, bf16[256,1024]{1,0:T(8,128)(2,1)S(1)}, bf16[1024,2048]{1,0:T(8,128)(2,1)S(1)}, bf16[512,768]{1,0:T(8,128...) custom-call(s32[1]{0:T(128)} %bitcast.core_ref, bf16[256,1024]{1,0:T(8,128)(2,1)} %bitcast.31, ...), custom_call_target="tpu_custom_call" | custom-call | flops 536870912 | bytes 4721668 | tf_op jit(solution)/shard_map/pallas_call | solution.py:246
  4.2 0.1 collective-permute-start
  4.3 0.0 copy-start
  4.3 0.0 copy-start.1
  4.3 0.0 slice-start
  4.3 0.7 shard_map.92.own_ref
  5.1 1.1 %collective-permute-done.recv_ref = bf16[128,2048]{1,0:T(8,128)(2,1)S(1)} collective-permute-done((bf16[128,2048]{1,0:T(8,128)(2,1)S(1)}, bf16[128,2048]{1,0:T(8,128)(2,1)S(1)}, u32[]{:S(2)}, u32[]{:S(2)}) %collective-permute-start) | collective-permute-done | bytes 524320 | tf_op jit(solution)/shard_map/ppermute | solution.py:301
  6.2 0.0 copy-done
  6.2 0.0 copy-done.1
  6.2 0.0 slice-start.1
  6.2 1.2 %shard_map.93 = (bf16[128,2048]{1,0:T(8,128)(2,1)S(1)}, bf16[512,1536]{1,0:T(8,128)(2,1)S(1)}) custom-call(f32[128,2048]{1,0:T(8,128)S(1)} %shard_map.92.own_ref, bf16[128,2048]{1,0:T(8,128)(2,1)S(1)} %collective-permute-done.recv_ref, bf16[128,2048]{1,0:T(8,128)(2,1)S(1)} %bitcast.29, f32[1,2048]{1,0:T(1,128)S(1)} %bitcast.30, ...), custom_call_target="tpu_custom_call" | custom-call | flops 4294967296 | bytes 2891776 | tf_op jit(solution)/shard_map/pallas_call | solution.py:246
  7.4 36.0 %all_to_all.10 = bf16[64,8,1536]{2,1,0:T(8,128)(2,1)S(1)} all-to-all(bf16[64,8,1536]{2,1,0:T(8,128)(2,1)S(1)} %bitcast.24), channel_id=1, replica_groups=mesh['tp'=2,'ep'=64] {'ep'}, dimensions={0} | all-to-all | bytes 3145728 | tf_op jit(solution)/shard_map/all_to_all | solution.py:318
  43.5 0.0 collective-permute-start.1
  43.5 3.4 %collective-permute-done.1.packed_ref = bf16[512,1536]{1,0:T(8,128)(2,1)S(1)} collective-permute-done((bf16[512,1536]{1,0:T(8,128)(2,1)S(1)}, bf16[512,1536]{1,0:T(8,128)(2,1)S(1)}, u32[]{:S(2)}, u32[]{:S(2)}) %collective-permute-start.1) | collective-permute-done | bytes 1572896 | tf_op jit(solution)/shard_map/ppermute | solution.py:321
  46.9 0.0 slice-done
  46.9 0.0 slice-done.1
  46.9 7.3 %shard_map.95 = (bf16[384,2048]{1,0:T(8,128)(2,1)S(1)}, bf16[2048,2048]{1,0:T(8,128)(2,1)S(1)}) custom-call(bf16[512,1536]{1,0:T(8,128)(2,1)S(1)} %collective-permute-done.1.packed_ref, bf16[2048,2048]{1,0:T(8,128)(2,1)S(1)} %bitcast.27, bf16[2048,2048]{1,0:T(8,128)(2,1)} %bitcast.35), custom_call_target="tpu_custom_call" | custom-call | flops 6442450944 | bytes 18350080 | tf_op jit(solution)/shard_map/pallas_call | solution.py:246
  54.2 0.4 collective-permute-start.2
  54.6 3.8 %shard_map.94.hidden_ref = bf16[384,2048]{1,0:T(8,128)(2,1)S(1)} custom-call(bf16[512,1536]{1,0:T(8,128)(2,1)S(1)} %bitcast.23, bf16[2048,2048]{1,0:T(8,128)(2,1)S(1)} %bitcast.28), custom_call_target="tpu_custom_call" | custom-call | flops 3221225472 | bytes 9961472 | tf_op jit(solution)/shard_map/pallas_call | solution.py:246
  58.4 3.4 %shard_map.96.own_ref = f32[384,2048]{1,0:T(8,128)S(1)} custom-call(bf16[384,2048]{1,0:T(8,128)(2,1)S(1)} %shard_map.94.hidden_ref, bf16[2048,2048]{1,0:T(8,128)(2,1)S(1)} %get-tuple-element.20.out_ref), custom_call_target="tpu_custom_call" | custom-call | flops 3221225472 | bytes 9961472 | tf_op jit(solution)/shard_map/pallas_call | solution.py:246
  61.8 0.0 collective-permute-done.2.recv_ref
  61.8 0.7 shard_map.97
  62.5 30.1 %all_to_all.11 = bf16[64,8,1536]{2,1,0:T(8,128)(2,1)S(1)} all-to-all(bf16[64,8,1536]{2,1,0:T(8,128)(2,1)S(1)} %bitcast.21), channel_id=1, replica_groups=mesh['tp'=2,'ep'=64] {'ep'}, dimensions={0} | all-to-all | bytes 3145728 | tf_op jit(solution)/shard_map/all_to_all | solution.py:318
  92.6 2.0 %shard_map.98 = bf16[128,2048]{1,0:T(8,128)(2,1)} custom-call(bf16[512,1536]{1,0:T(8,128)(2,1)S(1)} %bitcast.20, bf16[128,2048]{1,0:T(8,128)(2,1)S(1)} %get-tuple-element.22.stream_ref, bf16[1536,512]{1,0:T(8,128)(2,1)S(1)} %get-tuple-element.23.take_ref, f32[128,2]{1,0:T(8,128)S(1)} %get-tuple-element.24.gate_ref), custom_call_target="tpu_custom_call" | custom-call | flops 1073741824 | bytes 3671040 | tf_op jit(solution)/shard_map/pallas_call | solution.py:246
  (1 shorter events, 0.0 us)
Async XLA Ops:
  4.2 2.0 %collective-permute-start = (bf16[128,2048]{1,0:T(8,128)(2,1)S(1)}, bf16[128,2048]{1,0:T(8,128)(2,1)S(1)}, u32[]{:S(2)}, u32[]{:S(2)}) collective-permute-start(bf16[128,2048]{1,0:T(8,128)(2,1)S(1)} %get-tuple-element.17), channel_id=1, source_target_pairs={{0,64},{64,0},{1,65},{65,1},{2,66},{66,2},{3,67},{67,3},{4,68},{68... | collective-permute-start | bytes 1572872 | tf_op jit(solution)/shard_map/ppermute | solution.py:301
  4.3 1.9 %copy-start = (bf16[1,128,2048]{2,1,0:T(8,128)(2,1)S(1)}, bf16[1,128,2048]{2,1,0:T(8,128)(2,1)}, u32[]{:S(2)}) copy-start(bf16[1,128,2048]{2,1,0:T(8,128)(2,1)} %param.11) | copy-start | bytes 1572868
  4.3 1.9 %copy-start.1 = (f32[2048]{0:T(1024)S(1)}, f32[2048]{0:T(1024)}, u32[]{:S(2)}) copy-start(f32[2048]{0:T(1024)} %param.12) | copy-start | bytes 24580
  4.3 42.6 %slice-start = ((s8[8388608]{0:T(1024)(128)(4,1)}), s8[4194304]{0:T(1024)(128)(4,1)S(1)}, s32[]{:S(2)}) async-start(s8[8388608]{0:T(1024)(128)(4,1)} %bitcast.25), calls=%async_computation.2 | async-start | bytes 8388608
  6.2 40.7 %slice-start.1 = ((s8[8388608]{0:T(1024)(128)(4,1)}), s8[4194304]{0:T(1024)(128)(4,1)S(1)}, s32[]{:S(2)}) async-start(s8[8388608]{0:T(1024)(128)(4,1)} %bitcast.25), calls=%async_computation.3 | async-start | bytes 8388608
  43.5 3.4 %collective-permute-start.1 = (bf16[512,1536]{1,0:T(8,128)(2,1)S(1)}, bf16[512,1536]{1,0:T(8,128)(2,1)S(1)}, u32[]{:S(2)}, u32[]{:S(2)}) collective-permute-start(bf16[512,1536]{1,0:T(8,128)(2,1)S(1)} %bitcast.22), channel_id=1, source_target_pairs={{0,64},{64,0},{1,65},{65,1},{2,66},{66,2},{3,67},{67,3},{4,68},{68... | collective-permute-start | bytes 4718600 | tf_op jit(solution)/shard_map/ppermute | solution.py:321
  54.2 7.6 %collective-permute-start.2 = (bf16[384,2048]{1,0:T(8,128)(2,1)S(1)}, bf16[384,2048]{1,0:T(8,128)(2,1)S(1)}, u32[]{:S(2)}, u32[]{:S(2)}) collective-permute-start(bf16[384,2048]{1,0:T(8,128)(2,1)S(1)} %get-tuple-element.21), channel_id=1, source_target_pairs={{0,64},{64,0},{1,65},{65,1},{2,66},{66,2},{3,67},{67,3},{4,68},{68... | collective-permute-start | bytes 4718600 | tf_op jit(solution)/shard_map/ppermute | solution.py:329

commit v10 on v9

--- a/solution.py
+++ b/solution.py
@@ -14,6 +14,7 @@
 FIRST = (0, 4)
 SOURCES = 32
 TILE = 512
+DEPTH = 512
 LIMIT = 16 << 20
 F32, BF16 = jnp.float32, jnp.bfloat16
 VMEM = pl.BlockSpec(memory_space=pltpu.VMEM)
@@ -212,28 +213,36 @@
         packed_ref[at, columns] = dot(movers[kind], stack_pieces(block, pieces, wide)).astype(BF16)
 
 
-def half_of(context_ref, half):
+def half_of(context_ref, half, columns=slice(None)):
     tokens = context_ref.shape[0] // 2
-    return context_ref[pl.ds(pl.multiple_of(half * tokens, tokens), tokens), :]
+    return context_ref[pl.ds(pl.multiple_of(half * tokens, tokens), tokens), columns]
 
 
 def project_kernel(experts, core_ref, context_hbm, weight_hbm, *refs):
     small_hbm, refs = refs[:3], refs[3:]
     other_ref, context_ref, weight_ref, *chosen = refs[:6]
-    small_refs, (small_sems, sem, sems) = refs[6:9], refs[9:]
+    small_refs, (total_ref, small_sems, sem, sems) = refs[6:9], refs[9:]
     loads = [pltpu.make_async_copy(a, b, small_sems.at[i]) for i, (a, b) in enumerate(zip(small_hbm, small_refs))]
     loads.append(pltpu.make_async_copy(context_hbm, context_ref, sem))
     for load in loads:
         load.start()
-    start_copies(weight_hbm, weight_ref, sems)
+    parts = [slice(i * DEPTH, (i + 1) * DEPTH) for i in range(weight_ref.shape[0] // DEPTH)]
+    copies = [pltpu.make_async_copy(weight_hbm.at[at, :], weight_ref.at[at, :], sems.at[i]) for i, at in enumerate(parts)]
+    for copy in copies:
+        copy.start()
     for load in loads[:3]:
         load.wait()
     select_kernel(experts, *small_refs, *chosen)
     loads[3].wait()
-    rows = half_of(context_ref, 1 - core_ref[0])
-    for i in range(weight_ref.shape[1] // TILE):
-        tile_copy(weight_hbm, weight_ref, sems, i).wait()
-        other_ref[:, columns_of(i)] = dot(rows, weight_ref[:, columns_of(i)]).astype(BF16)
+    for i, (copy, at) in enumerate(zip(copies, parts)):
+        copy.wait()
+        term = dot(half_of(context_ref, 1 - core_ref[0], at), weight_ref[at, :])
+        if i == 0:
+            total_ref[...] = term
+        elif i < len(parts) - 1:
+            total_ref[...] += term
+        else:
+            other_ref[...] = (total_ref[...] + term).astype(BF16)
 
 
 def own_kernel(core_ref, context_ref, weight_ref, own_ref):
@@ -295,7 +304,13 @@
         ],
         (core, context, out_weight, *small),
         specs=[SMEM] + [HBM] * 5,
-        scratch=[*map(vmem, small), pltpu.SemaphoreType.DMA((3,)), pltpu.SemaphoreType.DMA(()), sems(features)],
+        scratch=[
+            *map(vmem, small),
+            pltpu.VMEM((tokens, features), F32),
+            pltpu.SemaphoreType.DMA((3,)),
+            pltpu.SemaphoreType.DMA(()),
+            pltpu.SemaphoreType.DMA((out_weight.shape[0] // DEPTH,)),
+        ],
         limit=54 << 20,
     )
     recv = lax.ppermute(other, "tp", SWAP)

time: 94.8 us -> 94 us (level)
  no operation moved by 1% of the time
where the time goes in v10:
time: 94 us; the launch traced here: 93.8 us
  blocking collectives  66.1 us (70%)
  Pallas kernels  22.4 us (24%)
  waiting for transfers between devices  4.54 us (5%)
    all_to_all x2, blocking collectives, exchange(): lax.all_to_all(blocks, 'ep', split_axis=0, concat_axis=0, tiled=True)  66.1 us
    pallas_call x8, Pallas kernels, call(): pl.pallas_call(kernel, in_specs=specs or [VMEM] * len(args), out_specs=ou...  22.4 us
    ppermute x1, waiting for transfers between devices, body(): rows_other = lax.ppermute(rows, 'tp', SWAP)  3.41 us
  transfers between devices with their start and end apart: 3, of which 2 were waited for; matrix products, arithmetic and copies ran while one was open for 0% of the time, Pallas kernels for 8%

profile of v10, /device:TPU:0, one launch (start us, length us, event | category | flops | bytes accessed | tf_op | source)
XLA Modules:
  0.0 93.8 jit_solution(8137976790633180116)
XLA Ops:
  0.0 3.4 %shard_map.91 = (bf16[128,2048]{1,0:T(8,128)(2,1)S(1)}, bf16[256,1024]{1,0:T(8,128)(2,1)S(1)}, bf16[1024,2048]{1,0:T(8,128)(2,1)S(1)}, bf16[512,768]{1,0:T(8,128...) custom-call(s32[1]{0:T(128)} %bitcast.core_ref, bf16[256,1024]{1,0:T(8,128)(2,1)} %bitcast.31, ...), custom_call_target="tpu_custom_call" | custom-call | flops 536870912 | bytes 4721668 | tf_op jit(solution)/shard_map/pallas_call | solution.py:255
  3.4 0.1 collective-permute-start
  3.5 0.0 copy-start
  3.5 0.0 copy-start.1
  3.5 0.0 slice-start
  3.5 0.7 shard_map.92.own_ref
  4.2 1.1 %collective-permute-done.recv_ref = bf16[128,2048]{1,0:T(8,128)(2,1)S(1)} collective-permute-done((bf16[128,2048]{1,0:T(8,128)(2,1)S(1)}, bf16[128,2048]{1,0:T(8,128)(2,1)S(1)}, u32[]{:S(2)}, u32[]{:S(2)}) %collective-permute-start) | collective-permute-done | bytes 524320 | tf_op jit(solution)/shard_map/ppermute | solution.py:316
  5.4 0.0 copy-done
  5.4 0.0 copy-done.1
  5.4 0.0 slice-start.1
  5.4 1.2 %shard_map.93 = (bf16[128,2048]{1,0:T(8,128)(2,1)S(1)}, bf16[512,1536]{1,0:T(8,128)(2,1)S(1)}) custom-call(f32[128,2048]{1,0:T(8,128)S(1)} %shard_map.92.own_ref, bf16[128,2048]{1,0:T(8,128)(2,1)S(1)} %collective-permute-done.recv_ref, bf16[128,2048]{1,0:T(8,128)(2,1)S(1)} %bitcast.29, f32[1,2048]{1,0:T(1,128)S(1)} %bitcast.30, ...), custom_call_target="tpu_custom_call" | custom-call | flops 4294967296 | bytes 2891776 | tf_op jit(solution)/shard_map/pallas_call | solution.py:255
  6.6 36.0 %all_to_all.10 = bf16[64,8,1536]{2,1,0:T(8,128)(2,1)S(1)} all-to-all(bf16[64,8,1536]{2,1,0:T(8,128)(2,1)S(1)} %bitcast.24), channel_id=1, replica_groups=mesh['tp'=2,'ep'=64] {'ep'}, dimensions={0} | all-to-all | bytes 3145728 | tf_op jit(solution)/shard_map/all_to_all | solution.py:333
  42.7 0.0 collective-permute-start.1
  42.7 3.4 %collective-permute-done.1.packed_ref = bf16[512,1536]{1,0:T(8,128)(2,1)S(1)} collective-permute-done((bf16[512,1536]{1,0:T(8,128)(2,1)S(1)}, bf16[512,1536]{1,0:T(8,128)(2,1)S(1)}, u32[]{:S(2)}, u32[]{:S(2)}) %collective-permute-start.1) | collective-permute-done | bytes 1572896 | tf_op jit(solution)/shard_map/ppermute | solution.py:336
  46.1 0.0 slice-done
  46.1 0.0 slice-done.1
  46.1 7.3 %shard_map.95 = (bf16[384,2048]{1,0:T(8,128)(2,1)S(1)}, bf16[2048,2048]{1,0:T(8,128)(2,1)S(1)}) custom-call(bf16[512,1536]{1,0:T(8,128)(2,1)S(1)} %collective-permute-done.1.packed_ref, bf16[2048,2048]{1,0:T(8,128)(2,1)S(1)} %bitcast.27, bf16[2048,2048]{1,0:T(8,128)(2,1)} %bitcast.35), custom_call_target="tpu_custom_call" | custom-call | flops 6442450944 | bytes 18350080 | tf_op jit(solution)/shard_map/pallas_call | solution.py:255
  53.4 0.4 collective-permute-start.2
  53.8 3.8 %shard_map.94.hidden_ref = bf16[384,2048]{1,0:T(8,128)(2,1)S(1)} custom-call(bf16[512,1536]{1,0:T(8,128)(2,1)S(1)} %bitcast.23, bf16[2048,2048]{1,0:T(8,128)(2,1)S(1)} %bitcast.28), custom_call_target="tpu_custom_call" | custom-call | flops 3221225472 | bytes 9961472 | tf_op jit(solution)/shard_map/pallas_call | solution.py:255
  57.6 3.4 %shard_map.96.own_ref = f32[384,2048]{1,0:T(8,128)S(1)} custom-call(bf16[384,2048]{1,0:T(8,128)(2,1)S(1)} %shard_map.94.hidden_ref, bf16[2048,2048]{1,0:T(8,128)(2,1)S(1)} %get-tuple-element.20.out_ref), custom_call_target="tpu_custom_call" | custom-call | flops 3221225472 | bytes 9961472 | tf_op jit(solution)/shard_map/pallas_call | solution.py:255
  61.0 0.0 collective-permute-done.2.recv_ref
  61.0 0.7 shard_map.97
  61.7 30.1 %all_to_all.11 = bf16[64,8,1536]{2,1,0:T(8,128)(2,1)S(1)} all-to-all(bf16[64,8,1536]{2,1,0:T(8,128)(2,1)S(1)} %bitcast.21), channel_id=1, replica_groups=mesh['tp'=2,'ep'=64] {'ep'}, dimensions={0} | all-to-all | bytes 3145728 | tf_op jit(solution)/shard_map/all_to_all | solution.py:333
  91.7 2.0 %shard_map.98 = bf16[128,2048]{1,0:T(8,128)(2,1)} custom-call(bf16[512,1536]{1,0:T(8,128)(2,1)S(1)} %bitcast.20, bf16[128,2048]{1,0:T(8,128)(2,1)S(1)} %get-tuple-element.22.stream_ref, bf16[1536,512]{1,0:T(8,128)(2,1)S(1)} %get-tuple-element.23.take_ref, f32[128,2]{1,0:T(8,128)S(1)} %get-tuple-element.24.gate_ref), custom_call_target="tpu_custom_call" | custom-call | flops 1073741824 | bytes 3671040 | tf_op jit(solution)/shard_map/pallas_call | solution.py:255
  (1 shorter events, 0.0 us)
Async XLA Ops:
  3.4 2.0 %collective-permute-start = (bf16[128,2048]{1,0:T(8,128)(2,1)S(1)}, bf16[128,2048]{1,0:T(8,128)(2,1)S(1)}, u32[]{:S(2)}, u32[]{:S(2)}) collective-permute-start(bf16[128,2048]{1,0:T(8,128)(2,1)S(1)} %get-tuple-element.17), channel_id=1, source_target_pairs={{0,64},{64,0},{1,65},{65,1},{2,66},{66,2},{3,67},{67,3},{4,68},{68... | collective-permute-start | bytes 1572872 | tf_op jit(solution)/shard_map/ppermute | solution.py:316
  3.5 1.9 %copy-start = (bf16[1,128,2048]{2,1,0:T(8,128)(2,1)S(1)}, bf16[1,128,2048]{2,1,0:T(8,128)(2,1)}, u32[]{:S(2)}) copy-start(bf16[1,128,2048]{2,1,0:T(8,128)(2,1)} %param.11) | copy-start | bytes 1572868
  3.5 1.9 %copy-start.1 = (f32[2048]{0:T(1024)S(1)}, f32[2048]{0:T(1024)}, u32[]{:S(2)}) copy-start(f32[2048]{0:T(1024)} %param.12) | copy-start | bytes 24580
  3.5 42.6 %slice-start = ((s8[8388608]{0:T(1024)(128)(4,1)}), s8[4194304]{0:T(1024)(128)(4,1)S(1)}, s32[]{:S(2)}) async-start(s8[8388608]{0:T(1024)(128)(4,1)} %bitcast.25), calls=%async_computation.2 | async-start | bytes 8388608
  5.4 40.7 %slice-start.1 = ((s8[8388608]{0:T(1024)(128)(4,1)}), s8[4194304]{0:T(1024)(128)(4,1)S(1)}, s32[]{:S(2)}) async-start(s8[8388608]{0:T(1024)(128)(4,1)} %bitcast.25), calls=%async_computation.3 | async-start | bytes 8388608
  42.7 3.4 %collective-permute-start.1 = (bf16[512,1536]{1,0:T(8,128)(2,1)S(1)}, bf16[512,1536]{1,0:T(8,128)(2,1)S(1)}, u32[]{:S(2)}, u32[]{:S(2)}) collective-permute-start(bf16[512,1536]{1,0:T(8,128)(2,1)S(1)} %bitcast.22), channel_id=1, source_target_pairs={{0,64},{64,0},{1,65},{65,1},{2,66},{66,2},{3,67},{67,3},{4,68},{68... | collective-permute-start | bytes 4718600 | tf_op jit(solution)/shard_map/ppermute | solution.py:336
  53.4 7.6 %collective-permute-start.2 = (bf16[384,2048]{1,0:T(8,128)(2,1)S(1)}, bf16[384,2048]{1,0:T(8,128)(2,1)S(1)}, u32[]{:S(2)}, u32[]{:S(2)}) collective-permute-start(bf16[384,2048]{1,0:T(8,128)(2,1)S(1)} %get-tuple-element.21), channel_id=1, source_target_pairs={{0,64},{64,0},{1,65},{65,1},{2,66},{66,2},{3,67},{67,3},{4,68},{68... | collective-permute-start | bytes 4718600 | tf_op jit(solution)/shard_map/ppermute | solution.py:344
